TPU v7x, 32 devices: a whole 2x2x4 slice. The times are simulated.
32 devices in a mesh: seq: 8 (over y, x, core), wshard: 4 (over z).
Axes of the slice: x: 2, y: 2, z: 4, core: 2. Of those that a mesh axis runs over, the one named last changes fastest.
Arguments:
- tokens: bfloat16 [8, 1024, 2048], P('wshard', 'seq')
- starts: int32 [8, 1024], P('wshard'), may hold values 0 or 1
- layer_index: int32 [1], replicated, may hold values from 0 to 23
- gain_mix: float32 [2048], replicated, may hold values from 0.5 to 1.5
- w_in: bfloat16 [2048, 2048], P('wshard'), may hold values from -0.125 to 0.125
- w_forget: bfloat16 [2048, 1024], P('wshard'), may hold values from -0.125 to 0.125
- bias_forget: float32 [1024], replicated, may hold values from 2 to 9
- theta: float32 [1024], replicated, may hold values from -1 to 1
- w_gate_out: bfloat16 [2048, 2048], P('wshard'), may hold values from -0.125 to 0.125
- gain_out: float32 [2048], replicated, may hold values from 0.5 to 1.5
- w_out: bfloat16 [2048, 2048], P('wshard'), may hold values from -0.1875 to 0.1875
- gain_ffn: float32 [2048], replicated, may hold values from 0.5 to 1.5
- w_ffgate: bfloat16 [2048, 5632], P('wshard'), may hold values from -0.125 to 0.125
- w_ffup: bfloat16 [2048, 5632], P('wshard'), may hold values from -0.125 to 0.125
- w_down: bfloat16 [5632, 2048], P('wshard'), may hold values from -0.15625 to 0.15625
- out_grad: bfloat16 [8, 1024, 2048], P('wshard', 'seq'), may hold values from -6 to 6
Outputs:
- result: bfloat16 [8, 1024, 2048], P('wshard', 'seq')
- grad_tokens: bfloat16 [8, 1024, 2048], P('wshard', 'seq')
- grad_gain_mix: float32 [2048], replicated
- grad_w_in: float32 [2048, 2048], P(('seq', 'wshard'))
- grad_w_forget: float32 [2048, 1024], P(('seq', 'wshard'))
- grad_bias_forget: float32 [1024], replicated
- grad_theta: float32 [1024], replicated
- grad_w_gate_out: float32 [2048, 2048], P(('seq', 'wshard'))
- grad_gain_out: float32 [2048], replicated
- grad_w_out: float32 [2048, 2048], P(('seq', 'wshard'))
- grad_gain_ffn: float32 [2048], replicated
- grad_w_ffgate: float32 [2048, 5632], P(('seq', 'wshard'))
- grad_w_ffup: float32 [2048, 5632], P(('seq', 'wshard'))
- grad_w_down: float32 [5632, 2048], P(('seq', 'wshard'))
- rms_values: float32 [3], replicated
Inputs may be any that keep to these rules, and one draw needn't show every extreme that they name: 1 marks the first token of a document inside a sequence; the state starts afresh there. `layer_index`: the layer's place among 24.
All inputs are finite; a program needn't handle non-finite values. No bound on the sum of `starts` on one device may be relied on, other than what follows from the above.
Results may differ from a plain program's by a relative error of at most 0.014.
Values may be sent and summed in bfloat16 or wider, within the bound.
No kernel may reach another device: no remote copies, remote signals or barrier semaphores. Data moves between devices by JAX's collectives and lax.ppermute only.
A program may use at most 512 MiB of HBM per device.

v0:
```python
import jax
import jax.numpy as jnp
from jax import lax
from jax.sharding import PartitionSpec as P

LAYERS = 24


EPS = 1e-06


def combine(first, second):
    left_re, left_im, base_re, base_im = first
    right_re, right_im, add_re, add_im = second
    return (
        left_re * right_re - left_im * right_im,
        left_re * right_im + left_im * right_re,
        right_re * base_re - right_im * base_im + add_re,
        right_re * base_im + right_im * base_re + add_im,
    )


def product(left, right, form):
    return jnp.einsum(form, left, right, preferred_element_type=jnp.float32)


def body(
    tokens,
    starts,
    layer_index,
    gain_mix,
    w_in,
    w_forget,
    bias_forget,
    theta,
    w_gate_out,
    gain_out,
    w_out,
    gain_ffn,
    w_ffgate,
    w_ffup,
    w_down,
    out_grad,
):
    seqs, seq_dev, width = tokens.shape
    rows = seqs * seq_dev
    chans = width // 2
    groups = lax.axis_size("seq")
    devices = groups * lax.axis_size("wshard")
    position = lax.axis_index("seq")
    floor = layer_index[0].astype(jnp.float32) / LAYERS
    full_in, full_forget, full_gate_out, full_out = (
        lax.all_gather(w_in, "wshard", axis=0, tiled=True),
        lax.all_gather(w_forget, "wshard", axis=0, tiled=True),
        lax.all_gather(w_gate_out, "wshard", axis=0, tiled=True),
        lax.all_gather(w_out, "wshard", axis=0, tiled=True),
    )
    full_ffgate, full_ffup, full_down = (
        lax.all_gather(w_ffgate, "wshard", axis=0, tiled=True),
        lax.all_gather(w_ffup, "wshard", axis=0, tiled=True),
        lax.all_gather(w_down, "wshard", axis=0, tiled=True),
    )
    hidden_width = full_down.shape[0]
    resid_in = tokens.reshape(rows, width).astype(jnp.float32)
    scale_in = lax.rsqrt(jnp.mean(resid_in * resid_in, axis=1, keepdims=True) + EPS)
    normed_in = (resid_in * scale_in * gain_mix).astype(jnp.bfloat16)
    pre_input = product(full_in, normed_in, "dc,td->ct")
    sig_input = jax.nn.sigmoid(pre_input)
    cand = (pre_input * sig_input).astype(jnp.bfloat16)
    forget_logit = (product(full_forget, normed_in, "dc,td->ct") + bias_forget[:, None]).astype(
        jnp.bfloat16
    )
    pre_gate = product(full_gate_out, normed_in, "dc,td->ct")
    packed = jnp.concatenate([cand, forget_logit], axis=0).reshape(3, chans, seqs, seq_dev)
    local = lax.all_to_all(packed, "seq", split_axis=1, concat_axis=3, tiled=True)
    share = chans // groups
    flags = starts.astype(jnp.float32)[None]
    angle = lax.dynamic_slice_in_dim(theta, position * share, share)[:, None, None]
    cand_re = local[0].astype(jnp.float32)
    cand_im = local[1].astype(jnp.float32)
    sig_forget = jax.nn.sigmoid(local[2].astype(jnp.float32))
    keep = (floor + (1.0 - floor) * sig_forget) * (1.0 - flags)
    cosine = jnp.cos(angle)
    sine = jnp.sin(angle)
    decay_re = keep * cosine
    decay_im = keep * sine
    prod_re, prod_im, state_re, state_im = lax.associative_scan(
        combine, (decay_re, decay_im, (1.0 - keep) * cand_re, (1.0 - keep) * cand_im), axis=2
    )
    nought = jnp.zeros_like(state_re[..., 0])
    prev_re = jnp.concatenate([nought[..., None], state_re[..., :-1]], axis=2)
    prev_im = jnp.concatenate([nought[..., None], state_im[..., :-1]], axis=2)
    state_low = jnp.stack([state_re, state_im]).astype(jnp.bfloat16)
    merged = lax.all_to_all(state_low, "seq", split_axis=3, concat_axis=1, tiled=True)
    mixed_state = merged.reshape(width, rows).astype(jnp.float32)
    scale_out = lax.rsqrt(jnp.mean(mixed_state * mixed_state, axis=0, keepdims=True) + EPS)
    sig_gate = jax.nn.sigmoid(pre_gate)
    normed_state = mixed_state * scale_out
    gated = (normed_state * gain_out[:, None] * sig_gate).astype(jnp.bfloat16)
    branch_mix = product(gated, full_out, "ct,cd->td")
    resid = resid_in + branch_mix
    scale_ffn = lax.rsqrt(jnp.mean(resid * resid, axis=1, keepdims=True) + EPS)
    normed_ffn = (resid * scale_ffn * gain_ffn).astype(jnp.bfloat16)
    ffn_gate = product(normed_ffn, full_ffgate, "td,df->tf")
    ffn_up = product(normed_ffn, full_ffup, "td,df->tf")
    sig_ffn = jax.nn.sigmoid(ffn_gate)
    silu_ffn = ffn_gate * sig_ffn
    ffn_hidden = (silu_ffn * ffn_up).astype(jnp.bfloat16)
    branch_ffn = product(ffn_hidden, full_down, "tf,fd->td")
    result = (resid + branch_ffn).astype(jnp.bfloat16)
    upstream = out_grad.reshape(rows, width)
    grad_hidden = product(upstream, full_down, "td,fd->tf")
    grad_gate = (grad_hidden * ffn_up * sig_ffn * (1.0 + ffn_gate * (1.0 - sig_ffn))).astype(
        jnp.bfloat16
    )
    grad_up = (grad_hidden * silu_ffn).astype(jnp.bfloat16)
    grad_normed_ffn = product(grad_gate, full_ffgate, "tf,df->td") + product(
        grad_up, full_ffup, "tf,df->td"
    )
    scaled_ffn = grad_normed_ffn * gain_ffn
    grad_resid = (
        upstream.astype(jnp.float32)
        + scale_ffn * scaled_ffn
        - resid * scale_ffn**3 * jnp.mean(scaled_ffn * resid, axis=1, keepdims=True)
    )
    grad_gain_ffn = jnp.sum(grad_normed_ffn * resid * scale_ffn, axis=0)
    grad_branch = grad_resid.astype(jnp.bfloat16)
    grad_gated = product(full_out, grad_branch, "cd,td->ct")
    grad_normed_state = grad_gated * gain_out[:, None] * sig_gate
    grad_gain_out = jnp.sum(grad_gated * normed_state * sig_gate, axis=1)
    grad_pre_gate = (
        grad_gated * normed_state * gain_out[:, None] * sig_gate * (1.0 - sig_gate)
    ).astype(jnp.bfloat16)
    grad_mixed = scale_out * grad_normed_state - mixed_state * scale_out**3 * jnp.mean(
        grad_normed_state * mixed_state, axis=0, keepdims=True
    )
    grad_low = grad_mixed.astype(jnp.bfloat16).reshape(2, chans, seqs, seq_dev)
    incoming = lax.all_to_all(grad_low, "seq", split_axis=1, concat_axis=3, tiled=True)
    arrive_re = incoming[0].astype(jnp.float32)
    arrive_im = incoming[1].astype(jnp.float32)
    next_re = jnp.concatenate([decay_re[..., 1:], jnp.ones_like(decay_re[..., :1])], axis=2)
    next_im = jnp.concatenate([-decay_im[..., 1:], jnp.zeros_like(decay_im[..., :1])], axis=2)
    reach_re, reach_im, adjoint_re, adjoint_im = lax.associative_scan(
        combine, (next_re, next_im, arrive_re, arrive_im), reverse=True, axis=2
    )
    turn_re = cosine * prev_re - sine * prev_im
    turn_im = sine * prev_re + cosine * prev_im
    grad_keep = adjoint_re * (turn_re - cand_re) + adjoint_im * (turn_im - cand_im)
    theta_part = -jnp.sum(keep * (adjoint_re * turn_im - adjoint_im * turn_re), axis=(1, 2))
    grad_forget = grad_keep * (1.0 - flags) * (1.0 - floor) * sig_forget * (1.0 - sig_forget)
    back_pack = jnp.stack(
        [(1.0 - keep) * adjoint_re, (1.0 - keep) * adjoint_im, grad_forget]
    ).astype(jnp.bfloat16)
    returned = lax.all_to_all(back_pack, "seq", split_axis=3, concat_axis=1, tiled=True)
    grad_theta = lax.dynamic_update_slice_in_dim(
        jnp.zeros((chans,), jnp.float32), theta_part, position * share, 0
    )
    grad_cand = returned[:2].reshape(width, rows).astype(jnp.float32)
    grad_forget_low = returned[2].reshape(chans, rows)
    grad_bias = jnp.sum(grad_forget_low.astype(jnp.float32), axis=1)
    grad_input = (grad_cand * sig_input * (1.0 + pre_input * (1.0 - sig_input))).astype(
        jnp.bfloat16
    )
    grad_normed_in = (
        product(full_in, grad_input, "dc,ct->td")
        + product(full_forget, grad_forget_low, "dc,ct->td")
        + product(full_gate_out, grad_pre_gate, "dc,ct->td")
    )
    scaled_in = grad_normed_in * gain_mix
    grad_tokens = (
        grad_resid
        + scale_in * scaled_in
        - resid_in * scale_in**3 * jnp.mean(scaled_in * resid_in, axis=1, keepdims=True)
    ).astype(jnp.bfloat16)
    grad_gain_mix = jnp.sum(grad_normed_in * resid_in * scale_in, axis=0)
    owned = lax.psum_scatter(
        jnp.concatenate(
            [
                product(normed_in, grad_input, "td,ct->dc"),
                product(normed_in, grad_forget_low, "td,ct->dc"),
                product(normed_in, grad_pre_gate, "td,ct->dc"),
                product(gated, grad_branch, "ct,td->cd"),
                product(normed_ffn, grad_gate, "td,tf->df"),
                product(normed_ffn, grad_up, "td,tf->df"),
            ],
            axis=1,
        ),
        ("seq", "wshard"),
        scatter_dimension=0,
        tiled=True,
    )
    grad_w_down = lax.psum_scatter(
        product(ffn_hidden, upstream, "tf,td->fd"),
        ("seq", "wshard"),
        scatter_dimension=0,
        tiled=True,
    )
    squares = jnp.stack(
        [
            jnp.sum(resid_in * resid_in),
            jnp.sum(branch_mix * branch_mix),
            jnp.sum(branch_ffn * branch_ffn),
        ]
    )
    grad_gain_mix, grad_bias, grad_theta, grad_gain_out, grad_gain_ffn, squares = lax.psum(
        (grad_gain_mix, grad_bias, grad_theta, grad_gain_out, grad_gain_ffn, squares),
        ("seq", "wshard"),
    )
    rms_values = jnp.sqrt(squares / (rows * width * devices))
    edge_two = width + chans
    edge_three = edge_two + width
    edge_four = edge_three + width
    edge_five = edge_four + hidden_width
    return (
        result.reshape(seqs, seq_dev, width),
        grad_tokens.reshape(seqs, seq_dev, width),
        grad_gain_mix,
        owned[:, :width],
        owned[:, width:edge_two],
        grad_bias,
        grad_theta,
        owned[:, edge_two:edge_three],
        grad_gain_out,
        owned[:, edge_three:edge_four],
        grad_gain_ffn,
        owned[:, edge_four:edge_five],
        owned[:, edge_five:],
        grad_w_down,
        rms_values,
    )


def solution(mesh):
    return jax.shard_map(
        body,
        mesh=mesh,
        in_specs=(
            P("wshard", "seq", None),
            P("wshard", None),
            P(),
            P(),
            P("wshard", None),
            P("wshard", None),
            P(),
            P(),
            P("wshard", None),
            P(),
            P("wshard", None),
            P(),
            P("wshard", None),
            P("wshard", None),
            P("wshard", None),
            P("wshard", "seq", None),
        ),
        out_specs=(
            P("wshard", "seq", None),
            P("wshard", "seq", None),
            P(),
            P(("seq", "wshard"), None),
            P(("seq", "wshard"), None),
            P(),
            P(),
            P(("seq", "wshard"), None),
            P(),
            P(("seq", "wshard"), None),
            P(),
            P(("seq", "wshard"), None),
            P(("seq", "wshard"), None),
            P(("seq", "wshard"), None),
            P(),
        ),
        check_vma=False,
    )
```

profile of v0, /device:TPU:4, one launch (start us, length us, event | category | flops | bytes accessed | tf_op | source)
XLA Modules:
  0.0 4318.2 jit_solution(12161429703156213365)
XLA Ops:
  15.1 76.6 %all-gather.10.cloned.1.call-done = bf16[2048,1024]{1,0:T(8,128)(2,1)} async-done(((bf16[512,1024]{1,0:T(8,128)(2,1)}), bf16[2048,1024]{1,0:T(8,128)(2,1)}) %all-gather.10.cloned.1.call-update) | async-done | bytes 4194320 | tf_op jit(solution)/shard_map/all_gather | solution.py:54
  95.1 146.3 %all-gather.8.cloned.1.call-done = bf16[2048,2048]{1,0:T(8,128)(2,1)} async-done(((bf16[512,2048]{1,0:T(8,128)(2,1)}), bf16[2048,2048]{1,0:T(8,128)(2,1)}) %all-gather.8.cloned.1.call-update) | async-done | bytes 8388624 | tf_op jit(solution)/shard_map/all_gather | solution.py:53
  241.3 7.1 multiply_convert_fusion.7
  264.7 18.0 all-to-all-done
  482.4 18.3 all_to_all.54
  508.8 8.5 multiply_convert_fusion.6
  517.3 22.8 all-gather.14.cloned.1.call-done
  540.1 6.9 multiply_reduce_fusion.6
  549.7 381.2 %all-gather.18.cloned.1.call-done = bf16[2048,5632]{1,0:T(8,128)(2,1)} async-done(((bf16[512,5632]{1,0:T(8,128)(2,1)}), bf16[2048,5632]{1,0:T(8,128)(2,1)}) %all-gather.18.cloned.1.call-update) | async-done | bytes 23068688 | tf_op jit(solution)/shard_map/all_gather | solution.py:60
  930.9 13.5 fusion.40
  944.4 377.3 %all-gather.16.cloned.1.call-done = bf16[2048,5632]{1,0:T(8,128)(2,1)} async-done(((bf16[512,5632]{1,0:T(8,128)(2,1)}), bf16[2048,5632]{1,0:T(8,128)(2,1)}) %all-gather.16.cloned.1.call-update) | async-done | bytes 23068688 | tf_op jit(solution)/shard_map/all_gather | solution.py:59
  1321.8 13.4 fusion.39
  1335.2 377.6 %all-gather.20.cloned.1.call-done = bf16[5632,2048]{1,0:T(8,128)(2,1)} async-done(((bf16[1408,2048]{1,0:T(8,128)(2,1)}), bf16[5632,2048]{1,0:T(8,128)(2,1)}) %all-gather.20.cloned.1.call-update) | async-done | bytes 23068688 | tf_op jit(solution)/shard_map/all_gather | solution.py:61
  1712.8 18.7 multiply_convert_fusion
  1731.5 12.5 fusion.41
  1744.0 14.5 multiply_reduce_fusion.2
  1758.5 14.8 multiply_reduce_fusion
  1773.3 9.0 multiply_reduce_fusion.3
  1943.4 8.8 rev.4
  1957.0 8.8 rev.5
  1977.7 18.3 all-to-all-done.3
  2006.8 8.2 convolution_dynamic-update-slice_fusion.4
  2019.5 8.3 convolution_dynamic-update-slice_fusion.3
  2027.9 8.2 convolution_dynamic-update-slice_fusion.2
  2036.0 19.6 convolution_dynamic-update-slice_fusion.1
  2055.6 19.8 convolution_dynamic-update-slice_fusion
  2075.5 27.2 fusion.43
  2105.8 7.5 fusion.42
  2114.8 8.9 fusion.16
  2123.7 40.2 all-reduce.84
  2168.0 1169.8 %reduce-scatter.3.cloned.1.call-done = f32[64,18432]{1,0:T(8,128)} async-done(((f32[2048,18432]{1,0:T(8,128)}), f32[64,18432]{1,0:T(8,128)}) %reduce-scatter.3.cloned.1.call-update) | async-done | bytes 4718608 | tf_op jit(solution)/shard_map/reduce_scatter | solution.py:176
  3345.6 965.8 %reduce-scatter.5.cloned.1.call-done = f32[176,2048]{1,0:T(8,128)} async-done(((f32[5632,2048]{1,0:T(8,128)}), f32[176,2048]{1,0:T(8,128)}) %reduce-scatter.5.cloned.1.call-update) | async-done | bytes 1441808 | tf_op jit(solution)/shard_map/reduce_scatter | solution.py:192
  (741 shorter events, 445.0 us)
Async XLA Ops:
  7.2 84.4 %all-gather.10.cloned.1.call-start = ((), (), s32[]{:S(2)}) async-start(), calls=%async_computation.7 | async-start | bytes 5242880 | tf_op jit(solution)/shard_map/all_gather | solution.py:54
  7.9 233.4 %all-gather.8.cloned.1.call-start = ((), (), s32[]{:S(2)}) async-start(), calls=%async_computation.6 | async-start | bytes 10485760 | tf_op jit(solution)/shard_map/all_gather | solution.py:53
  8.7 500.1 %all-gather.12.cloned.1.call-start = ((), (), s32[]{:S(2)}) async-start(), calls=%async_computation.8 | async-start | bytes 10485760 | tf_op jit(solution)/shard_map/all_gather | solution.py:55
  9.4 530.7 %all-gather.14.cloned.1.call-start = ((), (), s32[]{:S(2)}) async-start(), calls=%async_computation.9 | async-start | bytes 10485760 | tf_op jit(solution)/shard_map/all_gather | solution.py:56
  10.0 921.0 %all-gather.18.cloned.1.call-start = ((), (), s32[]{:S(2)}) async-start(), calls=%async_computation.11 | async-start | bytes 28835840 | tf_op jit(solution)/shard_map/all_gather | solution.py:60
  10.6 1311.2 %all-gather.16.cloned.1.call-start = ((), (), s32[]{:S(2)}) async-start(), calls=%async_computation.10 | async-start | bytes 28835840 | tf_op jit(solution)/shard_map/all_gather | solution.py:59
  11.2 1701.6 %all-gather.20.cloned.1.call-start = ((), (), s32[]{:S(2)}) async-start(), calls=%async_computation.12 | async-start | bytes 28835840 | tf_op jit(solution)/shard_map/all_gather | solution.py:61
  12.4 79.3 %copy-start.106 = (f32[1024]{0:T(1024)S(1)}, f32[1024]{0:T(1024)}, u32[]{:S(2)}) copy-start(f32[1024]{0:T(1024)} %param.22) | copy-start | bytes 12292
  15.0 226.3 %copy-start.4 = (bf16[256,2048]{1,0:T(8,128)(2,1)}, bf16[256,2048]{1,0:T(8,128)(2,1)S(1)}, u32[]{:S(2)}) copy-start(bf16[256,2048]{1,0:T(8,128)(2,1)S(1)} %fusion.10) | copy-start | bytes 3145732
  258.5 24.2 all-to-all-start
  264.6 28.8 copy-start.83
  264.6 28.8 copy-start.85
  264.7 28.8 copy-start.70
  399.3 19.1 copy-start.64
  400.6 17.8 copy-start.66
  403.5 19.8 copy-start.58
  403.5 19.8 copy-start.60
  1758.5 14.8 copy-start.15
  1758.5 14.8 copy-start.27
  1792.3 44.5 %all-to-all-start.2 = ((bf16[2,1024,2,128]{3,2,0,1:T(2,128)(2,1)}), bf16[2,1024,2,128]{3,2,0,1:T(2,128)(2,1)}, u32[]{:S(2)}, u32[]{:S(2)}) async-start(bf16[2,1024,2,128]{3,2,0,1:T(2,128)(2,1)} %copy.91), calls=%async_computation.2 | async-start | bytes 2097152 | tf_op jit(solution)/shard_map/all_to_all | solution.py:138
  1806.6 11.9 copy-start.39
  1818.5 14.9 copy-start.6
  1888.9 32.2 copy-start.37
  1895.1 28.8 copy-start.38
  1908.6 22.1 copy-start.65
  1908.6 22.1 copy-start.67
  1910.6 17.9 copy-start.72
  1910.7 17.8 copy-start.73
  1971.9 24.0 all-to-all-start.3
  1976.3 1361.5 %reduce-scatter.3.cloned.1.call-start = ((), (), s32[]{:S(2)}) async-start(), calls=%async_computation.13 | async-start | bytes 155713536 | tf_op jit(solution)/shard_map/reduce_scatter | solution.py:176
  2075.4 2236.0 %reduce-scatter.5.cloned.1.call-start = ((), (), s32[]{:S(2)}) async-start(), calls=%async_computation.14 | async-start | bytes 47579136 | tf_op jit(solution)/shard_map/reduce_scatter | solution.py:192
  2114.8 49.7 %copy-start.14 = (f32[256,2048]{1,0:T(8,128)S(1)}, f32[256,2048]{1,0:T(8,128)}, u32[]{:S(2)}) copy-start(f32[256,2048]{1,0:T(8,128)} %copy-done.12) | copy-start | bytes 6291460
  (87 other events, 446.7 us)
Sparse Core Ops, SparseCore 0:
  9.6 81.9 all-gather.9
  93.2 148.1 all-gather.7
  242.9 147.8 all-gather.11
  392.2 147.8 all-gather.13
  541.6 389.3 all-gather.17
  932.4 389.3 all-gather.15
  1323.4 389.3 all-gather.19
  2075.5 1262.2 reduce-scatter.2
  3340.8 970.5 reduce-scatter.4
where the time goes:
time: 4330 us; the launch traced here: 4320 us
  waiting for transfers between devices  3560 us (82%)
  local copies, waits for them, and re-layouts  330 us (8%)
  matrix products  236 us (5%)
  other arithmetic  104 us (2%)
  blocking collectives  58.5 us (1%)
    reduce_scatter x1, waiting for transfers between devices, body(): lax.psum_scatter(jnp.concatenate([product(normed_in, grad_input, 'td,ct->...  1170 us
    reduce_scatter x1, waiting for transfers between devices, body(): lax.psum_scatter(product(ffn_hidden, upstream, 'tf,td->fd'), ('seq', 'wsh...  966 us
    all_gather x1, waiting for transfers between devices, body(): lax.all_gather(w_ffup, 'wshard', axis=0, tiled=True)  381 us
    all_gather x1, waiting for transfers between devices, body(): lax.all_gather(w_down, 'wshard', axis=0, tiled=True)  378 us
    all_gather x1, waiting for transfers between devices, body(): lax.all_gather(w_ffgate, 'wshard', axis=0, tiled=True)  377 us
    dot_general x21, matrix products, product(): return jnp.einsum(form, left, right, preferred_element_type=jnp.float32)  236 us
    all_gather x1, waiting for transfers between devices, body(): lax.all_gather(w_in, 'wshard', axis=0, tiled=True)  146 us
    slice x132, local copies, waits for them, and re-layouts, body(): lax.associative_scan(combine, (next_re, next_im, arrive_re, arrive_im), r...  110 us
  transfers between devices with their start and end apart: 12, of which 10 were waited for; matrix products, arithmetic and copies ran while one was open for 9% of the time, Pallas kernels for 0%

commit v1 on v0

v1 whole, which is shorter than its diff:
```python
import functools

import jax
import jax.numpy as jnp
from jax import lax
from jax.experimental import pallas as pl
from jax.experimental.pallas import tpu as pltpu
from jax.sharding import PartitionSpec as P

LAYERS = 24
EPS = 1e-06
BF = jnp.bfloat16
F32 = jnp.float32


def dot(left, right, form):
    return jnp.einsum(form, left, right, preferred_element_type=F32)


def gather_seq(value):
    return lax.all_gather(value, "seq", axis=0, tiled=True)


def scatter_seq(value):
    return lax.psum_scatter(value, "seq", scatter_dimension=0, tiled=True)


def gather_shard(value):
    return lax.all_gather(value, "wshard", axis=0, tiled=True)


def scatter_shard(value):
    return lax.psum_scatter(value, "wshard", scatter_dimension=0, tiled=True)


def column_parts(array, count):
    width = array.shape[-1] // count
    if width % 128 == 0:
        return [(array, width, index) for index in range(count)]
    return [
        (array[..., index * width : (index + 1) * width], width, 0) for index in range(count)
    ]


def part_spec(groups, tokens, width, index):
    mode = pl.Buffered(1) if groups * tokens > 2048 else None
    return pl.BlockSpec(
        (groups, 1, tokens, width), lambda b, index=index: (0, b, 0, index), pipeline_mode=mode
    )


def row_spec(width, index):
    return pl.BlockSpec((1, width), lambda b, index=index: (0, index))


def flat(ref):
    groups, _, tokens, width = ref.shape
    return ref[...].reshape(groups * tokens, width)


def forward_kernel(
    floor_ref,
    pre_re,
    pre_im,
    pre_forget,
    gate_re,
    gate_im,
    flag_ref,
    bias_ref,
    theta_ref,
    gain_re,
    gain_im,
    state_re,
    state_im,
    gated_re,
    gated_im,
    square_ref,
    keep_s,
    val_re,
    val_im,
    prod_re,
    prod_im,
    carry_re,
    carry_im,
):
    groups, _, tokens, width = pre_re.shape
    floor = floor_ref[0]
    cosine = jnp.cos(theta_ref[...])
    sine = jnp.sin(theta_ref[...])
    logit = (flat(pre_forget) + bias_ref[...]).astype(BF).astype(F32)
    keep = (floor + (1.0 - floor) * jax.nn.sigmoid(logit)) * (1.0 - flat(flag_ref))
    keep_s[...] = keep
    fresh = 1.0 - keep
    value = flat(pre_re)
    val_re[...] = fresh * (value * jax.nn.sigmoid(value)).astype(BF).astype(F32)
    value = flat(pre_im)
    val_im[...] = fresh * (value * jax.nn.sigmoid(value)).astype(BF).astype(F32)

    def step(t, carry):
        h_re, h_im, p_re, p_im = carry
        rows = pl.ds(t, groups, stride=tokens)
        held = keep_s[rows, :]
        a_re = held * cosine
        a_im = held * sine
        n_re = a_re * h_re - a_im * h_im + val_re[rows, :]
        n_im = a_re * h_im + a_im * h_re + val_im[rows, :]
        q_re = a_re * p_re - a_im * p_im
        q_im = a_re * p_im + a_im * p_re
        val_re[rows, :] = n_re
        val_im[rows, :] = n_im
        prod_re[rows, :] = q_re
        prod_im[rows, :] = q_im
        return n_re, n_im, q_re, q_im

    zero = jnp.zeros((groups, width), F32)
    lax.fori_loop(0, tokens, step, (zero, zero, zero + 1.0, zero), unroll=8)
    c_re = jnp.zeros((1, width), F32)
    c_im = jnp.zeros((1, width), F32)
    for group in range(groups):
        carry_re[group : group + 1, :] = c_re
        carry_im[group : group + 1, :] = c_im
        last = (group + 1) * tokens - 1
        p_re = prod_re[last : last + 1, :]
        p_im = prod_im[last : last + 1, :]
        c_re, c_im = (
            p_re * c_re - p_im * c_im + val_re[last : last + 1, :],
            p_re * c_im + p_im * c_re + val_im[last : last + 1, :],
        )
    for group in range(groups):
        rows = slice(group * tokens, (group + 1) * tokens)
        c_re = carry_re[group : group + 1, :]
        c_im = carry_im[group : group + 1, :]
        p_re = prod_re[rows, :]
        p_im = prod_im[rows, :]
        h_re = val_re[rows, :] + p_re * c_re - p_im * c_im
        h_im = val_im[rows, :] + p_re * c_im + p_im * c_re
        state_re[group, 0] = h_re
        state_im[group, 0] = h_im
        m_re = h_re.astype(BF).astype(F32)
        m_im = h_im.astype(BF).astype(F32)
        gated_re[group, 0] = (m_re * gain_re[...] * jax.nn.sigmoid(gate_re[group, 0])).astype(BF)
        gated_im[group, 0] = (m_im * gain_im[...] * jax.nn.sigmoid(gate_im[group, 0])).astype(BF)
        square_ref[group, 0] = jnp.sum(m_re * m_re + m_im * m_im, axis=1, keepdims=True)


def backward_kernel(
    floor_ref,
    pre_re,
    pre_im,
    pre_forget,
    gate_re,
    gate_im,
    flag_ref,
    bias_ref,
    theta_ref,
    gain_re,
    gain_im,
    state_re,
    state_im,
    up_re,
    up_im,
    scale_ref,
    term_ref,
    out_re,
    out_im,
    out_forget,
    out_gate_re,
    out_gate_im,
    sum_bias,
    sum_theta,
    sum_gain_re,
    sum_gain_im,
    keep_s,
    adj_re,
    adj_im,
    prod_re,
    prod_im,
    carry_re,
    carry_im,
):
    groups, _, tokens, width = pre_re.shape
    rows_all = groups * tokens
    floor = floor_ref[0]
    cosine = jnp.cos(theta_ref[...])
    sine = jnp.sin(theta_ref[...])
    open_ = 1.0 - flat(flag_ref)
    logit = (flat(pre_forget) + bias_ref[...]).astype(BF).astype(F32)
    sig_forget = jax.nn.sigmoid(logit)
    keep = (floor + (1.0 - floor) * sig_forget) * open_
    keep_s[0:rows_all, :] = keep
    keep_s[rows_all : rows_all + tokens, :] = jnp.zeros((tokens, width), F32)
    scale = flat(scale_ref)
    term = flat(term_ref)

    @pl.when(pl.program_id(0) == 0)
    def _():
        sum_bias[...] = jnp.zeros_like(sum_bias)
        sum_theta[...] = jnp.zeros_like(sum_theta)
        sum_gain_re[...] = jnp.zeros_like(sum_gain_re)
        sum_gain_im[...] = jnp.zeros_like(sum_gain_im)

    for state, up, gate, gain, sum_gain, out_gate, adj in (
        (state_re, up_re, gate_re, gain_re, sum_gain_re, out_gate_re, adj_re),
        (state_im, up_im, gate_im, gain_im, sum_gain_im, out_gate_im, adj_im),
    ):
        mixed = flat(state).astype(BF).astype(F32)
        grad = flat(up)
        sig = jax.nn.sigmoid(flat(gate))
        inner = grad * sig
        normed = inner * mixed * scale
        sum_gain[...] += jnp.sum(normed, axis=0, keepdims=True)
        gate_grad = (normed * gain[...] * (1.0 - sig)).astype(BF)
        out_gate[...] = gate_grad.reshape(out_gate.shape)
        adj[...] = (scale * (inner * gain[...]) - mixed * term).astype(BF).astype(F32)

    def step(index, carry):
        g_re, g_im, p_re, p_im = carry
        t = tokens - 1 - index
        rows = pl.ds(t, groups, stride=tokens)
        held = keep_s[pl.ds(t + 1, groups, stride=tokens), :]
        a_re = held * cosine
        a_im = held * sine
        n_re = a_re * g_re + a_im * g_im + adj_re[rows, :]
        n_im = a_re * g_im - a_im * g_re + adj_im[rows, :]
        q_re = a_re * p_re + a_im * p_im
        q_im = a_re * p_im - a_im * p_re
        adj_re[rows, :] = n_re
        adj_im[rows, :] = n_im
        prod_re[rows, :] = q_re
        prod_im[rows, :] = q_im
        return n_re, n_im, q_re, q_im

    zero = jnp.zeros((groups, width), F32)
    lax.fori_loop(0, tokens, step, (zero, zero, zero + 1.0, zero), unroll=8)
    c_re = jnp.zeros((1, width), F32)
    c_im = jnp.zeros((1, width), F32)
    for group in reversed(range(groups)):
        carry_re[group : group + 1, :] = c_re
        carry_im[group : group + 1, :] = c_im
        first = group * tokens
        p_re = prod_re[first : first + 1, :]
        p_im = prod_im[first : first + 1, :]
        c_re, c_im = (
            p_re * c_re - p_im * c_im + adj_re[first : first + 1, :],
            p_re * c_im + p_im * c_re + adj_im[first : first + 1, :],
        )
    row_index = lax.broadcasted_iota(jnp.int32, (tokens, width), 0)
    tail_re = jnp.zeros((1, width), F32)
    tail_im = jnp.zeros((1, width), F32)
    total_theta = jnp.zeros((1, width), F32)
    total_bias = jnp.zeros((1, width), F32)
    for group in range(groups):
        rows = slice(group * tokens, (group + 1) * tokens)
        c_re = carry_re[group : group + 1, :]
        c_im = carry_im[group : group + 1, :]
        p_re = prod_re[rows, :]
        p_im = prod_im[rows, :]
        g_re = adj_re[rows, :] + p_re * c_re - p_im * c_im
        g_im = adj_im[rows, :] + p_re * c_im + p_im * c_re
        h_re = state_re[group, 0]
        h_im = state_im[group, 0]
        prev_re = jnp.where(row_index == 0, tail_re, pltpu.roll(h_re, 1, 0))
        prev_im = jnp.where(row_index == 0, tail_im, pltpu.roll(h_im, 1, 0))
        tail_re = h_re[tokens - 1 :, :]
        tail_im = h_im[tokens - 1 :, :]
        turn_re = cosine * prev_re - sine * prev_im
        turn_im = sine * prev_re + cosine * prev_im
        held = keep_s[rows, :]
        fresh = 1.0 - held
        x_re = pre_re[group, 0]
        x_im = pre_im[group, 0]
        s_re = jax.nn.sigmoid(x_re)
        s_im = jax.nn.sigmoid(x_im)
        cand_re = (x_re * s_re).astype(BF).astype(F32)
        cand_im = (x_im * s_im).astype(BF).astype(F32)
        grad_keep = g_re * (turn_re - cand_re) + g_im * (turn_im - cand_im)
        total_theta -= jnp.sum(
            held * (g_re * turn_im - g_im * turn_re), axis=0, keepdims=True
        )
        logit = (pre_forget[group, 0] + bias_ref[...]).astype(BF).astype(F32)
        sig = jax.nn.sigmoid(logit)
        grad_forget = (
            grad_keep * (1.0 - flag_ref[group, 0]) * ((1.0 - floor) * (sig * (1.0 - sig)))
        ).astype(BF)
        total_bias += jnp.sum(grad_forget.astype(F32), axis=0, keepdims=True)
        out_forget[group, 0] = grad_forget
        cand_grad = (fresh * g_re).astype(BF).astype(F32)
        out_re[group, 0] = (cand_grad * s_re * (1.0 + x_re * (1.0 - s_re))).astype(BF)
        cand_grad = (fresh * g_im).astype(BF).astype(F32)
        out_im[group, 0] = (cand_grad * s_im * (1.0 + x_im * (1.0 - s_im))).astype(BF)
    sum_theta[...] += total_theta
    sum_bias[...] += total_bias


def recur_forward(floor, pre, flags, bias, theta, gain):
    groups, seqs, tokens, _ = pre.shape
    parts = column_parts(pre, 5)
    width = parts[0][1]
    gains = column_parts(gain, 2)
    operands = [floor] + [p[0] for p in parts] + [flags, bias, theta] + [g[0] for g in gains]
    in_specs = (
        [pl.BlockSpec(memory_space=pltpu.SMEM)]
        + [part_spec(groups, tokens, width, p[2]) for p in parts]
        + [part_spec(groups, tokens, 1, 0), row_spec(width, 0), row_spec(width, 0)]
        + [row_spec(width, g[2]) for g in gains]
    )
    whole = pltpu.VMEM((groups * tokens, width), F32)
    shape = (groups, seqs, tokens, width)
    return pl.pallas_call(
        forward_kernel,
        grid=(seqs,),
        in_specs=in_specs,
        out_specs=[part_spec(groups, tokens, width, 0)] * 4 + [part_spec(groups, tokens, 1, 0)],
        out_shape=[
            jax.ShapeDtypeStruct(shape, F32),
            jax.ShapeDtypeStruct(shape, F32),
            jax.ShapeDtypeStruct(shape, BF),
            jax.ShapeDtypeStruct(shape, BF),
            jax.ShapeDtypeStruct((groups, seqs, tokens, 1), F32),
        ],
        scratch_shapes=[whole] * 5 + [pltpu.VMEM((groups, width), F32)] * 2,
        compiler_params=pltpu.CompilerParams(vmem_limit_bytes=56 * 2**20),
        cost_estimate=pl.CostEstimate(
            flops=60 * groups * seqs * tokens * width,
            bytes_accessed=32 * groups * seqs * tokens * width,
            transcendentals=5 * groups * seqs * tokens * width,
        ),
        name="recur_forward",
    )(*operands)


def recur_backward(floor, pre, flags, bias, theta, gain, state_re, state_im, up, scale, term):
    groups, seqs, tokens, _ = pre.shape
    parts = column_parts(pre, 5)
    width = parts[0][1]
    gains = column_parts(gain, 2)
    ups = column_parts(up, 2)
    operands = (
        [floor]
        + [p[0] for p in parts]
        + [flags, bias, theta]
        + [g[0] for g in gains]
        + [state_re, state_im]
        + [u[0] for u in ups]
        + [scale, term]
    )
    one = part_spec(groups, tokens, 1, 0)
    in_specs = (
        [pl.BlockSpec(memory_space=pltpu.SMEM)]
        + [part_spec(groups, tokens, width, p[2]) for p in parts]
        + [one, row_spec(width, 0), row_spec(width, 0)]
        + [row_spec(width, g[2]) for g in gains]
        + [part_spec(groups, tokens, width, 0)] * 2
        + [part_spec(groups, tokens, width, u[2]) for u in ups]
        + [one, one]
    )
    whole = pltpu.VMEM((groups * tokens, width), F32)
    shape = (groups, seqs, tokens, width)
    return pl.pallas_call(
        backward_kernel,
        grid=(seqs,),
        in_specs=in_specs,
        out_specs=[part_spec(groups, tokens, width, 0)] * 5 + [row_spec(width, 0)] * 4,
        out_shape=[jax.ShapeDtypeStruct(shape, BF)] * 5
        + [jax.ShapeDtypeStruct((1, width), F32)] * 4,
        scratch_shapes=[pltpu.VMEM(((groups + 1) * tokens, width), F32)]
        + [whole] * 4
        + [pltpu.VMEM((groups, width), F32)] * 2,
        compiler_params=pltpu.CompilerParams(vmem_limit_bytes=56 * 2**20),
        cost_estimate=pl.CostEstimate(
            flops=100 * groups * seqs * tokens * width,
            bytes_accessed=50 * groups * seqs * tokens * width,
            transcendentals=8 * groups * seqs * tokens * width,
        ),
        name="recur_backward",
    )(*operands)


def body(
    tokens,
    starts,
    layer_index,
    gain_mix,
    w_in,
    w_forget,
    bias_forget,
    theta,
    w_gate_out,
    gain_out,
    w_out,
    gain_ffn,
    w_ffgate,
    w_ffup,
    w_down,
    out_grad,
):
    seqs, seq_dev, width = tokens.shape
    rows = seqs * seq_dev
    groups = lax.axis_size("seq")
    planes = lax.axis_size("wshard")
    devices = groups * planes
    place = lax.axis_index("seq")
    total = groups * rows
    floor = layer_index.astype(F32) / LAYERS

    def own_columns(array):
        block = w_out.shape[0] if array.shape[-1] % w_down.shape[0] else w_down.shape[0]
        run = block // groups
        split = array.reshape(array.shape[:-1] + (array.shape[-1] // block, block))
        part = lax.dynamic_slice_in_dim(split, place * run, run, split.ndim - 1)
        return part.reshape(array.shape[:-1] + (-1,))

    def own_rows(array):
        run = array.shape[0] // groups
        return lax.dynamic_slice_in_dim(array, place * run, run, 0)

    rec_w = gather_shard(
        jnp.concatenate(
            [own_columns(w_in), own_columns(w_forget), own_columns(w_gate_out)], axis=1
        )
    )
    out_w = gather_shard(own_rows(w_out))
    ff_w = gather_shard(jnp.concatenate([own_columns(w_ffgate), own_columns(w_ffup)], axis=1))
    down_w = gather_shard(own_rows(w_down))
    hidden = down_w.shape[0]
    mixw = out_w.shape[0]
    chan = mixw // 2

    resid_in = tokens.reshape(rows, width).astype(F32)
    scale_in = lax.rsqrt(jnp.mean(resid_in * resid_in, axis=1, keepdims=True) + EPS)
    normed_in_own = (resid_in * scale_in * gain_mix).astype(BF)
    normed_in = gather_seq(normed_in_own)
    upstream_own = out_grad.reshape(rows, width)
    upstream = gather_seq(upstream_own)

    flags = starts.astype(F32).reshape(seqs, groups, seq_dev).transpose(1, 0, 2)[..., None]
    bias_own = own_columns(bias_forget[None])
    theta_own = own_columns(theta[None])
    gain_own = own_columns(gain_out[None])

    pre = dot(normed_in, rec_w, "td,dc->tc").reshape(groups, seqs, seq_dev, 5 * chan)
    state_re, state_im, gated_re, gated_im, square = recur_forward(
        floor, pre, flags, bias_own, theta_own, gain_own
    )
    gated = jnp.concatenate([gated_re, gated_im], axis=-1).reshape(total, mixw)
    mean_square = lax.psum(square.reshape(groups, rows), "seq") / width
    scale_all = lax.rsqrt(mean_square + EPS)
    scale_out = lax.dynamic_index_in_dim(scale_all, place, 0, keepdims=False)[:, None]
    branch_mix = scale_out * scatter_seq(dot(gated, out_w, "tc,cd->td").astype(BF)).astype(F32)
    resid = resid_in + branch_mix
    scale_ffn = lax.rsqrt(jnp.mean(resid * resid, axis=1, keepdims=True) + EPS)
    normed_ffn = gather_seq((resid * scale_ffn * gain_ffn).astype(BF))

    ff = dot(normed_ffn, ff_w, "td,df->tf")
    ffn_gate, ffn_up = ff[:, :hidden], ff[:, hidden:]
    sig_ffn = jax.nn.sigmoid(ffn_gate)
    silu_ffn = ffn_gate * sig_ffn
    ffn_hidden = (silu_ffn * ffn_up).astype(BF)
    grad_hidden = dot(upstream, down_w, "td,fd->tf")
    grad_gate = (grad_hidden * ffn_up * sig_ffn * (1.0 + ffn_gate * (1.0 - sig_ffn))).astype(BF)
    grad_up = (grad_hidden * silu_ffn).astype(BF)
    grad_ff = jnp.concatenate([grad_gate, grad_up], axis=1)
    grad_normed_ffn = scatter_seq(dot(grad_ff, ff_w, "tf,df->td").astype(BF)).astype(F32)
    branch_ffn = scatter_seq(dot(ffn_hidden, down_w, "tf,fd->td").astype(BF)).astype(F32)
    result = (resid + branch_ffn).astype(BF)

    scaled_ffn = grad_normed_ffn * gain_ffn
    grad_resid = (
        upstream_own.astype(F32)
        + scale_ffn * scaled_ffn
        - resid * scale_ffn**3 * jnp.mean(scaled_ffn * resid, axis=1, keepdims=True)
    )
    grad_gain_ffn = jnp.sum(grad_normed_ffn * resid * scale_ffn, axis=0)
    grad_branch_own = grad_resid.astype(BF)
    overlap = jnp.sum(grad_branch_own.astype(F32) * branch_mix, axis=1)
    term_own = scale_out[:, 0] ** 2 * overlap / width
    term_all = lax.all_gather(term_own, "seq", axis=0, tiled=True)
    grad_branch = gather_seq(grad_branch_own)
    grad_gated = dot(grad_branch, out_w, "td,cd->tc").reshape(groups, seqs, seq_dev, mixw)

    shape_one = (groups, seqs, seq_dev, 1)
    *grad_parts, sum_bias, sum_theta, sum_gain_re, sum_gain_im = recur_backward(
        floor,
        pre,
        flags,
        bias_own,
        theta_own,
        gain_own,
        state_re,
        state_im,
        grad_gated,
        scale_all.reshape(shape_one),
        term_all.reshape(shape_one),
    )
    grad_pre = jnp.concatenate(grad_parts, axis=-1).reshape(total, 5 * chan)
    grad_normed_in = scatter_seq(dot(grad_pre, rec_w, "tc,dc->td").astype(BF)).astype(F32)
    scaled_in = grad_normed_in * gain_mix
    grad_tokens = (
        grad_resid
        + scale_in * scaled_in
        - resid_in * scale_in**3 * jnp.mean(scaled_in * resid_in, axis=1, keepdims=True)
    ).astype(BF)
    grad_gain_mix = jnp.sum(grad_normed_in * resid_in * scale_in, axis=0)

    def to_owner(grad):
        run = grad.shape[0] // devices
        part = grad.astype(BF).reshape(groups, planes, run, -1).transpose(1, 0, 2, 3)
        part = scatter_shard(part.reshape(grad.shape))
        part = part.reshape(groups, run, -1)
        return lax.all_to_all(part, "seq", split_axis=0, concat_axis=0, tiled=True)

    def columns(part, block_run):
        source, run, cols = part.shape
        split = part.reshape(source, run, cols // block_run, block_run)
        return split.transpose(1, 2, 0, 3).reshape(run, -1).astype(F32)

    scaled_gated = (
        gated.astype(F32) * scale_all.reshape(total, 1)
    ).astype(BF)
    ff_grad = to_owner(dot(normed_ffn, grad_ff, "td,tf->df"))
    grad_w_ffgate = columns(ff_grad[..., :hidden], hidden // planes)
    grad_w_ffup = columns(ff_grad[..., hidden:], hidden // planes)
    rec_grad = to_owner(dot(normed_in, grad_pre, "td,tc->dc"))
    grad_w_in = columns(rec_grad[..., :mixw], mixw // planes)
    grad_w_forget = columns(rec_grad[..., mixw : mixw + chan], mixw // planes)
    grad_w_gate = columns(rec_grad[..., mixw + chan :], mixw // planes)

    pairs = []
    for s in range(groups):
        for w in range(planes):
            block = w * groups + s
            pairs.append((s * planes + w, block))

    def rows_to_owner(grad):
        part = scatter_shard(grad.astype(BF))
        return lax.ppermute(part, ("seq", "wshard"), pairs).astype(F32)

    grad_w_down = rows_to_owner(dot(ffn_hidden, upstream, "tf,td->fd"))
    grad_w_out = rows_to_owner(dot(scaled_gated, grad_branch, "tc,td->cd"))

    def spread(part, count):
        run = mixw // planes
        zero = jnp.zeros((count, groups, run), F32)
        zero = lax.dynamic_update_slice(zero, part.reshape(count, 1, run), (0, place, 0))
        return zero.reshape(-1)

    squares = jnp.stack(
        [
            jnp.sum(resid_in * resid_in),
            jnp.sum(branch_mix * branch_mix),
            jnp.sum(branch_ffn * branch_ffn),
        ]
    )
    half = planes // 2
    grad_gain_mix, grad_bias, grad_theta, grad_gain_out, grad_gain_ffn, squares = lax.psum(
        (
            grad_gain_mix,
            spread(sum_bias, half),
            spread(sum_theta, half),
            spread(jnp.concatenate([sum_gain_re, sum_gain_im], axis=1), planes),
            grad_gain_ffn,
            squares,
        ),
        ("seq", "wshard"),
    )
    rms_values = jnp.sqrt(squares / (rows * width * devices))
    return (
        result.reshape(seqs, seq_dev, width),
        grad_tokens.reshape(seqs, seq_dev, width),
        grad_gain_mix,
        grad_w_in,
        grad_w_forget,
        grad_bias,
        grad_theta,
        grad_w_gate,
        grad_gain_out,
        grad_w_out,
        grad_gain_ffn,
        grad_w_ffgate,
        grad_w_ffup,
        grad_w_down,
        rms_values,
    )


def solution(mesh):
    whole = P()
    rowed = P("wshard", None)
    stream = P("wshard", "seq", None)
    owned = P(("seq", "wshard"), None)
    return jax.shard_map(
        body,
        mesh=mesh,
        in_specs=(
            stream,
            rowed,
            whole,
            whole,
            rowed,
            rowed,
            whole,
            whole,
            rowed,
            whole,
            rowed,
            whole,
            rowed,
            rowed,
            rowed,
            stream,
        ),
        out_specs=(
            stream,
            stream,
            whole,
            owned,
            owned,
            whole,
            whole,
            owned,
            whole,
            owned,
            whole,
            owned,
            owned,
            owned,
            whole,
        ),
        check_vma=False,
    )
```

time: 4330 us -> 1170 us (0.27)
  waiting for transfers between devices: 3560 us -> 785 us
  local copies, waits for them, and re-layouts: 330 us -> 78.2 us
  matrix products: 236 us -> 145 us
  other arithmetic: 104 us -> 36 us
    reduce_scatter x2 -> x8, waiting for transfers between devices: 2140 us -> 408 us  [the longest x4 218 us: scatter_seq(): return lax.psum_scatter(value, 'seq', scatter_dimension=0, tiled=True)]
    all_gather x7 -> x8, waiting for transfers between devices: 1380 us -> 377 us  [the longest x4 200 us: gather_shard(): return lax.all_gather(value, 'wshard', axis=0, tiled=True)]
    slice x258 -> x0, local copies, waits for them, and re-layouts: 223 us -> none  [the longest x132 110 us: body(): lax.associative_scan(combine, (next_re, next_im, arrive_re, arrive_im), r...]
    dot_general x21 -> x12, matrix products: 236 us -> 145 us  [dot(): return jnp.einsum(form, left, right, preferred_element_type=F32)]
    add x69 -> x0, other arithmetic: 43.9 us -> none  [the longest x24 17.2 us: combine(): right_re * base_im + right_im * base_re + add_im]
  transfers between devices with their start and end apart: 12 -> 20, of which waited for: 10 -> 16; matrix products, arithmetic and copies ran while one was open for 9% -> 16% of each run, Pallas kernels for 0% -> 2%
where the time goes in v1:
time: 1170 us; the launch traced here: 1160 us
  waiting for transfers between devices  785 us (67%)
  matrix products  145 us (12%)
  local copies, waits for them, and re-layouts  78.2 us (7%)
  blocking collectives  62.9 us (5%)
  other arithmetic  36 us (3%)
  Pallas kernels  25.2 us (2%)
  between operations  15.5 us (1%)
  starting transfers between devices  15.1 us (1%)
    reduce_scatter x4, waiting for transfers between devices, scatter_seq(): return lax.psum_scatter(value, 'seq', scatter_dimension=0, tiled=True)  218 us
    all_gather x4, waiting for transfers between devices, gather_shard(): return lax.all_gather(value, 'wshard', axis=0, tiled=True)  200 us
    reduce_scatter x4, waiting for transfers between devices, scatter_shard(): return lax.psum_scatter(value, 'wshard', scatter_dimension=0, tiled=True)  189 us
    all_gather x4, waiting for transfers between devices, gather_seq(): return lax.all_gather(value, 'seq', axis=0, tiled=True)  177 us
    dot_general x12, matrix products, dot(): return jnp.einsum(form, left, right, preferred_element_type=F32)  145 us
    psum x1, blocking collectives, body(): lax.psum((grad_gain_mix, spread(sum_bias, half), spread(sum_theta, half),...  41.3 us
    unnamed x74, local copies, waits for them, and re-layouts  35.4 us
    convert_element_type x15, local copies, waits for them, and re-layouts, columns(): return split.transpose(1, 2, 0, 3).reshape(run, -1).astype(F32)  24.2 us
  transfers between devices with their start and end apart: 20, of which 16 were waited for; matrix products, arithmetic and copies ran while one was open for 16% of the time, Pallas kernels for 2%

profile of v1, /device:TPU:4, one launch (start us, length us, event | category | flops | bytes accessed | tf_op | source)
XLA Modules:
  0.0 1163.1 jit_solution(10724290346191877291)
XLA Ops:
  29.2 47.5 %all-gather.12.cloned.1.call-done = bf16[2048,640]{0,1:T(8,128)(2,1)} async-done(((bf16[512,640]{0,1:T(8,128)(2,1)}), bf16[2048,640]{0,1:T(8,128)(2,1)}) %all-gather.12.cloned.1.call-update) | async-done | bytes 2621456 | tf_op jit(solution)/shard_map/all_gather | solution.py:29
  76.6 55.3 %all-gather.10.cloned.1.call-done = bf16[2048,2048]{1,0:T(8,128)(2,1)} async-done(((bf16[256,2048]{1,0:T(8,128)(2,1)}), bf16[2048,2048]{1,0:T(8,128)(2,1)}) %all-gather.10.cloned.1.call-update) | async-done | bytes 8388624 | tf_op jit(solution)/shard_map/all_gather | solution.py:21
  132.0 11.5 fusion.34
  143.5 10.3 recur_forward.1
  155.1 7.4 all-gather.14.cloned.1.call-done
  169.4 8.4 copy.69
  177.8 8.9 copy.68
  191.0 13.6 %psum.49 = f32[8,256]{1,0:T(8,128)S(1)} all-reduce(f32[8,256]{1,0:T(8,128)S(1)} %bitcast.191), channel_id=1, replica_groups=mesh['seq'=8,'wshard'=4] {'seq'}, use_global_device_ids=true, to_apply=%region_1.0 | all-reduce | flops 2048 | bytes 16384 | tf_op jit(solution)/shard_map/psum | solution.py:446
  205.2 35.3 %reduce-scatter.9.cloned.1.call-done = bf16[256,2048]{1,0:T(8,128)(2,1)} async-done(((bf16[2048,2048]{1,0:T(8,128)(2,1)}), bf16[256,2048]{1,0:T(8,128)(2,1)}) %reduce-scatter.9.cloned.1.call-update) | async-done | bytes 1048592 | tf_op jit(solution)/shard_map/reduce_scatter | solution.py:25
  247.1 102.3 %all-gather.18.cloned.1.call-done = bf16[2048,1408]{0,1:T(8,128)(2,1)} async-done(((bf16[512,1408]{0,1:T(8,128)(2,1)}), bf16[2048,1408]{0,1:T(8,128)(2,1)}) %all-gather.18.cloned.1.call-update) | async-done | bytes 5767184 | tf_op jit(solution)/shard_map/all_gather | solution.py:29
  349.4 54.8 %all-gather.16.cloned.1.call-done = bf16[2048,2048]{1,0:T(8,128)(2,1)} async-done(((bf16[256,2048]{1,0:T(8,128)(2,1)}), bf16[2048,2048]{1,0:T(8,128)(2,1)}) %all-gather.16.cloned.1.call-update) | async-done | bytes 8388624 | tf_op jit(solution)/shard_map/all_gather | solution.py:21
  404.2 18.7 %fusion.35 = f32[2048,1408]{0,1:T(8,128)} fusion(bf16[2048,2048]{1,0:T(8,128)(2,1)} %all-gather.16.cloned.1.call-done, bf16[2048,1408]{0,1:T(8,128)(2,1)} %all-gather.18.cloned.1.call-done), kind=kOutput, calls=%fused_computation.101 | convolution fusion | flops 11811160064 | bytes 25690112 | tf_op jit(solution)/shard_map/td,df->tf/dot_general | solution.py:17
  422.9 42.5 %all-gather.20.cloned.1.call-done = bf16[704,2048]{1,0:T(8,128)(2,1)} async-done(((bf16[176,2048]{1,0:T(8,128)(2,1)}), bf16[704,2048]{1,0:T(8,128)(2,1)}) %all-gather.20.cloned.1.call-update) | async-done | bytes 2883600 | tf_op jit(solution)/shard_map/all_gather | solution.py:29
  465.4 54.8 %all-gather.22.cloned.1.call-done = bf16[2048,2048]{1,0:T(8,128)(2,1)} async-done(((bf16[256,2048]{1,0:T(8,128)(2,1)}), bf16[2048,2048]{1,0:T(8,128)(2,1)}) %all-gather.22.cloned.1.call-update) | async-done | bytes 8388624 | tf_op jit(solution)/shard_map/all_gather | solution.py:21
  520.2 15.8 %fusion.2 = (bf16[2048,704]{0,1:T(8,128)(2,1)S(1)}, bf16[2048,704]{0,1:T(8,128)(2,1)}, bf16[2048,704]{0,1:T(8,128)(2,1)}) fusion(f32[2048,1408]{0,1:T(8,128)} %fusion.35, bf16[704,2048]{1,0:T(8,128)(2,1)} %all-gather.20.cloned.1.call-done, bf16[2048,2048]{1,0:T(8,128)(2,1)} %all-gather.22.cloned.1.call-done), kind=kOutput, calls=%fused_computation.10 | convolution fusion | flops 5927206912 | bytes 31457280 | tf_op jit(solution)/shard_map/td,fd->tf/dot_general | solution.py:17
  537.6 17.6 %convolution_convert_fusion.1 = bf16[2048,2048]{1,0:T(8,128)(2,1)} fusion(bf16[2048,1408]{0,1:T(8,128)(2,1)S(1)} %copy-done.27, bf16[2048,704]{0,1:T(8,128)(2,1)} %get-tuple-element.59, bf16[2048,704]{0,1:T(8,128)(2,1)S(1)} %get-tuple-element.58), kind=kOutput, calls=%fused_computation.1 | convolution fusion | flops 11826888704 | bytes 19922944 | tf_op jit(solution)/shard_map/tf,df->td/dot_general | solution.py:17
  555.3 71.6 %reduce-scatter.13.cloned.1.call-done = bf16[256,2048]{1,0:T(8,128)(2,1)} async-done(((bf16[2048,2048]{1,0:T(8,128)(2,1)}), bf16[256,2048]{1,0:T(8,128)(2,1)}) %reduce-scatter.13.cloned.1.call-update) | async-done | bytes 1048592 | tf_op jit(solution)/shard_map/reduce_scatter | solution.py:25
  632.2 17.2 %convolution_convert_fusion.4 = bf16[2048,1408]{1,0:T(8,128)(2,1)S(1)} fusion(bf16[2048,2048]{1,0:T(8,128)(2,1)} %all-gather.16.cloned.1.call-done, bf16[2048,704]{0,1:T(8,128)(2,1)} %get-tuple-element.59, bf16[2048,704]{0,1:T(8,128)(2,1)} %copy-done.30), kind=kOutput, calls=%fused_computation.4 | convolution fusion | flops 11825577984 | bytes 19922944 | tf_op jit(solution)/shard_map/td,tf->df/dot_general | solution.py:17
  652.5 10.6 convolution_convert_fusion.5
  664.7 8.0 all-gather
  674.1 12.4 %all-gather.24.cloned.1.call-done = bf16[2048,2048]{1,0:T(8,128)(2,1)} async-done(((bf16[256,2048]{1,0:T(8,128)(2,1)}), bf16[2048,2048]{1,0:T(8,128)(2,1)}) %all-gather.24.cloned.1.call-update) | async-done | bytes 8388624 | tf_op jit(solution)/shard_map/all_gather | solution.py:21
  693.5 14.9 %recur_backward.1 = (bf16[8,2,128,128]{3,2,1,0:T(8,128)(2,1)}, bf16[8,2,128,128]{3,2,1,0:T(8,128)(2,1)}, bf16[8,2,128,128]{3,2,1,0:T(8,128)(2,1)}, bf16[8,2,128,...) custom-call(f32[1]{0:T(128)S(6)} %div.31.floor_ref, ...), custom_call_target="tpu_custom_call" | custom-call | flops 26214400 | bytes 13107200 | tf_op jit(solution)/shard_map/recur_backward/pallas_call | solution.py:359
  712.4 10.2 convolution_convert_fusion.6
  732.7 11.2 convolution_convert_fusion
  743.9 11.3 convolution_convert_fusion.2
  755.2 36.1 %reduce-scatter.21.cloned.1.call-done = bf16[512,1408]{1,0:T(8,128)(2,1)} async-done(((bf16[2048,1408]{1,0:T(8,128)(2,1)}), bf16[512,1408]{1,0:T(8,128)(2,1)}) %reduce-scatter.21.cloned.1.call-update) | async-done | bytes 1441808 | tf_op jit(solution)/shard_map/reduce_scatter | solution.py:33
  795.6 54.7 %reduce-scatter.23.cloned.1.call-done = bf16[176,2048]{1,0:T(8,128)(2,1)} async-done(((bf16[704,2048]{1,0:T(8,128)(2,1)}), bf16[176,2048]{1,0:T(8,128)(2,1)}) %reduce-scatter.23.cloned.1.call-update) | async-done | bytes 720912 | tf_op jit(solution)/shard_map/reduce_scatter | solution.py:33
  852.2 73.7 %reduce-scatter.17.cloned.1.call-done = bf16[512,640]{1,0:T(8,128)(2,1)} async-done(((bf16[2048,640]{1,0:T(8,128)(2,1)}), bf16[512,640]{1,0:T(8,128)(2,1)}) %reduce-scatter.17.cloned.1.call-update) | async-done | bytes 655376 | tf_op jit(solution)/shard_map/reduce_scatter | solution.py:33
  933.9 24.8 %reduce-scatter.19.cloned.1.call-done = bf16[64,2048]{1,0:T(8,128)(2,1)} async-done(((bf16[256,2048]{1,0:T(8,128)(2,1)}), bf16[64,2048]{1,0:T(8,128)(2,1)}) %reduce-scatter.19.cloned.1.call-update) | async-done | bytes 262160 | tf_op jit(solution)/shard_map/reduce_scatter | solution.py:33
  993.7 38.6 %reduce-scatter.15.cloned.1.call-done = bf16[256,2048]{1,0:T(8,128)(2,1)} async-done(((bf16[2048,2048]{1,0:T(8,128)(2,1)}), bf16[256,2048]{1,0:T(8,128)(2,1)}) %reduce-scatter.15.cloned.1.call-update) | async-done | bytes 1048592 | tf_op jit(solution)/shard_map/reduce_scatter | solution.py:25
  1034.1 72.8 %reduce-scatter.11.cloned.1.call-done = bf16[256,2048]{1,0:T(8,128)(2,1)} async-done(((bf16[2048,2048]{1,0:T(8,128)(2,1)}), bf16[256,2048]{1,0:T(8,128)(2,1)}) %reduce-scatter.11.cloned.1.call-update) | async-done | bytes 1048592 | tf_op jit(solution)/shard_map/reduce_scatter | solution.py:25
  1114.3 41.3 %all-reduce = (f32[2048]{0:T(1024)}, f32[1024]{0:T(1024)}, f32[1024]{0:T(1024)}, f32[2048]{0:T(1024)}, f32[2048]{0:T(1024)}, /*index=5*/f32[3]{0:T(128)S(1)}) all-reduce(f32[2048]{0:T(1024)S(1)} %get-tuple-element.45, f32[1024]{0:T(1024)S(1)} %reshape.252, ...), channel_id=1, replica_groups=mesh['seq'=8,'wshard'=4] {'seq','wshard'}, use_global_device_ids=true, to_apply=%region_11.12 | all-reduce | flops 8195 | bytes 65560 | tf_op jit(solution)/shard_map/psum | solution.py:555
  (193 shorter events, 133.7 us)
Async XLA Ops:
  7.2 17.1 %copy-start = (bf16[512,2048]{1,0:T(8,128)(2,1)S(1)}, bf16[512,2048]{1,0:T(8,128)(2,1)}, u32[]{:S(2)}) copy-start(bf16[512,2048]{1,0:T(8,128)(2,1)} %param.26) | copy-start | bytes 6291460
  7.2 69.5 %all-gather.12.cloned.1.call-start = ((), (), s32[]{:S(2)}) async-start(), calls=%async_computation.11 | async-start | bytes 3276800 | tf_op jit(solution)/shard_map/all_gather | solution.py:29
  20.5 111.5 %all-gather.10.cloned.1.call-start = ((), (), s32[]{:S(2)}) async-start(), calls=%async_computation.10 | async-start | bytes 9437184 | tf_op jit(solution)/shard_map/all_gather | solution.py:21
  21.8 6.7 copy-start.22
  24.2 138.3 %all-gather.14.cloned.1.call-start = ((), (), s32[]{:S(2)}) async-start(), calls=%async_computation.12 | async-start | bytes 1310720 | tf_op jit(solution)/shard_map/all_gather | solution.py:29
  25.0 215.5 %reduce-scatter.9.cloned.1.call-start = ((), (), s32[]{:S(2)}) async-start(), calls=%async_computation.13 | async-start | bytes 9437184 | tf_op jit(solution)/shard_map/reduce_scatter | solution.py:25
  155.1 14.2 %copy-start.4 = (bf16[8,2,128,256]{3,2,1,0:T(8,128)(2,1)}, bf16[8,2,128,256]{3,2,1,0:T(8,128)(2,1)S(1)}, u32[]{:S(2)}) copy-start(bf16[8,2,128,256]{3,2,1,0:T(8,128)(2,1)S(1)} %pad_maximum_fusion.4) | copy-start | bytes 3145732
  169.3 180.1 %all-gather.18.cloned.1.call-start = ((), (), s32[]{:S(2)}) async-start(), calls=%async_computation.15 | async-start | bytes 7208960 | tf_op jit(solution)/shard_map/all_gather | solution.py:29
  189.3 53.0 %copy-start.12 = (f32[2048]{0:T(1024)S(1)}, f32[2048]{0:T(1024)}, u32[]{:S(2)}) copy-start(f32[2048]{0:T(1024)} %param.27) | copy-start | bytes 24580
  189.4 214.8 %all-gather.16.cloned.1.call-start = ((), (), s32[]{:S(2)}) async-start(), calls=%async_computation.14 | async-start | bytes 9437184 | tf_op jit(solution)/shard_map/all_gather | solution.py:21
  243.9 221.5 %all-gather.20.cloned.1.call-start = ((), (), s32[]{:S(2)}) async-start(), calls=%async_computation.16 | async-start | bytes 3604480 | tf_op jit(solution)/shard_map/all_gather | solution.py:29
  246.1 274.2 %all-gather.22.cloned.1.call-start = ((), (), s32[]{:S(2)}) async-start(), calls=%async_computation.18 | async-start | bytes 9437184 | tf_op jit(solution)/shard_map/all_gather | solution.py:21
  246.8 380.1 %reduce-scatter.13.cloned.1.call-start = ((), (), s32[]{:S(2)}) async-start(), calls=%async_computation.19 | async-start | bytes 9437184 | tf_op jit(solution)/shard_map/reduce_scatter | solution.py:25
  520.2 17.4 %copy-start.27 = (bf16[2048,1408]{0,1:T(8,128)(2,1)S(1)}, bf16[2048,1408]{0,1:T(8,128)(2,1)}, u32[]{:S(2)}) copy-start(bf16[2048,1408]{0,1:T(8,128)(2,1)} %all-gather.18.cloned.1.call-done) | copy-start | bytes 17301508
  555.2 74.8 %copy-start.6 = (bf16[2,128,2048]{2,1,0:T(8,128)(2,1)S(1)}, bf16[2,128,2048]{2,1,0:T(8,128)(2,1)}, u32[]{:S(2)}) copy-start(bf16[2,128,2048]{2,1,0:T(8,128)(2,1)} %param.31) | copy-start | bytes 3145732
  555.2 131.2 %all-gather.24.cloned.1.call-start = ((), (), s32[]{:S(2)}) async-start(), calls=%async_computation.20 | async-start | bytes 9437184 | tf_op jit(solution)/shard_map/all_gather | solution.py:21
  632.1 159.2 %reduce-scatter.21.cloned.1.call-start = ((), (), s32[]{:S(2)}) async-start(), calls=%async_computation.24 | async-start | bytes 7208960 | tf_op jit(solution)/shard_map/reduce_scatter | solution.py:33
  652.4 197.8 %reduce-scatter.23.cloned.1.call-start = ((), (), s32[]{:S(2)}) async-start(), calls=%async_computation.25 | async-start | bytes 3604480 | tf_op jit(solution)/shard_map/reduce_scatter | solution.py:33
  663.1 23.4 %copy-start.9 = (bf16[256,2048]{1,0:T(8,128)(2,1)S(1)}, bf16[256,2048]{1,0:T(8,128)(2,1)}, u32[]{:S(2)}) copy-start(bf16[256,2048]{1,0:T(8,128)(2,1)} %all-gather.14.cloned.1.call-done) | copy-start | bytes 3145732
  663.1 262.8 %reduce-scatter.17.cloned.1.call-start = ((), (), s32[]{:S(2)}) async-start(), calls=%async_computation.22 | async-start | bytes 3276800 | tf_op jit(solution)/shard_map/reduce_scatter | solution.py:33
  712.4 10.3 copy-start.13
  724.4 234.2 %reduce-scatter.19.cloned.1.call-start = ((), (), s32[]{:S(2)}) async-start(), calls=%async_computation.23 | async-start | bytes 1310720 | tf_op jit(solution)/shard_map/reduce_scatter | solution.py:33
  732.4 299.8 %reduce-scatter.15.cloned.1.call-start = ((), (), s32[]{:S(2)}) async-start(), calls=%async_computation.21 | async-start | bytes 9437184 | tf_op jit(solution)/shard_map/reduce_scatter | solution.py:25
  743.9 363.0 %reduce-scatter.11.cloned.1.call-start = ((), (), s32[]{:S(2)}) async-start(), calls=%async_computation.17 | async-start | bytes 9437184 | tf_op jit(solution)/shard_map/reduce_scatter | solution.py:25
  755.2 176.2 %copy-start.20 = (f32[2,128]{1,0:T(2,128)S(1)}, f32[2,128]{1,0:T(2,128)}, u32[]{:S(2)}) copy-start(f32[2,128]{1,0:T(2,128)} %copy-done.19) | copy-start | bytes 3076
  791.4 60.8 %all-to-all-start.1 = ((bf16[8,64,1408]{2,1,0:T(8,128)(2,1)}), bf16[8,64,1408]{2,1,0:T(8,128)(2,1)S(1)}, u32[]{:S(2)}, u32[]{:S(2)}) async-start(bf16[8,64,1408]{2,1,0:T(8,128)(2,1)} %bitcast.171), calls=%async_computation.8 | async-start | bytes 2883584 | tf_op jit(solution)/shard_map/all_to_all | solution.py:510
  850.3 81.2 %collective-permute-start.1 = (bf16[176,2048]{1,0:T(8,128)(2,1)}, bf16[176,2048]{1,0:T(8,128)(2,1)}, u32[]{:S(2)}, u32[]{:S(2)}) collective-permute-start(bf16[176,2048]{1,0:T(8,128)(2,1)} %reduce-scatter.23.cloned.1.call-done), channel_id=1, source_target_pairs={{0,0},{1,8},{2,16},{3,24},{4,1},{5,9},{6,17},{7,25},{8,2},{9,10},{... | collective-permute-start | bytes 2162696 | tf_op jit(solution)/shard_map/ppermute | solution.py:536
  925.9 58.9 %all-to-all-start = ((bf16[8,64,640]{2,1,0:T(8,128)(2,1)}), bf16[8,64,640]{2,1,0:T(8,128)(2,1)}, u32[]{:S(2)}, u32[]{:S(2)}) async-start(bf16[8,64,640]{2,1,0:T(8,128)(2,1)} %bitcast.177), calls=%async_computation.5 | async-start | bytes 1310720 | tf_op jit(solution)/shard_map/all_to_all | solution.py:510
  958.7 25.3 %collective-permute-start = (bf16[64,2048]{1,0:T(8,128)(2,1)}, bf16[64,2048]{1,0:T(8,128)(2,1)S(1)}, u32[]{:S(2)}, u32[]{:S(2)}) collective-permute-start(bf16[64,2048]{1,0:T(8,128)(2,1)} %reduce-scatter.19.cloned.1.call-done), channel_id=1, source_target_pairs={{0,0},{1,8},{2,16},{3,24},{4,1},{5,9},{6,17},{7,25},{8,2},{9,10},{... | collective-permute-start | bytes 786440 | tf_op jit(solution)/shard_map/ppermute | solution.py:536
  991.4 40.8 %copy-start.15 = (f32[2048]{0:T(1024)S(1)}, f32[2048]{0:T(1024)}, u32[]{:S(2)}) copy-start(f32[2048]{0:T(1024)} %param.19) | copy-start | bytes 24580
  991.4 40.8 %copy-start.18 = (f32[256]{0:T(256)S(1)}, f32[256]{0:T(256)}, u32[]{:S(2)}) copy-start(f32[256]{0:T(256)} %copy-done.17) | copy-start | bytes 3076
  1034.1 122.0 %copy-start.1 = (bf16[512,2048]{1,0:T(8,128)(2,1)S(1)}, bf16[512,2048]{1,0:T(8,128)(2,1)}, u32[]{:S(2)}) copy-start(bf16[512,2048]{1,0:T(8,128)(2,1)} %param.26) | copy-start | bytes 6291460
  (19 other events, 66.0 us)
Sparse Core Ops, SparseCore 0:
  20.6 55.9 all-gather.11
  79.1 52.8 all-gather.9
  134.1 28.2 all-gather.13
  169.5 70.9 reduce-scatter.8
  242.6 106.7 all-gather.17
  351.9 52.2 all-gather.15
  405.8 59.5 all-gather.19
  467.5 52.7 all-gather.21
  555.3 71.5 reduce-scatter.12
  632.2 54.1 all-gather.23
  688.7 102.5 reduce-scatter.20
  793.5 56.7 reduce-scatter.22
  852.6 73.2 reduce-scatter.16
  928.6 30.0 reduce-scatter.18
  962.4 69.8 reduce-scatter.14
  1035.5 71.2 reduce-scatter.10

commit v2 on v1

v2 whole, which is shorter than its diff:
```python
import functools

import jax
import jax.numpy as jnp
from jax import lax
from jax.experimental import pallas as pl
from jax.experimental.pallas import tpu as pltpu
from jax.sharding import PartitionSpec as P

LAYERS = 24
EPS = 1e-06
BF = jnp.bfloat16
F32 = jnp.float32


def dot(left, right, form):
    return jnp.einsum(form, left, right, preferred_element_type=F32)


def swap(value, bit):
    size = lax.axis_size("seq")
    return lax.ppermute(value, "seq", [(i, i ^ bit) for i in range(size)])


def chip_bits():
    size = lax.axis_size("seq")
    return [1 << i for i in range(1, size.bit_length() - 1)]


def gather_even(own):
    bits = chip_bits()
    if len(bits) == 2:
        first, second = bits
        half = own.shape[0] // 2
        from_first = swap(own, first)
        from_second = swap(own, second)
        top = swap(from_first[:half], second)
        low = swap(from_second[half:], first)
        return jnp.concatenate([own, from_first, from_second, top, low], axis=0)
    held = own
    for bit in bits:
        held = jnp.concatenate([held, swap(held, bit)], axis=0)
    return held


def gather_seq(own):
    even = gather_even(own)
    return even, swap(even, 1)


def scatter_seq(even, odd):
    bits = chip_bits()
    joint = even.astype(F32) + swap(odd, 1).astype(F32)
    if len(bits) == 2:
        first, second = bits
        rows = joint.shape[0] // 4
        half = rows // 2
        low_joint = joint.astype(BF)
        near_first, near_second, far = (
            low_joint[rows : 2 * rows],
            low_joint[2 * rows : 3 * rows],
            low_joint[3 * rows :],
        )
        far_top = swap(far[:half], first)
        far_low = swap(far[half:], second)
        first_top = swap(near_first[:half], first)
        second_low = swap(near_second[half:], second)
        first_low = swap((near_first[half:].astype(F32) + far_low.astype(F32)).astype(BF), first)
        second_top = swap(
            (near_second[:half].astype(F32) + far_top.astype(F32)).astype(BF), second
        )
        first_all = jnp.concatenate([first_top, first_low], axis=0).astype(F32)
        second_all = jnp.concatenate([second_top, second_low], axis=0).astype(F32)
        return joint[:rows] + first_all + second_all
    for bit in reversed(bits):
        half = joint.shape[0] // 2
        joint = joint[:half] + swap(joint[half:].astype(BF), bit).astype(F32)
    return joint


def gather_small(own):
    held = own
    for bit in chip_bits() + [1]:
        held = jnp.concatenate([held, swap(held, bit)], axis=0)
    return held


def scatter_small(blocks):
    for bit in [1] + list(reversed(chip_bits())):
        half = blocks.shape[0] // 2
        blocks = blocks[:half] + swap(blocks[half:], bit)
    return blocks


def sum_all(value):
    for bit in [1] + chip_bits():
        value = value + swap(value, bit)
    planes = lax.axis_size("wshard")
    bit = 1
    while bit < planes:
        value = value + lax.ppermute(value, "wshard", [(i, i ^ bit) for i in range(planes)])
        bit *= 2
    return value


def gather_shard(value):
    return lax.all_gather(value, "wshard", axis=0, tiled=True)


def scatter_shard(value):
    return lax.psum_scatter(value, "wshard", scatter_dimension=0, tiled=True)


def slot_of(place, group, groups):
    key = place ^ group
    return (key >> 1) + (key & 1) * (groups // 2)


def group_of(place, half, index):
    return place ^ ((index << 1) | half)


def token_rows(slot, tokens):
    return pl.ds(pl.multiple_of(slot * tokens, tokens), tokens)


def keep_of(pre, flag, bias, floor, chan):
    logit = (pre[:, 2 * chan : 3 * chan] + bias).astype(BF).astype(F32)
    sig = jax.nn.sigmoid(logit)
    return (floor + (1.0 - floor) * sig) * (1.0 - flag), sig


def forward_kernel(
    place_ref,
    floor_ref,
    pre_even,
    pre_odd,
    flag_ref,
    bias_ref,
    theta_ref,
    gain_ref,
    state_ref,
    gated_even,
    gated_odd,
    square_ref,
    keep_s,
    val_re,
    val_im,
    prod_re,
    prod_im,
    carry_re,
    carry_im,
):
    groups, _, tokens, _ = flag_ref.shape
    chan = keep_s.shape[1]
    half_groups = groups // 2
    floor = floor_ref[0]
    place = place_ref[0]
    cosine = jnp.cos(theta_ref[...])
    sine = jnp.sin(theta_ref[...])

    for half, pre_ref in ((0, pre_even), (1, pre_odd)):

        @pl.loop(0, half_groups)
        def _(index, half=half, pre_ref=pre_ref):
            slot = index + half * half_groups
            rows = token_rows(slot, tokens)
            pre = pre_ref[index, 0]
            keep, _ = keep_of(pre, flag_ref[slot, 0], bias_ref[...], floor, chan)
            keep_s[rows, :] = keep
            fresh = 1.0 - keep
            value = pre[:, :chan]
            val_re[rows, :] = fresh * (value * jax.nn.sigmoid(value)).astype(BF).astype(F32)
            value = pre[:, chan : 2 * chan]
            val_im[rows, :] = fresh * (value * jax.nn.sigmoid(value)).astype(BF).astype(F32)

    def step(t, carry):
        h_re, h_im, p_re, p_im = carry
        rows = pl.ds(t, groups, stride=tokens)
        held = keep_s[rows, :]
        a_re = held * cosine
        a_im = held * sine
        n_re = a_re * h_re - a_im * h_im + val_re[rows, :]
        n_im = a_re * h_im + a_im * h_re + val_im[rows, :]
        q_re = a_re * p_re - a_im * p_im
        q_im = a_re * p_im + a_im * p_re
        val_re[rows, :] = n_re
        val_im[rows, :] = n_im
        prod_re[rows, :] = q_re
        prod_im[rows, :] = q_im
        return n_re, n_im, q_re, q_im

    zero = jnp.zeros((groups, chan), F32)
    lax.fori_loop(0, tokens, step, (zero, zero, zero + 1.0, zero), unroll=8)

    def link(group, carry):
        c_re, c_im = carry
        slot = slot_of(place, group, groups)
        carry_re[pl.ds(slot, 1), :] = c_re
        carry_im[pl.ds(slot, 1), :] = c_im
        last = pl.ds(slot * tokens + tokens - 1, 1)
        p_re = prod_re[last, :]
        p_im = prod_im[last, :]
        return (
            p_re * c_re - p_im * c_im + val_re[last, :],
            p_re * c_im + p_im * c_re + val_im[last, :],
        )

    nought = jnp.zeros((1, chan), F32)
    lax.fori_loop(0, groups, link, (nought, nought))

    for half, pre_ref, gated_ref in ((0, pre_even, gated_even), (1, pre_odd, gated_odd)):

        @pl.loop(0, half_groups)
        def _(index, half=half, pre_ref=pre_ref, gated_ref=gated_ref):
            slot = index + half * half_groups
            rows = token_rows(slot, tokens)
            c_re = carry_re[pl.ds(slot, 1), :]
            c_im = carry_im[pl.ds(slot, 1), :]
            p_re = prod_re[rows, :]
            p_im = prod_im[rows, :]
            h_re = val_re[rows, :] + p_re * c_re - p_im * c_im
            h_im = val_im[rows, :] + p_re * c_im + p_im * c_re
            state_ref[slot, 0, :, :chan] = h_re
            state_ref[slot, 0, :, chan:] = h_im
            m_re = h_re.astype(BF).astype(F32)
            m_im = h_im.astype(BF).astype(F32)
            gate = jax.nn.sigmoid(pre_ref[index, 0, :, 3 * chan :]) * gain_ref[...]
            gated_ref[index, 0, :, :chan] = (m_re * gate[:, :chan]).astype(BF)
            gated_ref[index, 0, :, chan:] = (m_im * gate[:, chan:]).astype(BF)
            square_ref[slot, 0] = jnp.sum(m_re * m_re + m_im * m_im, axis=1, keepdims=True)


def backward_kernel(
    place_ref,
    floor_ref,
    pre_even,
    pre_odd,
    flag_ref,
    bias_ref,
    theta_ref,
    gain_ref,
    state_ref,
    up_even,
    up_odd,
    scale_ref,
    term_ref,
    out_even,
    out_odd,
    sum_bias,
    sum_theta,
    sum_gain,
    keep_s,
    adj_re,
    adj_im,
    prod_re,
    prod_im,
    carry_re,
    carry_im,
    next_s,
):
    groups, _, tokens, _ = flag_ref.shape
    chan = keep_s.shape[1]
    half_groups = groups // 2
    floor = floor_ref[0]
    place = place_ref[0]
    cosine = jnp.cos(theta_ref[...])
    sine = jnp.sin(theta_ref[...])

    @pl.when(pl.program_id(0) == 0)
    def _():
        sum_bias[...] = jnp.zeros_like(sum_bias)
        sum_theta[...] = jnp.zeros_like(sum_theta)
        sum_gain[...] = jnp.zeros_like(sum_gain)

    for half, pre_ref, up_ref, out_ref in (
        (0, pre_even, up_even, out_even),
        (1, pre_odd, up_odd, out_odd),
    ):

        @pl.loop(0, half_groups)
        def _(index, half=half, pre_ref=pre_ref, up_ref=up_ref, out_ref=out_ref):
            slot = index + half * half_groups
            rows = token_rows(slot, tokens)
            pre = pre_ref[index, 0]
            keep, _ = keep_of(pre, flag_ref[slot, 0], bias_ref[...], floor, chan)
            keep_s[rows, :] = keep
            scale = scale_ref[slot, 0]
            mixed = state_ref[slot, 0].astype(BF).astype(F32)
            sig = jax.nn.sigmoid(pre[:, 3 * chan :])
            inner = up_ref[index, 0] * sig
            normed = inner * mixed * scale
            sum_gain[...] += jnp.sum(normed, axis=0, keepdims=True)
            out_ref[index, 0, :, 3 * chan :] = (normed * gain_ref[...] * (1.0 - sig)).astype(BF)
            grad = (scale * (inner * gain_ref[...]) - mixed * term_ref[slot, 0]).astype(BF)
            adj_re[rows, :] = grad[:, :chan].astype(F32)
            adj_im[rows, :] = grad[:, chan:].astype(F32)

    @pl.loop(0, groups)
    def _(group):
        slot = slot_of(place, group, groups)
        after = slot_of(place, lax.min(group + 1, groups - 1), groups)
        row = keep_s[pl.ds(after * tokens, 1), :]
        next_s[pl.ds(slot, 1), :] = jnp.where(group == groups - 1, 0.0, row)

    def turn(t, held, carry):
        g_re, g_im, p_re, p_im = carry
        rows = pl.ds(t, groups, stride=tokens)
        a_re = held * cosine
        a_im = held * sine
        n_re = a_re * g_re + a_im * g_im + adj_re[rows, :]
        n_im = a_re * g_im - a_im * g_re + adj_im[rows, :]
        q_re = a_re * p_re + a_im * p_im
        q_im = a_re * p_im - a_im * p_re
        adj_re[rows, :] = n_re
        adj_im[rows, :] = n_im
        prod_re[rows, :] = q_re
        prod_im[rows, :] = q_im
        return n_re, n_im, q_re, q_im

    def step(index, carry):
        t = tokens - 2 - index
        return turn(t, keep_s[pl.ds(t + 1, groups, stride=tokens), :], carry)

    zero = jnp.zeros((groups, chan), F32)
    carry = turn(tokens - 1, next_s[...], (zero, zero, zero + 1.0, zero))
    lax.fori_loop(0, tokens - 1, step, carry, unroll=4)

    def link(index, carry):
        c_re, c_im = carry
        slot = slot_of(place, groups - 1 - index, groups)
        carry_re[pl.ds(slot, 1), :] = c_re
        carry_im[pl.ds(slot, 1), :] = c_im
        first = pl.ds(slot * tokens, 1)
        p_re = prod_re[first, :]
        p_im = prod_im[first, :]
        return (
            p_re * c_re - p_im * c_im + adj_re[first, :],
            p_re * c_im + p_im * c_re + adj_im[first, :],
        )

    nought = jnp.zeros((1, chan), F32)
    lax.fori_loop(0, groups, link, (nought, nought))
    head = lax.broadcasted_iota(jnp.int32, (tokens, 2 * chan), 0) == 0

    for half, pre_ref, out_ref in ((0, pre_even, out_even), (1, pre_odd, out_odd)):

        @pl.loop(0, half_groups)
        def _(index, half=half, pre_ref=pre_ref, out_ref=out_ref):
            slot = index + half * half_groups
            rows = token_rows(slot, tokens)
            group = group_of(place, half, index)
            before = slot_of(place, lax.max(group - 1, 0), groups)
            tail = jnp.where(group == 0, 0.0, state_ref[before, 0, tokens - 1 :, :])
            prev = jnp.where(head, tail, pltpu.roll(state_ref[slot, 0], 1, 0))
            prev_re = prev[:, :chan]
            prev_im = prev[:, chan:]
            c_re = carry_re[pl.ds(slot, 1), :]
            c_im = carry_im[pl.ds(slot, 1), :]
            p_re = prod_re[rows, :]
            p_im = prod_im[rows, :]
            g_re = adj_re[rows, :] + p_re * c_re - p_im * c_im
            g_im = adj_im[rows, :] + p_re * c_im + p_im * c_re
            turn_re = cosine * prev_re - sine * prev_im
            turn_im = sine * prev_re + cosine * prev_im
            flag = flag_ref[slot, 0]
            pre = pre_ref[index, 0]
            keep, sig = keep_of(pre, flag, bias_ref[...], floor, chan)
            fresh = 1.0 - keep
            x_re = pre[:, :chan]
            x_im = pre[:, chan : 2 * chan]
            s_re = jax.nn.sigmoid(x_re)
            s_im = jax.nn.sigmoid(x_im)
            cand_re = (x_re * s_re).astype(BF).astype(F32)
            cand_im = (x_im * s_im).astype(BF).astype(F32)
            grad_keep = g_re * (turn_re - cand_re) + g_im * (turn_im - cand_im)
            sum_theta[...] -= jnp.sum(
                keep * (g_re * turn_im - g_im * turn_re), axis=0, keepdims=True
            )
            grad_forget = (
                grad_keep * (1.0 - flag) * ((1.0 - floor) * (sig * (1.0 - sig)))
            ).astype(BF)
            sum_bias[...] += jnp.sum(grad_forget.astype(F32), axis=0, keepdims=True)
            out_ref[index, 0, :, 2 * chan : 3 * chan] = grad_forget
            cand_grad = (fresh * g_re).astype(BF).astype(F32)
            out_ref[index, 0, :, :chan] = (
                cand_grad * s_re * (1.0 + x_re * (1.0 - s_re))
            ).astype(BF)
            cand_grad = (fresh * g_im).astype(BF).astype(F32)
            out_ref[index, 0, :, chan : 2 * chan] = (
                cand_grad * s_im * (1.0 + x_im * (1.0 - s_im))
            ).astype(BF)


def block_spec(groups, tokens, width):
    mode = pl.Buffered(1) if groups > 4 and width % 128 and width > 1 else None
    return pl.BlockSpec((groups, 1, tokens, width), lambda b: (0, b, 0, 0), pipeline_mode=mode)


def row_spec(width):
    return pl.BlockSpec((1, width), lambda b: (0, 0))


def recur_forward(place, floor, pre_even, pre_odd, flags, bias, theta, gain):
    groups, seqs, tokens, _ = flags.shape
    chan = bias.shape[1]
    half = groups // 2
    scalar = pl.BlockSpec(memory_space=pltpu.SMEM)
    rows = groups * tokens
    pre_spec = block_spec(half, tokens, 5 * chan)
    one = block_spec(groups, tokens, 1)
    gated = block_spec(half, tokens, 2 * chan)
    gated_shape = jax.ShapeDtypeStruct((half, seqs, tokens, 2 * chan), BF)
    size = seqs * rows * chan
    return pl.pallas_call(
        forward_kernel,
        grid=(seqs,),
        in_specs=[
            scalar,
            scalar,
            pre_spec,
            pre_spec,
            one,
            row_spec(chan),
            row_spec(chan),
            row_spec(2 * chan),
        ],
        out_specs=[block_spec(groups, tokens, 2 * chan), gated, gated, one],
        out_shape=[
            jax.ShapeDtypeStruct((groups, seqs, tokens, 2 * chan), F32),
            gated_shape,
            gated_shape,
            jax.ShapeDtypeStruct((groups, seqs, tokens, 1), F32),
        ],
        scratch_shapes=[pltpu.VMEM((rows, chan), F32)] * 5
        + [pltpu.VMEM((groups, chan), F32)] * 2,
        compiler_params=pltpu.CompilerParams(vmem_limit_bytes=56 * 2**20),
        cost_estimate=pl.CostEstimate(
            flops=60 * size, bytes_accessed=32 * size, transcendentals=5 * size
        ),
        name="recur_forward",
    )(place, floor, pre_even, pre_odd, flags, bias, theta, gain)


def recur_backward(
    place, floor, pre_even, pre_odd, flags, bias, theta, gain, state, up_even, up_odd, scale, term
):
    groups, seqs, tokens, _ = flags.shape
    chan = bias.shape[1]
    half = groups // 2
    scalar = pl.BlockSpec(memory_space=pltpu.SMEM)
    rows = groups * tokens
    pre_spec = block_spec(half, tokens, 5 * chan)
    one = block_spec(groups, tokens, 1)
    up_spec = block_spec(half, tokens, 2 * chan)
    out_shape = jax.ShapeDtypeStruct((half, seqs, tokens, 5 * chan), BF)
    size = seqs * rows * chan
    return pl.pallas_call(
        backward_kernel,
        grid=(seqs,),
        in_specs=[
            scalar,
            scalar,
            pre_spec,
            pre_spec,
            one,
            row_spec(chan),
            row_spec(chan),
            row_spec(2 * chan),
            block_spec(groups, tokens, 2 * chan),
            up_spec,
            up_spec,
            one,
            one,
        ],
        out_specs=[pre_spec, pre_spec, row_spec(chan), row_spec(chan), row_spec(2 * chan)],
        out_shape=[
            out_shape,
            out_shape,
            jax.ShapeDtypeStruct((1, chan), F32),
            jax.ShapeDtypeStruct((1, chan), F32),
            jax.ShapeDtypeStruct((1, 2 * chan), F32),
        ],
        scratch_shapes=[pltpu.VMEM((rows, chan), F32)] * 5
        + [pltpu.VMEM((groups, chan), F32)] * 3,
        compiler_params=pltpu.CompilerParams(vmem_limit_bytes=56 * 2**20),
        cost_estimate=pl.CostEstimate(
            flops=100 * size, bytes_accessed=50 * size, transcendentals=8 * size
        ),
        name="recur_backward",
    )(
        place, floor, pre_even, pre_odd, flags, bias, theta, gain, state, up_even, up_odd, scale, term
    )


def body(
    tokens,
    starts,
    layer_index,
    gain_mix,
    w_in,
    w_forget,
    bias_forget,
    theta,
    w_gate_out,
    gain_out,
    w_out,
    gain_ffn,
    w_ffgate,
    w_ffup,
    w_down,
    out_grad,
):
    seqs, seq_dev, width = tokens.shape
    rows = seqs * seq_dev
    groups = lax.axis_size("seq")
    planes = lax.axis_size("wshard")
    half = groups // 2
    devices = groups * planes
    place = lax.axis_index("seq")
    floor = layer_index.astype(F32) / LAYERS
    mix_run = w_out.shape[0] // groups
    ffn_run = w_down.shape[0] // groups
    chan = mix_run * planes // 2
    hidden = ffn_run * planes

    def own_columns(array, run):
        count = array.shape[1] // (run * groups)
        column = lax.broadcasted_iota(jnp.int32, (array.shape[1], count * run), 0)
        index = lax.broadcasted_iota(jnp.int32, (array.shape[1], count * run), 1)
        block = index // run
        chosen = column == block * (run * groups) + place * run + (index - block * run)
        return dot(array, chosen.astype(BF), "rc,cj->rj").astype(BF)

    def own_parts(vector):
        count = vector.shape[0] // (mix_run * groups)
        split = vector.reshape(count, groups, mix_run)
        return lax.dynamic_slice_in_dim(split, place, 1, 1).reshape(1, count * mix_run)

    def own_rows(array):
        run = array.shape[0] // groups
        return lax.dynamic_slice_in_dim(array, place * run, run, 0)

    resid_in = tokens.reshape(rows, width).astype(F32)
    scale_in = lax.rsqrt(jnp.mean(resid_in * resid_in, axis=1, keepdims=True) + EPS)
    normed_own = (resid_in * scale_in * gain_mix).astype(BF)
    normed_even, normed_odd = gather_seq(normed_own)
    upstream_own = out_grad.reshape(rows, width)

    rec_w = gather_shard(
        jnp.concatenate(
            [
                own_columns(w_in, mix_run),
                own_columns(w_forget, mix_run),
                own_columns(w_gate_out, mix_run),
            ],
            axis=1,
        )
    )
    out_w = gather_shard(own_rows(w_out))
    ff_w = gather_shard(
        jnp.concatenate([own_columns(w_ffgate, ffn_run), own_columns(w_ffup, ffn_run)], axis=1)
    )
    down_w = gather_shard(own_rows(w_down))

    slots = lax.broadcasted_iota(jnp.int32, (groups, groups), 0)
    sources = lax.broadcasted_iota(jnp.int32, (groups, groups), 1)
    keys = jnp.where(slots < half, 2 * slots, 2 * (slots - half) + 1)
    chosen = ((place ^ keys) == sources).astype(F32)
    marks = starts.astype(F32).reshape(seqs, groups, seq_dev).transpose(1, 0, 2)
    flags = jnp.sum(chosen[:, :, None, None] * marks[None], axis=1)[..., None]
    bias_own = own_parts(bias_forget)
    theta_own = own_parts(theta)
    gain_own = own_parts(gain_out)
    place_one = place.reshape(1)

    def blocks(array):
        return array.reshape(half, seqs, seq_dev, -1)

    pre_even = blocks(dot(normed_even, rec_w, "td,dc->tc"))
    pre_odd = blocks(dot(normed_odd, rec_w, "td,dc->tc"))
    state, gated_even, gated_odd, square = recur_forward(
        place_one, floor, pre_even, pre_odd, flags, bias_own, theta_own, gain_own
    )
    gated_even = gated_even.reshape(half * rows, 2 * chan)
    gated_odd = gated_odd.reshape(half * rows, 2 * chan)

    def mix(gated):
        return dot(gated, out_w, "tc,cd->td").astype(BF)

    square_own = scatter_small(square.reshape(groups, rows))
    scale_own = lax.rsqrt(square_own / width + EPS)
    scale_out = scale_own.reshape(rows, 1)
    branch_mix = scale_out * scatter_seq(mix(gated_even), mix(gated_odd))
    resid = resid_in + branch_mix
    scale_ffn = lax.rsqrt(jnp.mean(resid * resid, axis=1, keepdims=True) + EPS)
    ffn_even, ffn_odd = gather_seq((resid * scale_ffn * gain_ffn).astype(BF))
    scale_all = gather_small(scale_own)
    up_even, up_odd = gather_seq(upstream_own)

    def ffn(normed, upstream):
        ff = dot(normed, ff_w, "td,df->tf")
        ffn_gate, ffn_up = ff[:, :hidden], ff[:, hidden:]
        sig_ffn = jax.nn.sigmoid(ffn_gate)
        silu_ffn = ffn_gate * sig_ffn
        ffn_hidden = (silu_ffn * ffn_up).astype(BF)
        grad_hidden = dot(upstream, down_w, "td,fd->tf")
        grad_gate = grad_hidden * ffn_up * sig_ffn * (1.0 + ffn_gate * (1.0 - sig_ffn))
        grad_up = grad_hidden * silu_ffn
        grad_ff = jnp.concatenate([grad_gate.astype(BF), grad_up.astype(BF)], axis=1)
        return ffn_hidden, grad_ff

    hidden_odd, grad_ff_odd = ffn(ffn_odd, up_odd)
    hidden_even, grad_ff_even = ffn(ffn_even, up_even)
    grad_normed_ffn = scatter_seq(
        dot(grad_ff_even, ff_w, "tf,df->td").astype(BF),
        dot(grad_ff_odd, ff_w, "tf,df->td").astype(BF),
    )
    branch_ffn = scatter_seq(
        dot(hidden_even, down_w, "tf,fd->td").astype(BF),
        dot(hidden_odd, down_w, "tf,fd->td").astype(BF),
    )
    result = (resid + branch_ffn).astype(BF)

    scaled_ffn = grad_normed_ffn * gain_ffn
    grad_resid = (
        upstream_own.astype(F32)
        + scale_ffn * scaled_ffn
        - resid * scale_ffn**3 * jnp.mean(scaled_ffn * resid, axis=1, keepdims=True)
    )
    grad_gain_ffn = jnp.sum(grad_normed_ffn * resid * scale_ffn, axis=0)
    grad_branch_own = grad_resid.astype(BF)
    overlap = jnp.sum(grad_branch_own.astype(F32) * branch_mix, axis=1)
    term_all = gather_small((scale_out[:, 0] ** 2 * overlap / width)[None])
    branch_even, branch_odd = gather_seq(grad_branch_own)
    grad_gated_even = blocks(dot(branch_even, out_w, "td,cd->tc"))
    grad_gated_odd = blocks(dot(branch_odd, out_w, "td,cd->tc"))

    shape_one = (groups, seqs, seq_dev, 1)
    grad_even, grad_odd, sum_bias, sum_theta, sum_gain = recur_backward(
        place_one,
        floor,
        pre_even,
        pre_odd,
        flags,
        bias_own,
        theta_own,
        gain_own,
        state,
        grad_gated_even,
        grad_gated_odd,
        scale_all.reshape(shape_one),
        term_all.reshape(shape_one),
    )
    grad_even = grad_even.reshape(half * rows, 5 * chan)
    grad_odd = grad_odd.reshape(half * rows, 5 * chan)
    grad_normed_in = scatter_seq(
        dot(grad_even, rec_w, "tc,dc->td").astype(BF),
        dot(grad_odd, rec_w, "tc,dc->td").astype(BF),
    )
    scaled_in = grad_normed_in * gain_mix
    grad_tokens = (
        grad_resid
        + scale_in * scaled_in
        - resid_in * scale_in**3 * jnp.mean(scaled_in * resid_in, axis=1, keepdims=True)
    ).astype(BF)
    grad_gain_mix = jnp.sum(grad_normed_in * resid_in * scale_in, axis=0)

    def pair_dot(left, right, form):
        return dot(left[0], right[0], form) + dot(left[1], right[1], form)

    def to_owner(grad):
        run = grad.shape[0] // devices
        part = grad.astype(BF).reshape(groups, planes, run, -1).transpose(1, 0, 2, 3)
        part = scatter_shard(part.reshape(grad.shape)).reshape(groups, run, -1)
        return lax.all_to_all(part, "seq", split_axis=0, concat_axis=0, tiled=True)

    def columns(part, run):
        source, count, cols = part.shape
        split = part.reshape(source, count, cols // run, run)
        return split.transpose(1, 2, 0, 3).reshape(count, -1).astype(F32)

    scaled_even = (gated_even.astype(F32) * scale_all[:half].reshape(-1, 1)).astype(BF)
    scaled_odd = (gated_odd.astype(F32) * scale_all[half:].reshape(-1, 1)).astype(BF)
    ff_grad = to_owner(
        pair_dot((ffn_even, ffn_odd), (grad_ff_even, grad_ff_odd), "td,tf->df")
    )
    grad_w_ffgate = columns(ff_grad[..., :hidden], ffn_run)
    grad_w_ffup = columns(ff_grad[..., hidden:], ffn_run)
    rec_grad = to_owner(pair_dot((normed_even, normed_odd), (grad_even, grad_odd), "td,tc->dc"))
    grad_w_in = columns(rec_grad[..., : 2 * chan], mix_run)
    grad_w_forget = columns(rec_grad[..., 2 * chan : 3 * chan], mix_run)
    grad_w_gate = columns(rec_grad[..., 3 * chan :], mix_run)

    pairs = [
        (s * planes + w, w * groups + s) for s in range(groups) for w in range(planes)
    ]

    def rows_to_owner(grad):
        part = scatter_shard(grad.astype(BF))
        return lax.ppermute(part, ("seq", "wshard"), pairs).astype(F32)

    grad_w_down = rows_to_owner(
        pair_dot((hidden_even, hidden_odd), (up_even, up_odd), "tf,td->fd")
    )
    grad_w_out = rows_to_owner(
        pair_dot((scaled_even, scaled_odd), (branch_even, branch_odd), "tc,td->cd")
    )

    def spread(part):
        count = part.shape[1] // mix_run
        zero = jnp.zeros((count, groups, mix_run), F32)
        zero = lax.dynamic_update_slice(zero, part.reshape(count, 1, mix_run), (0, place, 0))
        return zero.reshape(-1)

    pieces = [
        spread(sum_bias),
        spread(sum_theta),
        spread(sum_gain),
        grad_gain_ffn,
        grad_gain_mix,
        jnp.stack(
            [
                jnp.sum(resid_in * resid_in),
                jnp.sum(branch_mix * branch_mix),
                jnp.sum(branch_ffn * branch_ffn),
            ]
        ),
    ]
    sums = sum_all(jnp.concatenate(pieces))
    cuts = []
    offset = 0
    for piece in pieces:
        cuts.append(sums[offset : offset + piece.shape[0]])
        offset += piece.shape[0]
    grad_bias, grad_theta, grad_gain_out, grad_gain_ffn, grad_gain_mix, squares = cuts
    rms_values = jnp.sqrt(squares / (rows * width * devices))
    return (
        result.reshape(seqs, seq_dev, width),
        grad_tokens.reshape(seqs, seq_dev, width),
        grad_gain_mix,
        grad_w_in,
        grad_w_forget,
        grad_bias,
        grad_theta,
        grad_w_gate,
        grad_gain_out,
        grad_w_out,
        grad_gain_ffn,
        grad_w_ffgate,
        grad_w_ffup,
        grad_w_down,
        rms_values,
    )


def solution(mesh):
    whole = P()
    rowed = P("wshard", None)
    stream = P("wshard", "seq", None)
    owned = P(("seq", "wshard"), None)
    return jax.shard_map(
        body,
        mesh=mesh,
        in_specs=(
            stream,
            rowed,
            whole,
            whole,
            rowed,
            rowed,
            whole,
            whole,
            rowed,
            whole,
            rowed,
            whole,
            rowed,
            rowed,
            rowed,
            stream,
        ),
        out_specs=(
            stream,
            stream,
            whole,
            owned,
            owned,
            whole,
            whole,
            owned,
            whole,
            owned,
            whole,
            owned,
            owned,
            owned,
            whole,
        ),
        check_vma=False,
    )
```

time: 1170 us -> 718 us (0.61)
  waiting for transfers between devices: 785 us -> 268 us
  blocking collectives: 62.9 us -> 0 us
  starting transfers between devices: 15.1 us -> 73.1 us
  matrix products: 145 us -> 185 us
  local copies, waits for them, and re-layouts: 78.2 us -> 94 us
    ppermute x0 -> x62, waiting for transfers between devices: none -> 220 us  [the longest x60 217 us: swap(): return lax.ppermute(value, 'seq', [(i, i ^ bit) for i in range(size)])]
    reduce_scatter x4 -> x0, waiting for transfers between devices: 218 us -> none  [scatter_seq(): return lax.psum_scatter(value, 'seq', scatter_dimension=0, tiled=True)]
    reduce_scatter x4, waiting for transfers between devices: 189 us -> 0.01 us  [scatter_shard(): return lax.psum_scatter(value, 'wshard', scatter_dimension=0, tiled=True)]
    all_gather x4 -> x0, waiting for transfers between devices: 177 us -> none  [gather_seq(): return lax.all_gather(value, 'seq', axis=0, tiled=True)]
    all_gather x4, waiting for transfers between devices: 200 us -> 34.2 us  [gather_shard(): return lax.all_gather(value, 'wshard', axis=0, tiled=True)]
    ppermute x0 -> x62, starting transfers between devices: none -> 57.9 us  [the longest x60 55.2 us: swap(): return lax.ppermute(value, 'seq', [(i, i ^ bit) for i in range(size)])]
    psum x2 -> x0, blocking collectives: 54.9 us -> none  [the longest x1 41.3 us: body(): lax.psum((grad_gain_mix, spread(sum_bias, half), spread(sum_theta, half),...]
    dot_general x12 -> x29, matrix products: 145 us -> 185 us  [dot(): return jnp.einsum(form, left, right, preferred_element_type=F32)]
  transfers between devices with their start and end apart: 20 -> 74, of which waited for: 16 -> 32; matrix products, arithmetic and copies ran while one was open for 16% -> 40% of each run, Pallas kernels for 2% -> 4%
where the time goes in v2:
time: 718 us; the launch traced here: 711 us
  waiting for transfers between devices  268 us (37%)
  matrix products  185 us (26%)
  local copies, waits for them, and re-layouts  94 us (13%)
  starting transfers between devices  73.1 us (10%)
  other arithmetic  46.2 us (6%)
  Pallas kernels  28.3 us (4%)
  between operations  16.2 us (2%)
    ppermute x60, waiting for transfers between devices, swap(): return lax.ppermute(value, 'seq', [(i, i ^ bit) for i in range(size)])  217 us
    dot_general x29, matrix products, dot(): return jnp.einsum(form, left, right, preferred_element_type=F32)  185 us
    ppermute x60, starting transfers between devices, swap(): return lax.ppermute(value, 'seq', [(i, i ^ bit) for i in range(size)])  55.2 us
    all_gather x4, waiting for transfers between devices, gather_shard(): return lax.all_gather(value, 'wshard', axis=0, tiled=True)  34.2 us
    convert_element_type x15, local copies, waits for them, and re-layouts, columns(): return split.transpose(1, 2, 0, 3).reshape(count, -1).astype(F32)  27.2 us
    unnamed x102, local copies, waits for them, and re-layouts  23.4 us
    pallas_call x1, Pallas kernels, recur_backward(): pl.pallas_call(backward_kernel, grid=(seqs,), in_specs=[scalar, scalar, p...  15.9 us
  transfers between devices with their start and end apart: 74, of which 32 were waited for; matrix products, arithmetic and copies ran while one was open for 40% of the time, Pallas kernels for 4%

profile of v2, /device:TPU:4, one launch (start us, length us, event | category | flops | bytes accessed | tf_op | source)
XLA Modules:
  0.0 711.4 jit_solution(5004299906564364716)
XLA Ops:
  17.6 22.9 %collective-permute-done = bf16[256,2048]{1,0:T(8,128)(2,1)S(1)} collective-permute-done((bf16[256,2048]{1,0:T(8,128)(2,1)S(1)}, bf16[256,2048]{1,0:T(8,128)(2,1)S(1)}, u32[]{:S(2)}, u32[]{:S(2)}) %collective-permute-start) | collective-permute-done | bytes 1048608 | tf_op jit(solution)/shard_map/ppermute | solution.py:22
  44.8 8.6 %collective-permute-done.2 = bf16[128,2048]{1,0:T(8,128)(2,1)S(1)} collective-permute-done((bf16[128,2048]{1,0:T(8,128)(2,1)S(1)}, bf16[128,2048]{1,0:T(8,128)(2,1)S(1)}, u32[]{:S(2)}, u32[]{:S(2)}) %collective-permute-start.2) | collective-permute-done | bytes 524320 | tf_op jit(solution)/shard_map/ppermute | solution.py:22
  59.4 7.9 %fusion.38 = bf16[512,704]{0,1:T(8,128)(2,1)} fusion(bf16[512,5632]{1,0:T(8,128)(2,1)} %param.29, s32[]{:T(128)S(6)} %mul.289, s32[704]{0:T(1024)S(1)} %get-tuple-element.115, s32[704]{0:T(1024)S(1)} %get-tuple-element.116, pred[704]{0:T(1024)(128)(4,1)S(1)} %fusion.67), kind=kOutput, calls=%fused_computation.78 | convolution fusion | flops 4088201216 | bytes 6494404 | tf_op jit(solution)/shard_map/rc,cj->rj/dot_general | solution.py:17
  69.4 8.1 %fusion.100 = f32[1024,640]{1,0:T(8,128)} fusion(bf16[1024,2048]{1,0:T(8,128)(2,1)} %constant_dynamic-update-slice_fusion, bf16[2048,640]{0,1:T(8,128)(2,1)} %all-gather.5.cloned.1.call-done), kind=kOutput, calls=%fused_computation.221 | convolution fusion | flops 2684354560 | bytes 9437184 | tf_op jit(solution)/shard_map/td,dc->tc/dot_general | solution.py:17
  77.5 7.2 %fusion.101 = f32[1024,640]{1,0:T(8,128)} fusion(bf16[1024,2048]{1,0:T(8,128)(2,1)} %collective-permute-done.4, bf16[2048,640]{0,1:T(8,128)(2,1)S(1)} %copy-done.8), kind=kOutput, calls=%fused_computation.222 | convolution fusion | flops 2684354560 | bytes 9437184 | tf_op jit(solution)/shard_map/td,dc->tc/dot_general | solution.py:17
  84.7 12.5 %recur_forward.1 = (f32[8,2,128,256]{3,2,1,0:T(8,128)}, bf16[4,2,128,256]{3,2,1,0:T(8,128)(2,1)}, bf16[4,2,128,256]{3,2,1,0:T(8,128)(2,1)}, f32[8,2,128,1]{3,2,1,0:T(8,128)}) custom-call(s32[1]{0:T(128)} %bitcast.1.place_ref, f32[1]{0:T(128)S(6)} %div.69.floor_ref, f32[4,2,128,640]{3,2,1,0:T(8,128)} %bitcast.160, f32[4,2,128,640]{3,2,1,0:T(8,128)} %bitcast.162, ...), custom_call_target="tpu_custom_call" | custom-call | flops 15728640 | bytes 8388608 | tf_op jit(solution)/shard_map/recur_forward/pallas_call | solution.py:415
  102.7 7.1 fusion.41
  119.9 10.2 %collective-permute-done.10 = bf16[128,2048]{1,0:T(8,128)(2,1)S(1)} collective-permute-done((bf16[128,2048]{1,0:T(8,128)(2,1)S(1)}, bf16[128,2048]{1,0:T(8,128)(2,1)S(1)}, u32[]{:S(2)}, u32[]{:S(2)}) %collective-permute-start.10) | collective-permute-done | bytes 524320 | tf_op jit(solution)/shard_map/ppermute | solution.py:22
  134.7 17.4 %collective-permute-done.6 = f32[2,256]{1,0:T(2,128)S(1)} collective-permute-done((f32[2,256]{1,0:T(2,128)S(1)}, f32[2,256]{1,0:T(2,128)S(1)}, u32[]{:S(2)}, u32[]{:S(2)}) %collective-permute-start.6) | collective-permute-done | bytes 2080 | tf_op jit(solution)/shard_map/ppermute | solution.py:22
  168.0 14.1 %collective-permute-done.27 = bf16[256,2048]{1,0:T(8,128)(2,1)} collective-permute-done((bf16[256,2048]{1,0:T(8,128)(2,1)}, bf16[256,2048]{1,0:T(8,128)(2,1)}, u32[]{:S(2)}, u32[]{:S(2)}) %collective-permute-start.27) | collective-permute-done | bytes 1048608 | tf_op jit(solution)/shard_map/ppermute | solution.py:22
  186.4 18.0 %collective-permute-done.15 = bf16[256,2048]{1,0:T(8,128)(2,1)S(1)} collective-permute-done((bf16[256,2048]{1,0:T(8,128)(2,1)}, bf16[256,2048]{1,0:T(8,128)(2,1)S(1)}, u32[]{:S(2)}, u32[]{:S(2)}) %collective-permute-start.15) | collective-permute-done | bytes 1048608 | tf_op jit(solution)/shard_map/ppermute | solution.py:22
  213.5 12.7 %collective-permute-done.17 = bf16[128,2048]{1,0:T(8,128)(2,1)S(1)} collective-permute-done((bf16[128,2048]{1,0:T(8,128)(2,1)S(1)}, bf16[128,2048]{1,0:T(8,128)(2,1)S(1)}, u32[]{:S(2)}, u32[]{:S(2)}) %collective-permute-start.17) | collective-permute-done | bytes 524320 | tf_op jit(solution)/shard_map/ppermute | solution.py:22
  232.4 12.2 %fusion.102 = f32[1024,1408]{1,0:T(8,128)} fusion(bf16[1024,2048]{1,0:T(8,128)(2,1)} %constant_dynamic-update-slice_fusion.5, bf16[2048,1408]{0,1:T(8,128)(2,1)} %all-gather.9.cloned.1.call-done), kind=kOutput, calls=%fused_computation.223 | convolution fusion | flops 5905580032 | bytes 15728640 | tf_op jit(solution)/shard_map/td,df->tf/dot_general | solution.py:17
  244.7 33.3 %all-gather.11.cloned.1.call-done = bf16[704,2048]{1,0:T(8,128)(2,1)} async-done(((bf16[176,2048]{1,0:T(8,128)(2,1)}), bf16[704,2048]{1,0:T(8,128)(2,1)}) %all-gather.11.cloned.1.call-update) | async-done | bytes 2883600 | tf_op jit(solution)/shard_map/all_gather | solution.py:107
  278.0 11.3 %multiply_convert_fusion.3 = (bf16[1024,704]{1,0:T(8,128)(2,1)}, bf16[1024,704]{1,0:T(8,128)(2,1)}, bf16[1024,704]{1,0:T(8,128)(2,1)}) fusion(f32[1024,1408]{1,0:T(8,128)} %fusion.102, bf16[1024,2048]{1,0:T(8,128)(2,1)} %constant_dynamic-update-slice_fusion.10, bf16[704,2048]{1,0:T(8,128)(2,1)} %all-gather.11.cloned.1.call-done), kind=kOutput, calls=%fused_computation.22 | convolution fusion | flops 2963603456 | bytes 17170432 | tf_op jit(solution)/shard_map/td,fd->tf/dot_general | solution.py:17
  289.3 8.9 %fusion.103 = f32[1024,1408]{1,0:T(8,128)S(1)} fusion(bf16[1024,2048]{1,0:T(8,128)(2,1)} %collective-permute-done.19, bf16[2048,1408]{0,1:T(8,128)(2,1)S(1)} %copy-done.31), kind=kOutput, calls=%fused_computation.224 | convolution fusion | flops 5905580032 | bytes 15728640 | tf_op jit(solution)/shard_map/td,df->tf/dot_general | solution.py:17
  304.7 8.4 %convolution_convert_fusion.1 = bf16[1024,2048]{1,0:T(8,128)(2,1)} fusion(bf16[2048,1408]{0,1:T(8,128)(2,1)S(1)} %copy-done.31, bf16[1024,704]{1,0:T(8,128)(2,1)S(1)} %get-tuple-element.55, bf16[1024,704]{1,0:T(8,128)(2,1)S(1)} %get-tuple-element.54), kind=kOutput, calls=%fused_computation.16 | convolution fusion | flops 5913444352 | bytes 12845056 | tf_op jit(solution)/shard_map/tf,df->td/dot_general | solution.py:17
  318.6 8.9 %fusion.31 = f32[2048,1408]{1,0:T(8,128)S(1)} fusion(bf16[1024,2048]{1,0:T(8,128)(2,1)} %collective-permute-done.19, bf16[1024,704]{1,0:T(8,128)(2,1)S(1)} %copy-done.41, bf16[1024,704]{1,0:T(8,128)(2,1)S(1)} %copy-done.39), kind=kOutput, calls=%fused_computation.74 | convolution fusion | flops 5911347200 | bytes 18612224 | tf_op jit(solution)/shard_map/td,tf->df/dot_general | solution.py:17
  327.5 10.5 %add_convert_fusion = bf16[2048,1408]{1,0:T(8,128)(2,1)S(1)} fusion(f32[2048,1408]{1,0:T(8,128)S(1)} %fusion.31, bf16[1024,2048]{1,0:T(8,128)(2,1)} %constant_dynamic-update-slice_fusion.5, bf16[1024,704]{1,0:T(8,128)(2,1)} %get-tuple-element.53, bf16[1024,704]{1,0:T(8,128)(2,1)} %get-tuple-element.52), kind=kOutput, calls=%fused_computation.6 | convolution fusion | flops 5917114368 | bytes 24379392 | tf_op jit(solution)/shard_map/td,tf->df/dot_general | solution.py:17
  341.0 10.3 %fusion.98 = (bf16[1024,2048]{1,0:T(8,128)(2,1)S(1)}, f32[1024,2048]{1,0:T(8,128)S(1)}) fusion(bf16[1024,2048]{1,0:T(8,128)(2,1)} %collective-permute-done.32, bf16[2048,1408]{0,1:T(8,128)(2,1)} %all-gather.9.cloned.1.call-done, bf16[1024,704]{1,0:T(8,128)(2,1)} %get-tuple-element.53, bf16[1024,704]{1,0:T(8,128)(2,1)} %get-tuple-element.52), kind=kOutput, calls=%fused_computation.219 | convolution fusion | flops 5921832960 | bytes 25427968 | tf_op jit(solution)/shard_map/tf,df->td/dot_general | solution.py:17
  368.8 8.8 %collective-permute-done.22 = bf16[128,2048]{1,0:T(8,128)(2,1)S(1)} collective-permute-done((bf16[128,2048]{1,0:T(8,128)(2,1)S(1)}, bf16[128,2048]{1,0:T(8,128)(2,1)S(1)}, u32[]{:S(2)}, u32[]{:S(2)}) %collective-permute-start.22) | collective-permute-done | bytes 524320 | tf_op jit(solution)/shard_map/ppermute | solution.py:22
  380.1 9.4 %collective-permute-done.33 = bf16[128,2048]{1,0:T(8,128)(2,1)S(1)} collective-permute-done((bf16[128,2048]{1,0:T(8,128)(2,1)S(1)}, bf16[128,2048]{1,0:T(8,128)(2,1)S(1)}, u32[]{:S(2)}, u32[]{:S(2)}) %collective-permute-start.33) | collective-permute-done | bytes 524320 | tf_op jit(solution)/shard_map/ppermute | solution.py:22
  392.4 8.3 %collective-permute-done.21 = bf16[128,2048]{1,0:T(8,128)(2,1)S(1)} collective-permute-done((bf16[128,2048]{1,0:T(8,128)(2,1)S(1)}, bf16[128,2048]{1,0:T(8,128)(2,1)S(1)}, u32[]{:S(2)}, u32[]{:S(2)}) %collective-permute-start.21) | collective-permute-done | bytes 524320 | tf_op jit(solution)/shard_map/ppermute | solution.py:22
  402.2 9.8 %collective-permute-done.35 = bf16[128,2048]{1,0:T(8,128)(2,1)S(1)} collective-permute-done((bf16[128,2048]{1,0:T(8,128)(2,1)S(1)}, bf16[128,2048]{1,0:T(8,128)(2,1)S(1)}, u32[]{:S(2)}, u32[]{:S(2)}) %collective-permute-start.35) | collective-permute-done | bytes 524320 | tf_op jit(solution)/shard_map/ppermute | solution.py:22
  411.9 10.0 %collective-permute-done.23 = bf16[128,2048]{1,0:T(8,128)(2,1)S(1)} collective-permute-done((bf16[128,2048]{1,0:T(8,128)(2,1)S(1)}, bf16[128,2048]{1,0:T(8,128)(2,1)S(1)}, u32[]{:S(2)}, u32[]{:S(2)}) %collective-permute-start.23) | collective-permute-done | bytes 524320 | tf_op jit(solution)/shard_map/ppermute | solution.py:22
  438.3 15.8 %collective-permute-done.39 = bf16[256,2048]{1,0:T(8,128)(2,1)S(1)} collective-permute-done((bf16[256,2048]{1,0:T(8,128)(2,1)S(1)}, bf16[256,2048]{1,0:T(8,128)(2,1)S(1)}, u32[]{:S(2)}, u32[]{:S(2)}) %collective-permute-start.39) | collective-permute-done | bytes 1048608 | tf_op jit(solution)/shard_map/ppermute | solution.py:22
  469.3 7.3 %add_convert_fusion.1 = bf16[704,2048]{1,0:T(8,128)(2,1)} fusion(f32[704,2048]{1,0:T(8,128)S(1)} %fusion.107, bf16[1024,704]{1,0:T(8,128)(2,1)S(1)} %copy-done.37, bf16[1024,2048]{1,0:T(8,128)(2,1)} %constant_dynamic-update-slice_fusion.10), kind=kOutput, calls=%fused_computation.13 | convolution fusion | flops 2955673600 | bytes 14286848 | tf_op jit(solution)/shard_map/tf,td->fd/dot_general | solution.py:17
  498.1 15.9 %recur_backward.1 = (bf16[4,2,128,640]{3,2,1,0:T(8,128)(2,1)}, bf16[4,2,128,640]{3,2,1,0:T(8,128)(2,1)}, f32[1,128]{1,0:T(1,128)}, f32[1,128]{1,0:T(1,128)}, f32[1,256]{1,0:T(1,128)}) custom-call(s32[1]{0:T(128)} %bitcast.1.place_ref, f32[1]{0:T(128)S(6)} %div.69.floor_ref, f32[4,2,128,640]{3,2,1,0:T(8,128)} %bitcast.161, f32[4,2,128,640]{3,2,1,0:T(8,128)} %bitcast.163, ...), custom_call_target="tpu_custom_call" | custom-call | flops 26214400 | bytes 13107200 | tf_op jit(solution)/shard_map/recur_backward/pallas_call | solution.py:458
  542.8 8.5 %fusion.99 = (bf16[1024,2048]{1,0:T(8,128)(2,1)}, f32[1024,2048]{1,0:T(8,128)}) fusion(bf16[1024,2048]{1,0:T(8,128)(2,1)} %collective-permute-done.50, bf16[1024,640]{1,0:T(8,128)(2,1)} %bitcast.172, bf16[2048,640]{0,1:T(8,128)(2,1)S(1)} %copy-done.9), kind=kOutput, calls=%fused_computation.220 | convolution fusion | flops 2694840320 | bytes 20709376 | tf_op jit(solution)/shard_map/tc,dc->td/dot_general | solution.py:17
  597.0 12.2 %collective-permute-done.51 = bf16[128,2048]{1,0:T(8,128)(2,1)S(1)} collective-permute-done((bf16[128,2048]{1,0:T(8,128)(2,1)}, bf16[128,2048]{1,0:T(8,128)(2,1)S(1)}, u32[]{:S(2)}, u32[]{:S(2)}) %collective-permute-start.51) | collective-permute-done | bytes 524320 | tf_op jit(solution)/shard_map/ppermute | solution.py:22
  609.2 11.9 %collective-permute-done.53 = bf16[128,2048]{1,0:T(8,128)(2,1)} collective-permute-done((bf16[128,2048]{1,0:T(8,128)(2,1)}, bf16[128,2048]{1,0:T(8,128)(2,1)}, u32[]{:S(2)}, u32[]{:S(2)}) %collective-permute-start.53) | collective-permute-done | bytes 524320 | tf_op jit(solution)/shard_map/ppermute | solution.py:22
  633.8 13.3 %collective-permute-done.63 = bf16[176,2048]{1,0:T(8,128)(2,1)} collective-permute-done((bf16[176,2048]{1,0:T(8,128)(2,1)}, bf16[176,2048]{1,0:T(8,128)(2,1)}, u32[]{:S(2)}, u32[]{:S(2)}) %collective-permute-start.63) | collective-permute-done | bytes 720928 | tf_op jit(solution)/shard_map/ppermute | solution.py:701
  (380 shorter events, 313.8 us)
Async XLA Ops:
  7.2 62.2 %all-gather.5.cloned.1.call-start = ((), (), s32[]{:S(2)}) async-start(), calls=%async_computation.6 | async-start | bytes 3276800 | tf_op jit(solution)/shard_map/all_gather | solution.py:107
  13.0 85.0 %all-gather.7.cloned.1.call-start = ((), (), s32[]{:S(2)}) async-start(), calls=%async_computation.7 | async-start | bytes 1310720 | tf_op jit(solution)/shard_map/all_gather | solution.py:107
  56.9 175.5 %all-gather.9.cloned.1.call-start = ((), (), s32[]{:S(2)}) async-start(), calls=%async_computation.8 | async-start | bytes 7208960 | tf_op jit(solution)/shard_map/all_gather | solution.py:107
  111.0 167.0 %all-gather.11.cloned.1.call-start = ((), (), s32[]{:S(2)}) async-start(), calls=%async_computation.9 | async-start | bytes 3604480 | tf_op jit(solution)/shard_map/all_gather | solution.py:107
  117.8 39.4 %collective-permute-start.14 = (bf16[128,2048]{1,0:T(8,128)(2,1)S(1)}, bf16[128,2048]{1,0:T(8,128)(2,1)S(1)}, u32[]{:S(2)}, u32[]{:S(2)}) collective-permute-start(bf16[128,2048]{1,0:T(8,128)(2,1)S(1)} %get-tuple-element.77), channel_id=1, source_target_pairs={{0,16},{4,20},{8,24},{12,28},{16,0},{20,4},{24,8},{28,12},{1,17},{... | collective-permute-start | bytes 1572872 | tf_op jit(solution)/shard_map/ppermute | solution.py:22
  119.3 38.5 %collective-permute-start.9 = (bf16[128,2048]{1,0:T(8,128)(2,1)S(1)}, bf16[128,2048]{1,0:T(8,128)(2,1)S(1)}, u32[]{:S(2)}, u32[]{:S(2)}) collective-permute-start(bf16[128,2048]{1,0:T(8,128)(2,1)S(1)} %get-tuple-element.76), channel_id=1, source_target_pairs={{0,8},{4,12},{8,0},{12,4},{16,24},{20,28},{24,16},{28,20},{1,9},{5... | collective-permute-start | bytes 1572872 | tf_op jit(solution)/shard_map/ppermute | solution.py:22
  131.0 26.8 %collective-permute-start.11 = (bf16[128,2048]{1,0:T(8,128)(2,1)S(1)}, bf16[128,2048]{1,0:T(8,128)(2,1)S(1)}, u32[]{:S(2)}, u32[]{:S(2)}) collective-permute-start(bf16[128,2048]{1,0:T(8,128)(2,1)S(1)} %get-tuple-element.80), channel_id=1, source_target_pairs={{0,8},{4,12},{8,0},{12,4},{16,24},{20,28},{24,16},{28,20},{1,9},{5... | collective-permute-start | bytes 1572872 | tf_op jit(solution)/shard_map/ppermute | solution.py:22
  155.7 26.4 %collective-permute-start.27 = (bf16[256,2048]{1,0:T(8,128)(2,1)}, bf16[256,2048]{1,0:T(8,128)(2,1)}, u32[]{:S(2)}, u32[]{:S(2)}) collective-permute-start(bf16[256,2048]{1,0:T(8,128)(2,1)} %bitcast.16), channel_id=1, source_target_pairs={{0,8},{4,12},{8,0},{12,4},{16,24},{20,28},{24,16},{28,20},{1,9},{5... | collective-permute-start | bytes 3145736 | tf_op jit(solution)/shard_map/ppermute | solution.py:22
  157.2 26.6 %collective-permute-start.28 = (bf16[256,2048]{1,0:T(8,128)(2,1)}, bf16[256,2048]{1,0:T(8,128)(2,1)}, u32[]{:S(2)}, u32[]{:S(2)}) collective-permute-start(bf16[256,2048]{1,0:T(8,128)(2,1)} %bitcast.16), channel_id=1, source_target_pairs={{0,16},{4,20},{8,24},{12,28},{16,0},{20,4},{24,8},{28,12},{1,17},{... | collective-permute-start | bytes 3145736 | tf_op jit(solution)/shard_map/ppermute | solution.py:22
  161.4 43.0 %collective-permute-start.15 = (bf16[256,2048]{1,0:T(8,128)(2,1)}, bf16[256,2048]{1,0:T(8,128)(2,1)S(1)}, u32[]{:S(2)}, u32[]{:S(2)}) collective-permute-start(bf16[256,2048]{1,0:T(8,128)(2,1)} %get-tuple-element.46), channel_id=1, source_target_pairs={{0,8},{4,12},{8,0},{12,4},{16,24},{20,28},{24,16},{28,20},{1,9},{5... | collective-permute-start | bytes 3145736 | tf_op jit(solution)/shard_map/ppermute | solution.py:22
  162.0 45.5 %collective-permute-start.16 = (bf16[256,2048]{1,0:T(8,128)(2,1)}, bf16[256,2048]{1,0:T(8,128)(2,1)}, u32[]{:S(2)}, u32[]{:S(2)}) collective-permute-start(bf16[256,2048]{1,0:T(8,128)(2,1)} %get-tuple-element.46), channel_id=1, source_target_pairs={{0,16},{4,20},{8,24},{12,28},{16,0},{20,4},{24,8},{28,12},{1,17},{... | collective-permute-start | bytes 3145736 | tf_op jit(solution)/shard_map/ppermute | solution.py:22
  165.5 390.8 %reduce-scatter.9.cloned.1.call-start = ((), (), s32[]{:S(2)}) async-start(), calls=%async_computation.12 | async-start | bytes 7208960 | tf_op jit(solution)/shard_map/reduce_scatter | solution.py:111
  183.2 47.1 %collective-permute-start.29 = (bf16[128,2048]{1,0:T(8,128)(2,1)S(1)}, bf16[128,2048]{1,0:T(8,128)(2,1)S(1)}, u32[]{:S(2)}, u32[]{:S(2)}) collective-permute-start(bf16[128,2048]{1,0:T(8,128)(2,1)S(1)} %slice.298), channel_id=1, source_target_pairs={{0,16},{4,20},{8,24},{12,28},{16,0},{20,4},{24,8},{28,12},{1,17},{... | collective-permute-start | bytes 1572872 | tf_op jit(solution)/shard_map/ppermute | solution.py:22
  184.9 46.3 %collective-permute-start.30 = (bf16[128,2048]{1,0:T(8,128)(2,1)S(1)}, bf16[128,2048]{1,0:T(8,128)(2,1)S(1)}, u32[]{:S(2)}, u32[]{:S(2)}) collective-permute-start(bf16[128,2048]{1,0:T(8,128)(2,1)S(1)} %slice.299), channel_id=1, source_target_pairs={{0,8},{4,12},{8,0},{12,4},{16,24},{20,28},{24,16},{28,20},{1,9},{5... | collective-permute-start | bytes 1572872 | tf_op jit(solution)/shard_map/ppermute | solution.py:22
  227.8 61.4 %collective-permute-start.19 = (bf16[1024,2048]{1,0:T(8,128)(2,1)}, bf16[1024,2048]{1,0:T(8,128)(2,1)}, u32[]{:S(2)}, u32[]{:S(2)}) collective-permute-start(bf16[1024,2048]{1,0:T(8,128)(2,1)} %constant_dynamic-update-slice_fusion.5), channel_id=1, source_target_pairs={{0,4},{4,0},{8,12},{12,8},{16,20},{20,16},{24,28},{28,24},{1,5},{5... | collective-permute-start | bytes 12582920 | tf_op jit(solution)/shard_map/ppermute | solution.py:22
  232.0 66.2 %collective-permute-start.31 = (bf16[1024,2048]{1,0:T(8,128)(2,1)}, bf16[1024,2048]{1,0:T(8,128)(2,1)}, u32[]{:S(2)}, u32[]{:S(2)}) collective-permute-start(bf16[1024,2048]{1,0:T(8,128)(2,1)} %constant_dynamic-update-slice_fusion.10), channel_id=1, source_target_pairs={{0,4},{4,0},{8,12},{12,8},{16,20},{20,16},{24,28},{28,24},{1,5},{5... | collective-permute-start | bytes 12582920 | tf_op jit(solution)/shard_map/ppermute | solution.py:22
  313.1 27.9 %collective-permute-start.32 = (bf16[1024,2048]{1,0:T(8,128)(2,1)}, bf16[1024,2048]{1,0:T(8,128)(2,1)}, u32[]{:S(2)}, u32[]{:S(2)}) collective-permute-start(bf16[1024,2048]{1,0:T(8,128)(2,1)} %convolution_convert_fusion.1), channel_id=1, source_target_pairs={{0,4},{4,0},{8,12},{12,8},{16,20},{20,16},{24,28},{28,24},{1,5},{5... | collective-permute-start | bytes 12582920 | tf_op jit(solution)/shard_map/ppermute | solution.py:22
  318.1 35.6 %collective-permute-start.20 = (bf16[1024,2048]{1,0:T(8,128)(2,1)}, bf16[1024,2048]{1,0:T(8,128)(2,1)}, u32[]{:S(2)}, u32[]{:S(2)}) collective-permute-start(bf16[1024,2048]{1,0:T(8,128)(2,1)} %convolution_convert_fusion.2), channel_id=1, source_target_pairs={{0,4},{4,0},{8,12},{12,8},{16,20},{20,16},{24,28},{28,24},{1,5},{5... | collective-permute-start | bytes 12582920 | tf_op jit(solution)/shard_map/ppermute | solution.py:22
  341.0 234.4 %reduce-scatter.11.cloned.1.call-start = ((), (), s32[]{:S(2)}) async-start(), calls=%async_computation.13 | async-start | bytes 3604480 | tf_op jit(solution)/shard_map/reduce_scatter | solution.py:111
  363.0 26.5 %collective-permute-start.33 = (bf16[128,2048]{1,0:T(8,128)(2,1)S(1)}, bf16[128,2048]{1,0:T(8,128)(2,1)S(1)}, u32[]{:S(2)}, u32[]{:S(2)}) collective-permute-start(bf16[128,2048]{1,0:T(8,128)(2,1)S(1)} %get-tuple-element.64), channel_id=1, source_target_pairs={{0,8},{4,12},{8,0},{12,4},{16,24},{20,28},{24,16},{28,20},{1,9},{5... | collective-permute-start | bytes 1572872 | tf_op jit(solution)/shard_map/ppermute | solution.py:22
  367.0 33.7 %collective-permute-start.21 = (bf16[128,2048]{1,0:T(8,128)(2,1)S(1)}, bf16[128,2048]{1,0:T(8,128)(2,1)S(1)}, u32[]{:S(2)}, u32[]{:S(2)}) collective-permute-start(bf16[128,2048]{1,0:T(8,128)(2,1)S(1)} %get-tuple-element.70), channel_id=1, source_target_pairs={{0,8},{4,12},{8,0},{12,4},{16,24},{20,28},{24,16},{28,20},{1,9},{5... | collective-permute-start | bytes 1572872 | tf_op jit(solution)/shard_map/ppermute | solution.py:22
  378.2 33.7 %collective-permute-start.35 = (bf16[128,2048]{1,0:T(8,128)(2,1)S(1)}, bf16[128,2048]{1,0:T(8,128)(2,1)S(1)}, u32[]{:S(2)}, u32[]{:S(2)}) collective-permute-start(bf16[128,2048]{1,0:T(8,128)(2,1)S(1)} %get-tuple-element.68), channel_id=1, source_target_pairs={{0,8},{4,12},{8,0},{12,4},{16,24},{20,28},{24,16},{28,20},{1,9},{5... | collective-permute-start | bytes 1572872 | tf_op jit(solution)/shard_map/ppermute | solution.py:22
  390.9 31.0 %collective-permute-start.23 = (bf16[128,2048]{1,0:T(8,128)(2,1)S(1)}, bf16[128,2048]{1,0:T(8,128)(2,1)S(1)}, u32[]{:S(2)}, u32[]{:S(2)}) collective-permute-start(bf16[128,2048]{1,0:T(8,128)(2,1)S(1)} %get-tuple-element.74), channel_id=1, source_target_pairs={{0,8},{4,12},{8,0},{12,4},{16,24},{20,28},{24,16},{28,20},{1,9},{5... | collective-permute-start | bytes 1572872 | tf_op jit(solution)/shard_map/ppermute | solution.py:22
  476.6 172.9 %reduce-scatter.7.cloned.1.call-start = ((), (), s32[]{:S(2)}) async-start(), calls=%async_computation.11 | async-start | bytes 1310720 | tf_op jit(solution)/shard_map/reduce_scatter | solution.py:111
  529.1 144.3 %reduce-scatter.5.cloned.1.call-start = ((), (), s32[]{:S(2)}) async-start(), calls=%async_computation.10 | async-start | bytes 3276800 | tf_op jit(solution)/shard_map/reduce_scatter | solution.py:111
  556.3 96.0 %all-to-all-start.1 = ((bf16[8,64,1408]{2,1,0:T(8,128)(2,1)}), bf16[8,64,1408]{2,1,0:T(8,128)(2,1)S(1)}, u32[]{:S(2)}, u32[]{:S(2)}) async-start(bf16[8,64,1408]{2,1,0:T(8,128)(2,1)} %bitcast.176), calls=%async_computation.4 | async-start | bytes 2883584 | tf_op jit(solution)/shard_map/all_to_all | solution.py:676
  560.7 48.5 %collective-permute-start.51 = (bf16[128,2048]{1,0:T(8,128)(2,1)}, bf16[128,2048]{1,0:T(8,128)(2,1)S(1)}, u32[]{:S(2)}, u32[]{:S(2)}) collective-permute-start(bf16[128,2048]{1,0:T(8,128)(2,1)} %get-tuple-element.58), channel_id=1, source_target_pairs={{0,8},{4,12},{8,0},{12,4},{16,24},{20,28},{24,16},{28,20},{1,9},{5... | collective-permute-start | bytes 1572872 | tf_op jit(solution)/shard_map/ppermute | solution.py:22
  562.2 47.0 %collective-permute-start.56 = (bf16[128,2048]{1,0:T(8,128)(2,1)}, bf16[128,2048]{1,0:T(8,128)(2,1)S(1)}, u32[]{:S(2)}, u32[]{:S(2)}) collective-permute-start(bf16[128,2048]{1,0:T(8,128)(2,1)} %get-tuple-element.59), channel_id=1, source_target_pairs={{0,16},{4,20},{8,24},{12,28},{16,0},{20,4},{24,8},{28,12},{1,17},{... | collective-permute-start | bytes 1572872 | tf_op jit(solution)/shard_map/ppermute | solution.py:22
  572.9 48.1 %collective-permute-start.53 = (bf16[128,2048]{1,0:T(8,128)(2,1)}, bf16[128,2048]{1,0:T(8,128)(2,1)}, u32[]{:S(2)}, u32[]{:S(2)}) collective-permute-start(bf16[128,2048]{1,0:T(8,128)(2,1)} %get-tuple-element.62), channel_id=1, source_target_pairs={{0,8},{4,12},{8,0},{12,4},{16,24},{20,28},{24,16},{28,20},{1,9},{5... | collective-permute-start | bytes 1572872 | tf_op jit(solution)/shard_map/ppermute | solution.py:22
  574.3 46.7 %collective-permute-start.55 = (bf16[128,2048]{1,0:T(8,128)(2,1)}, bf16[128,2048]{1,0:T(8,128)(2,1)}, u32[]{:S(2)}, u32[]{:S(2)}) collective-permute-start(bf16[128,2048]{1,0:T(8,128)(2,1)} %get-tuple-element.63), channel_id=1, source_target_pairs={{0,16},{4,20},{8,24},{12,28},{16,0},{20,4},{24,8},{28,12},{1,17},{... | collective-permute-start | bytes 1572872 | tf_op jit(solution)/shard_map/ppermute | solution.py:22
  575.3 71.8 %collective-permute-start.63 = (bf16[176,2048]{1,0:T(8,128)(2,1)}, bf16[176,2048]{1,0:T(8,128)(2,1)}, u32[]{:S(2)}, u32[]{:S(2)}) collective-permute-start(bf16[176,2048]{1,0:T(8,128)(2,1)} %reduce-scatter.11.cloned.1.call-done), channel_id=1, source_target_pairs={{0,0},{1,8},{2,16},{3,24},{4,1},{5,9},{6,17},{7,25},{8,2},{9,10},{... | collective-permute-start | bytes 2162696 | tf_op jit(solution)/shard_map/ppermute | solution.py:701
  652.3 27.6 %collective-permute-start.59 = (f32[8195]{0:T(1024)S(1)}, f32[8195]{0:T(1024)S(1)}, u32[]{:S(2)}, u32[]{:S(2)}) collective-permute-start(f32[8195]{0:T(1024)S(1)} %add.269), channel_id=1, source_target_pairs={{0,16},{4,20},{8,24},{12,28},{16,0},{20,4},{24,8},{28,12},{1,17},{... | collective-permute-start | bytes 98348 | tf_op jit(solution)/shard_map/ppermute | solution.py:22
  (84 other events, 1175.0 us)
Sparse Core Ops, SparseCore 0:
  13.1 55.9 all-gather.4
  71.3 26.7 all-gather.6
  111.1 107.3 all-gather.8
  220.5 57.4 all-gather.10
  341.1 100.9 reduce-scatter.8
  476.7 55.0 reduce-scatter.10
  534.6 26.9 reduce-scatter.6
  564.1 74.0 reduce-scatter.4

commit v3 on v2

--- a/solution.py
+++ b/solution.py
@@ -27,7 +27,7 @@
     return [1 << i for i in range(1, size.bit_length() - 1)]
 
 
-def gather_even(own):
+def plain_even(own):
     bits = chip_bits()
     if len(bits) == 2:
         first, second = bits
@@ -43,12 +43,12 @@
     return held
 
 
-def gather_seq(own):
-    even = gather_even(own)
+def plain_gather(own):
+    even = plain_even(own)
     return even, swap(even, 1)
 
 
-def scatter_seq(even, odd):
+def plain_scatter(even, odd):
     bits = chip_bits()
     joint = even.astype(F32) + swap(odd, 1).astype(F32)
     if len(bits) == 2:
@@ -78,17 +78,72 @@
     return joint
 
 
+def gather_first(own):
+    return tuple(swap(own, bit) for bit in chip_bits())
+
+
+def gather_far(own, stage):
+    first, second = chip_bits()
+    half = own.shape[0] // 2
+    return swap(stage[0][:half], second), swap(stage[1][half:], first)
+
+
+def cross(pieces):
+    return tuple(swap(piece, 1) for piece in pieces)
+
+
+def joints(even, crossed):
+    half = even[0].shape[0] // 2
+    sums = []
+    for index in (1, 2, 3):
+        for rows in (slice(0, half), slice(half, None)):
+            both = even[index][rows].astype(F32) + crossed[index][rows].astype(F32)
+            sums.append(both.astype(BF))
+    return tuple(sums)
+
+
+def scatter_first(sums):
+    first, second = chip_bits()
+    return swap(sums[4], first), swap(sums[5], second), swap(sums[0], first), swap(sums[3], second)
+
+
+def scatter_last(even, crossed, sums, stage):
+    first, second = chip_bits()
+    far_top, far_low, first_top, second_low = stage
+    first_low = swap((sums[1].astype(F32) + far_low.astype(F32)).astype(BF), first)
+    second_top = swap((sums[2].astype(F32) + far_top.astype(F32)).astype(BF), second)
+    first_all = jnp.concatenate([first_top, first_low], axis=0).astype(F32)
+    second_all = jnp.concatenate([second_top, second_low], axis=0).astype(F32)
+    return even[0].astype(F32) + crossed[0].astype(F32) + first_all + second_all
+
+
+def tied(*values):
+    return lax.optimization_barrier(values)
+
+
+def grow(held, bit):
+    return jnp.concatenate([held, swap(held, bit)], axis=0)
+
+
+def shrink(blocks, bit):
+    half = blocks.shape[0] // 2
+    return blocks[:half] + swap(blocks[half:], bit)
+
+
+def slot_rows(held):
+    pairs = held.reshape(held.shape[0] // 2, 2, -1)
+    return pairs.transpose(1, 0, 2).reshape(held.shape)
+
+
 def gather_small(own):
-    held = own
-    for bit in chip_bits() + [1]:
-        held = jnp.concatenate([held, swap(held, bit)], axis=0)
-    return held
+    for bit in [1] + chip_bits():
+        own = grow(own, bit)
+    return slot_rows(own)
 
 
 def scatter_small(blocks):
     for bit in [1] + list(reversed(chip_bits())):
-        half = blocks.shape[0] // 2
-        blocks = blocks[:half] + swap(blocks[half:], bit)
+        blocks = shrink(blocks, bit)
     return blocks
 
 
@@ -103,12 +158,35 @@
     return value
 
 
-def gather_shard(value):
-    return lax.all_gather(value, "wshard", axis=0, tiled=True)
-
-
-def scatter_shard(value):
-    return lax.psum_scatter(value, "wshard", scatter_dimension=0, tiled=True)
+LANES = 128
+SMALL = pl.CostEstimate(flops=1024, transcendentals=0, bytes_accessed=1024)
+
+
+def filler(flops):
+    return pl.CostEstimate(flops=flops, transcendentals=0, bytes_accessed=1024)
+
+
+def pack(arrays):
+    lines = []
+    for array in arrays:
+        count, rows, cols = array.shape
+        split = array.reshape(count, rows, cols // LANES, LANES).transpose(0, 2, 1, 3)
+        lines.append(split.reshape(count, rows * cols // LANES, LANES))
+    return jnp.concatenate(lines, axis=1)
+
+
+def gather_packed(packed):
+    return lax.all_gather(packed, "wshard", axis=0, tiled=True)
+
+
+def scatter_packed(packed):
+    return lax.psum_scatter(
+        packed.reshape(-1, LANES), "wshard", scatter_dimension=0, tiled=True
+    )
+
+
+def after(value, *others):
+    return lax.optimization_barrier((value, others))[0]
 
 
 def slot_of(place, group, groups):
@@ -247,6 +325,8 @@
     term_ref,
     out_even,
     out_odd,
+    scaled_even,
+    scaled_odd,
     sum_bias,
     sum_theta,
     sum_gain,
@@ -273,13 +353,15 @@
         sum_theta[...] = jnp.zeros_like(sum_theta)
         sum_gain[...] = jnp.zeros_like(sum_gain)
 
-    for half, pre_ref, up_ref, out_ref in (
-        (0, pre_even, up_even, out_even),
-        (1, pre_odd, up_odd, out_odd),
+    for half, pre_ref, up_ref, out_ref, scaled_ref in (
+        (0, pre_even, up_even, out_even, scaled_even),
+        (1, pre_odd, up_odd, out_odd, scaled_odd),
     ):
 
         @pl.loop(0, half_groups)
-        def _(index, half=half, pre_ref=pre_ref, up_ref=up_ref, out_ref=out_ref):
+        def _(
+            index, half=half, pre_ref=pre_ref, up_ref=up_ref, out_ref=out_ref, scaled_ref=scaled_ref
+        ):
             slot = index + half * half_groups
             rows = token_rows(slot, tokens)
             pre = pre_ref[index, 0]
@@ -289,6 +371,7 @@
             mixed = state_ref[slot, 0].astype(BF).astype(F32)
             sig = jax.nn.sigmoid(pre[:, 3 * chan :])
             inner = up_ref[index, 0] * sig
+            scaled_ref[index, 0] = (mixed * gain_ref[...] * sig * scale).astype(BF)
             normed = inner * mixed * scale
             sum_gain[...] += jnp.sum(normed, axis=0, keepdims=True)
             out_ref[index, 0, :, 3 * chan :] = (normed * gain_ref[...] * (1.0 - sig)).astype(BF)
@@ -435,9 +518,7 @@
         scratch_shapes=[pltpu.VMEM((rows, chan), F32)] * 5
         + [pltpu.VMEM((groups, chan), F32)] * 2,
         compiler_params=pltpu.CompilerParams(vmem_limit_bytes=56 * 2**20),
-        cost_estimate=pl.CostEstimate(
-            flops=60 * size, bytes_accessed=32 * size, transcendentals=5 * size
-        ),
+        cost_estimate=SMALL,
         name="recur_forward",
     )(place, floor, pre_even, pre_odd, flags, bias, theta, gain)
 
@@ -454,6 +535,7 @@
     one = block_spec(groups, tokens, 1)
     up_spec = block_spec(half, tokens, 2 * chan)
     out_shape = jax.ShapeDtypeStruct((half, seqs, tokens, 5 * chan), BF)
+    scaled_shape = jax.ShapeDtypeStruct((half, seqs, tokens, 2 * chan), BF)
     size = seqs * rows * chan
     return pl.pallas_call(
         backward_kernel,
@@ -473,10 +555,20 @@
             one,
             one,
         ],
-        out_specs=[pre_spec, pre_spec, row_spec(chan), row_spec(chan), row_spec(2 * chan)],
+        out_specs=[
+            pre_spec,
+            pre_spec,
+            up_spec,
+            up_spec,
+            row_spec(chan),
+            row_spec(chan),
+            row_spec(2 * chan),
+        ],
         out_shape=[
             out_shape,
             out_shape,
+            scaled_shape,
+            scaled_shape,
             jax.ShapeDtypeStruct((1, chan), F32),
             jax.ShapeDtypeStruct((1, chan), F32),
             jax.ShapeDtypeStruct((1, 2 * chan), F32),
@@ -484,16 +576,614 @@
         scratch_shapes=[pltpu.VMEM((rows, chan), F32)] * 5
         + [pltpu.VMEM((groups, chan), F32)] * 3,
         compiler_params=pltpu.CompilerParams(vmem_limit_bytes=56 * 2**20),
-        cost_estimate=pl.CostEstimate(
-            flops=100 * size, bytes_accessed=50 * size, transcendentals=8 * size
-        ),
+        cost_estimate=SMALL,
         name="recur_backward",
     )(
         place, floor, pre_even, pre_odd, flags, bias, theta, gain, state, up_even, up_odd, scale, term
     )
 
 
-def body(
+def unpack_columns(packed, out):
+    planes = packed.shape[0]
+    rows = out.shape[0] // planes
+    for plane in range(planes):
+        for tile in range(out.shape[1] // LANES):
+            out[plane * rows : (plane + 1) * rows, tile * LANES : (tile + 1) * LANES] = packed[
+                plane, tile * rows : (tile + 1) * rows, :
+            ]
+
+
+def unpack_rows(packed, first, out):
+    planes = packed.shape[0]
+    rows = out.shape[0] // planes
+    for plane in range(planes):
+        for tile in range(out.shape[1] // LANES):
+            base = first + tile * rows
+            out[plane * rows : (plane + 1) * rows, tile * LANES : (tile + 1) * LANES] = packed[
+                plane, base : base + rows, :
+            ]
+
+
+def dot_nn(left, right):
+    return jnp.dot(left, right, preferred_element_type=F32)
+
+
+def dot_nt(left, right):
+    return lax.dot_general(left, right, (((1,), (1,)), ((), ())), preferred_element_type=F32)
+
+
+def dot_tn(left, right):
+    return lax.dot_general(left, right, (((0,), (0,)), ((), ())), preferred_element_type=F32)
+
+
+def dot_nn(left, right):
+    return jnp.dot(left, right, preferred_element_type=F32)
+
+
+def dot_nt(left, right):
+    return lax.dot_general(left, right, (((1,), (1,)), ((), ())), preferred_element_type=F32)
+
+
+def dot_tn(left, right):
+    return lax.dot_general(left, right, (((0,), (0,)), ((), ())), preferred_element_type=F32)
+
+
+PIECES = 5
+ANYWHERE = pl.BlockSpec(memory_space=pl.ANY)
+SCALAR = pl.BlockSpec(memory_space=pltpu.SMEM)
+
+
+def slot_copies(pieces, held, sems, slot):
+    if slot < 3:
+        return [pltpu.make_async_copy(pieces[slot], held.at[slot], sems.at[slot])]
+    half = held.shape[1] // 2
+    return [
+        pltpu.make_async_copy(
+            pieces[3 + part], held.at[3, part * half : (part + 1) * half], sems.at[3 + part]
+        )
+        for part in range(2)
+    ]
+
+
+def ffn_kernel(based, last, *refs):
+    packed_ref = refs[0]
+    normed, up = refs[1 : 1 + PIECES], refs[1 + PIECES : 1 + 2 * PIECES]
+    rest = list(refs[1 + 2 * PIECES :])
+    base_ref = rest.pop(0) if based else None
+    hidden_ref, grad_ref = rest[:2]
+    backs = rest[2 : 6 if last else 3]
+    ff_s, down_s, normed_s, up_s, normed_sems, up_sems = rest[6 if last else 3 :]
+    hidden = down_s.shape[0]
+    step = pl.program_id(0)
+    slots = normed_s.shape[0]
+
+    @pl.when(step == 0)
+    def _():
+        for slot in range(slots):
+            for copy in slot_copies(normed, normed_s, normed_sems, slot):
+                copy.start()
+            for copy in slot_copies(up, up_s, up_sems, slot):
+                copy.start()
+        first = ff_s.shape[0] // packed_ref.shape[0] * (ff_s.shape[1] // LANES)
+        unpack_columns(packed_ref, ff_s)
+        unpack_rows(packed_ref, first, down_s)
+
+    for slot in range(slots):
+
+        @pl.when(step == slot)
+        def _(slot=slot):
+            for copy in slot_copies(normed, normed_s, normed_sems, slot):
+                copy.wait()
+            for copy in slot_copies(up, up_s, up_sems, slot):
+                copy.wait()
+
+    ff = dot_nn(normed_s[step], ff_s[...])
+    gate, value = ff[:, :hidden], ff[:, hidden:]
+    sig = jax.nn.sigmoid(gate)
+    silu = gate * sig
+    hidden_ref[...] = (silu * value).astype(BF)
+    grad = dot_nt(up_s[step], down_s[...])
+    grad_ref[:, :hidden] = (grad * value * sig * (1.0 + gate * (1.0 - sig))).astype(BF)
+    grad_ref[:, hidden:] = (grad * silu).astype(BF)
+    back = dot_nt(grad_ref[...], ff_s[...])
+    if based:
+        back = back + base_ref[...]
+    if last:
+        for slot in range(slots):
+
+            @pl.when(step == slot)
+            def _(slot=slot):
+                backs[slot][...] = back.astype(BF)
+    else:
+        backs[0][...] = back
+
+
+def ffn_call(normed, upstream, packed, ff_cols, base, last):
+    rows, width = normed[0].shape
+    slots = 4
+    tokens = slots * rows
+    hidden = ff_cols // 2
+    wide = pl.BlockSpec((rows, width), lambda i: (i, 0))
+    whole = pl.BlockSpec((rows, width), lambda i: (0, 0))
+    operands = [packed, *normed, *upstream]
+    in_specs = [
+        pl.BlockSpec(packed.shape, lambda i: (0, 0, 0), pipeline_mode=pl.Buffered(1)),
+    ] + [ANYWHERE] * (2 * PIECES)
+    if base is not None:
+        operands.append(base)
+        in_specs.append(wide)
+    backs = [jax.ShapeDtypeStruct((tokens, width), F32)]
+    if last:
+        backs = [jax.ShapeDtypeStruct((rows, width), BF)] * slots
+    return pl.pallas_call(
+        functools.partial(ffn_kernel, base is not None, last),
+        grid=(slots,),
+        in_specs=in_specs,
+        out_specs=[
+            pl.BlockSpec((rows, hidden), lambda i: (i, 0)),
+            pl.BlockSpec((rows, ff_cols), lambda i: (i, 0)),
+        ]
+        + ([whole] * slots if last else [wide]),
+        out_shape=[
+            jax.ShapeDtypeStruct((tokens, hidden), BF),
+            jax.ShapeDtypeStruct((tokens, ff_cols), BF),
+            *backs,
+        ],
+        scratch_shapes=[
+            pltpu.VMEM((width, ff_cols), BF),
+            pltpu.VMEM((hidden, width), BF),
+            pltpu.VMEM((slots, rows, width), BF),
+            pltpu.VMEM((slots, rows, width), BF),
+            pltpu.SemaphoreType.DMA((PIECES,)),
+            pltpu.SemaphoreType.DMA((PIECES,)),
+        ],
+        compiler_params=pltpu.CompilerParams(vmem_limit_bytes=56 * 2**20),
+        cost_estimate=SMALL,
+        name="ffn",
+    )(*operands)
+
+
+def grads_kernel(planes, *refs):
+    left = refs[: 2 * PIECES]
+    up = refs[2 * PIECES : 4 * PIECES]
+    cols_even, cols_odd, rows_even, rows_odd, out_ref = refs[4 * PIECES :]
+    step = pl.program_id(0)
+    steps = pl.num_programs(0)
+    block = left[0].shape[1]
+    run = block // planes
+    tiles = cols_even.shape[1] // LANES
+    count = rows_even.shape[1] // planes
+
+    def joined(pieces):
+        return jnp.concatenate([piece[...] for piece in pieces], axis=0)
+
+    grad = dot_tn(joined(left[:PIECES]), cols_even[...])
+    grad = (grad + dot_tn(joined(left[PIECES:]), cols_odd[...])).astype(BF)
+    for plane in range(planes):
+        for tile in range(tiles):
+            lines = pl.ds(pl.multiple_of((step * tiles + tile) * run, run), run)
+            out_ref[plane, lines, :] = grad[
+                plane * run : (plane + 1) * run, tile * LANES : (tile + 1) * LANES
+            ]
+    grad = dot_tn(rows_even[...], joined(up[:PIECES]))
+    grad = (grad + dot_tn(rows_odd[...], joined(up[PIECES:]))).astype(BF)
+    first = block // planes * tiles * steps
+    for plane in range(planes):
+        for tile in range(block // LANES):
+            base = first + (step * (block // LANES) + tile) * count
+            lines = pl.ds(pl.multiple_of(base, 16), count)
+            out_ref[plane, lines, :] = grad[
+                plane * count : (plane + 1) * count, tile * LANES : (tile + 1) * LANES
+            ]
+
+
+def grads_call(groups, planes, left, cols, rows, up):
+    width = left[0][0].shape[1]
+    tokens = cols[0].shape[0]
+    block = width // groups
+    col_count = cols[0].shape[1]
+    row_count = rows[0].shape[1]
+    lines = (col_count * width + row_count * width) // (planes * LANES)
+    pieces = [*left[0], *left[1], *up[0], *up[1]]
+
+    def whole(array):
+        return pl.BlockSpec(array.shape, lambda i: (0, 0), pipeline_mode=pl.Buffered(1))
+
+    return pl.pallas_call(
+        functools.partial(grads_kernel, planes),
+        grid=(groups,),
+        in_specs=[pl.BlockSpec((piece.shape[0], block), lambda i: (0, i)) for piece in pieces]
+        + [whole(cols[0]), whole(cols[1]), whole(rows[0]), whole(rows[1])],
+        out_specs=pl.BlockSpec((planes, lines, LANES), lambda i: (0, 0, 0)),
+        out_shape=jax.ShapeDtypeStruct((planes, lines, LANES), BF),
+        compiler_params=pltpu.CompilerParams(vmem_limit_bytes=56 * 2**20),
+        cost_estimate=filler(4 * tokens * width * (col_count + row_count)),
+        name="weight_grads",
+    )(*pieces, *cols, *rows)
+
+
+def result_kernel(firsts, *refs):
+    hidden_first, hidden_second, packed_first, packed_second = refs[:4]
+    outs, down_s = refs[4:-1], refs[-1]
+    rows = hidden_first.shape[1]
+    step = pl.program_id(0)
+
+    @pl.when(step == 0)
+    def _():
+        unpack_rows(packed_first, firsts[0], down_s.at[:rows])
+        unpack_rows(packed_second, firsts[1], down_s.at[rows:])
+
+    out = dot_nn(hidden_first[...], down_s[:rows, :]) + dot_nn(hidden_second[...], down_s[rows:, :])
+    for slot in range(len(outs)):
+
+        @pl.when(step == slot)
+        def _(slot=slot):
+            outs[slot][...] = out.astype(BF)
+
+
+def result_call(hidden, packed, width):
+    slots = 4
+    tokens = hidden[0].shape[0]
+    rows = tokens // slots
+    total = sum(item.shape[1] for item in hidden)
+    firsts = tuple(
+        part.shape[1] - item.shape[1] // part.shape[0] * width // LANES
+        for part, item in zip(packed, hidden)
+    )
+    return pl.pallas_call(
+        functools.partial(result_kernel, firsts),
+        grid=(slots,),
+        in_specs=[pl.BlockSpec((rows, item.shape[1]), lambda i: (i, 0)) for item in hidden]
+        + [
+            pl.BlockSpec(part.shape, lambda i: (0, 0, 0), pipeline_mode=pl.Buffered(1))
+            for part in packed
+        ],
+        out_specs=[pl.BlockSpec((rows, width), lambda i: (0, 0))] * slots,
+        out_shape=[jax.ShapeDtypeStruct((rows, width), BF)] * slots,
+        scratch_shapes=[pltpu.VMEM((total, width), BF)],
+        compiler_params=pltpu.CompilerParams(vmem_limit_bytes=48 * 2**20),
+        cost_estimate=filler(2 * tokens * width * total),
+        name="ffn_result",
+    )(*hidden, *packed)
+
+
+def seq_copies(pieces, held, sems, seq):
+    tokens = held.shape[2]
+    rows = slice(seq * tokens, (seq + 1) * tokens)
+    copies = [
+        pltpu.make_async_copy(pieces[slot].at[rows], held.at[seq, slot], sems.at[seq, slot])
+        for slot in range(3)
+    ]
+    copies.append(pltpu.make_async_copy(pieces[3 + seq], held.at[seq, 3], sems.at[seq, 3]))
+    return copies
+
+
+def fetch(groups):
+    seqs = groups[0][1].shape[0]
+
+    @pl.when(pl.program_id(0) == 0)
+    def _():
+        for seq in range(seqs):
+            for pieces, held, sems in groups:
+                for copy in seq_copies(pieces, held, sems, seq):
+                    copy.start()
+
+
+def arrive(groups):
+    for seq in range(groups[0][1].shape[0]):
+
+        @pl.when(pl.program_id(0) == seq)
+        def _(seq=seq):
+            for pieces, held, sems in groups:
+                for copy in seq_copies(pieces, held, sems, seq):
+                    copy.wait()
+
+
+def unpack_mix(packed_ref, rec_s, out_s):
+    @pl.when(pl.program_id(0) == 0)
+    def _():
+        lines = rec_s.shape[0] // packed_ref.shape[0] * (rec_s.shape[1] // LANES)
+        unpack_columns(packed_ref, rec_s)
+        unpack_rows(packed_ref, lines, out_s)
+
+
+def mix_forward_kernel(*refs):
+    place_ref, floor_ref, packed_ref, flag_ref, bias_ref, theta_ref, gain_ref = refs[:7]
+    refs = refs[7:]
+    even, odd = refs[:PIECES], refs[PIECES : 2 * PIECES]
+    refs = refs[2 * PIECES :]
+    pre_even, pre_odd, state_ref, square_ref = refs[:4]
+    mix_even, mix_odd = refs[4:8], refs[8:12]
+    rec_s, out_s, gated_even, gated_odd, x_even, x_odd, sems_even, sems_odd = refs[12:20]
+    scratch = refs[20:]
+    half, _, tokens, _ = pre_even.shape
+    seq = pl.program_id(0)
+    groups = ((even, x_even, sems_even), (odd, x_odd, sems_odd))
+    fetch(groups)
+    unpack_mix(packed_ref, rec_s, out_s)
+    arrive(groups)
+    for x_ref, pre_ref in ((x_even, pre_even), (x_odd, pre_odd)):
+
+        @pl.loop(0, half, step=2)
+        def _(index, x_ref=x_ref, pre_ref=pre_ref):
+            pair = pl.ds(index, 2)
+            x = x_ref[seq, pair].reshape(2 * tokens, -1)
+            pre_ref[pair, 0] = dot_nn(x, rec_s[...]).reshape(2, tokens, -1)
+
+    forward_kernel(
+        place_ref,
+        floor_ref,
+        pre_even,
+        pre_odd,
+        flag_ref,
+        bias_ref,
+        theta_ref,
+        gain_ref,
+        state_ref,
+        gated_even,
+        gated_odd,
+        square_ref,
+        *scratch,
+    )
+    for gated_ref, mixes in ((gated_odd, mix_odd), (gated_even, mix_even)):
+        for index in range(0, half, 2):
+            gated = gated_ref[index : index + 2, 0].reshape(2 * tokens, -1)
+            mix = dot_nn(gated, out_s[...]).astype(BF)
+            mixes[index][0] = mix[:tokens]
+            mixes[index + 1][0] = mix[tokens:]
+
+
+def mix_forward(place, floor, even, odd, packed, flags, bias, theta, gain):
+    groups, seqs, tokens, _ = flags.shape
+    chan = bias.shape[1]
+    half = groups // 2
+    width = even[0].shape[-1]
+    rows = groups * tokens
+    pre_spec = block_spec(half, tokens, 5 * chan)
+    one = block_spec(groups, tokens, 1)
+    pre_shape = jax.ShapeDtypeStruct((half, seqs, tokens, 5 * chan), F32)
+    mix_spec = pl.BlockSpec((1, tokens, width), lambda b: (b, 0, 0))
+    mix_shape = jax.ShapeDtypeStruct((seqs, tokens, width), BF)
+    gated = pltpu.VMEM((half, 1, tokens, 2 * chan), BF)
+    held = pltpu.VMEM((seqs, half, tokens, width), BF)
+    sems = pltpu.SemaphoreType.DMA((seqs, half))
+    return pl.pallas_call(
+        mix_forward_kernel,
+        grid=(seqs,),
+        in_specs=[
+            SCALAR,
+            SCALAR,
+            pl.BlockSpec(packed.shape, lambda b: (0, 0, 0), pipeline_mode=pl.Buffered(1)),
+            one,
+            row_spec(chan),
+            row_spec(chan),
+            row_spec(2 * chan),
+        ]
+        + [ANYWHERE] * (2 * PIECES),
+        out_specs=[pre_spec, pre_spec, block_spec(groups, tokens, 2 * chan), one]
+        + [mix_spec] * (2 * half),
+        out_shape=[
+            pre_shape,
+            pre_shape,
+            jax.ShapeDtypeStruct((groups, seqs, tokens, 2 * chan), F32),
+            jax.ShapeDtypeStruct((groups, seqs, tokens, 1), F32),
+        ]
+        + [mix_shape] * (2 * half),
+        scratch_shapes=[
+            pltpu.VMEM((width, 5 * chan), BF),
+            pltpu.VMEM((2 * chan, width), BF),
+            gated,
+            gated,
+            held,
+            held,
+            sems,
+            sems,
+        ]
+        + [pltpu.VMEM((rows, chan), F32)] * 5
+        + [pltpu.VMEM((groups, chan), F32)] * 2,
+        compiler_params=pltpu.CompilerParams(vmem_limit_bytes=60 * 2**20),
+        cost_estimate=SMALL,
+        name="mix_forward",
+    )(place, floor, packed, flags, bias, theta, gain, *even, *odd)
+
+
+def mix_backward_kernel(*refs):
+    place_ref, floor_ref, packed_ref = refs[:3]
+    pre_even, pre_odd, flag_ref, bias_ref, theta_ref, gain_ref, state_ref = refs[3:10]
+    scale_ref, term_ref = refs[10:12]
+    refs = refs[12:]
+    even, odd = refs[:PIECES], refs[PIECES : 2 * PIECES]
+    refs = refs[2 * PIECES :]
+    out_even, out_odd, scaled_even, scaled_odd, sum_bias, sum_theta, sum_gain = refs[:7]
+    back_even, back_odd = refs[7:11], refs[11:15]
+    rec_s, out_s, up_even, up_odd, x_even, x_odd, sems_even, sems_odd = refs[15:23]
+    scratch = refs[23:]
+    half, _, tokens, _ = pre_even.shape
+    seq = pl.program_id(0)
+    groups = ((even, x_even, sems_even), (odd, x_odd, sems_odd))
+    fetch(groups)
+    unpack_mix(packed_ref, rec_s, out_s)
+    arrive(groups)
+    for x_ref, up_ref in ((x_even, up_even), (x_odd, up_odd)):
+
+        @pl.loop(0, half, step=2)
+        def _(index, x_ref=x_ref, up_ref=up_ref):
+            pair = pl.ds(index, 2)
+            branch = x_ref[seq, pair].reshape(2 * tokens, -1)
+            up_ref[pair, 0] = dot_nt(branch, out_s[...]).reshape(2, tokens, -1)
+
+    backward_kernel(
+        place_ref,
+        floor_ref,
+        pre_even,
+        pre_odd,
+        flag_ref,
+        bias_ref,
+        theta_ref,
+        gain_ref,
+        state_ref,
+        up_even,
+        up_odd,
+        scale_ref,
+        term_ref,
+        out_even,
+        out_odd,
+        scaled_even,
+        scaled_odd,
+        sum_bias,
+        sum_theta,
+        sum_gain,
+        *scratch,
+    )
+    for out_ref, backs in ((out_odd, back_odd), (out_even, back_even)):
+        for index in range(0, half, 2):
+            grad = out_ref[index : index + 2, 0].reshape(2 * tokens, -1)
+            back = dot_nt(grad, rec_s[...]).astype(BF)
+            backs[index][0] = back[:tokens]
+            backs[index + 1][0] = back[tokens:]
+
+
+def mix_backward(
+    place, floor, packed, pre_even, pre_odd, flags, bias, theta, gain, state, scale, term,
+    even, odd,
+):
+    groups, seqs, tokens, _ = flags.shape
+    chan = bias.shape[1]
+    half = groups // 2
+    width = even[0].shape[-1]
+    rows = groups * tokens
+    pre_spec = block_spec(half, tokens, 5 * chan)
+    one = block_spec(groups, tokens, 1)
+    pair_spec = block_spec(half, tokens, 2 * chan)
+    back_spec = pl.BlockSpec((1, tokens, width), lambda b: (b, 0, 0))
+    pre_shape = jax.ShapeDtypeStruct((half, seqs, tokens, 5 * chan), BF)
+    pair_shape = jax.ShapeDtypeStruct((half, seqs, tokens, 2 * chan), BF)
+    up = pltpu.VMEM((half, 1, tokens, 2 * chan), F32)
+    held = pltpu.VMEM((seqs, half, tokens, width), BF)
+    sems = pltpu.SemaphoreType.DMA((seqs, half))
+    return pl.pallas_call(
+        mix_backward_kernel,
+        grid=(seqs,),
+        in_specs=[
+            SCALAR,
+            SCALAR,
+            pl.BlockSpec(packed.shape, lambda b: (0, 0, 0), pipeline_mode=pl.Buffered(1)),
+            pre_spec,
+            pre_spec,
+            one,
+            row_spec(chan),
+            row_spec(chan),
+            row_spec(2 * chan),
+            block_spec(groups, tokens, 2 * chan),
+            one,
+            one,
+        ]
+        + [ANYWHERE] * (2 * PIECES),
+        out_specs=[
+            pre_spec,
+            pre_spec,
+            pair_spec,
+            pair_spec,
+            row_spec(chan),
+            row_spec(chan),
+            row_spec(2 * chan),
+        ]
+        + [back_spec] * (2 * half),
+        out_shape=[
+            pre_shape,
+            pre_shape,
+            pair_shape,
+            pair_shape,
+            jax.ShapeDtypeStruct((1, chan), F32),
+            jax.ShapeDtypeStruct((1, chan), F32),
+            jax.ShapeDtypeStruct((1, 2 * chan), F32),
+        ]
+        + [jax.ShapeDtypeStruct((seqs, tokens, width), BF)] * (2 * half),
+        scratch_shapes=[
+            pltpu.VMEM((width, 5 * chan), BF),
+            pltpu.VMEM((2 * chan, width), BF),
+            up,
+            up,
+            held,
+            held,
+            sems,
+            sems,
+        ]
+        + [pltpu.VMEM((rows, chan), F32)] * 5
+        + [pltpu.VMEM((groups, chan), F32)] * 3,
+        compiler_params=pltpu.CompilerParams(vmem_limit_bytes=60 * 2**20),
+        cost_estimate=SMALL,
+        name="mix_backward",
+    )(
+        place, floor, packed, pre_even, pre_odd, flags, bias, theta, gain, state, scale,
+        term, *even, *odd,
+    )
+
+
+def assemble_tiles_kernel(shares, *refs):
+    sources, outs = refs[: len(shares)], refs[len(shares) :]
+    groups = sources[0].shape[0]
+    run = sum(shares)
+    for group in range(groups):
+        wides = [
+            jnp.concatenate(
+                [source[group, tile].astype(F32) for tile in range(source.shape[1])], axis=1
+            )
+            for source in sources
+        ]
+        firsts = [0] * len(shares)
+        for out in outs:
+            for block in range(out.shape[1] // (groups * run)):
+                base = (block * groups + group) * run
+                for index, share in enumerate(shares):
+                    first = firsts[index]
+                    out[:, base : base + share] = wides[index][:, first : first + share]
+                    firsts[index] += share
+                    base += share
+
+
+def assemble_tiles(parts, shares, widths):
+    rows = parts[0].shape[2]
+    return pl.pallas_call(
+        functools.partial(assemble_tiles_kernel, shares),
+        out_shape=[jax.ShapeDtypeStruct((rows, width), F32) for width in widths],
+        compiler_params=pltpu.CompilerParams(vmem_limit_bytes=48 * 2**20),
+        cost_estimate=SMALL,
+        name="assemble_columns",
+    )(*parts)
+
+
+def assemble_rows_kernel(*refs):
+    out = refs[-1]
+    base = 0
+    for source in refs[:-1]:
+        tiles, rows, _ = source.shape
+        for tile in range(tiles):
+            out[base : base + rows, tile * LANES : (tile + 1) * LANES] = source[tile].astype(F32)
+        base += rows
+
+
+def assemble_rows(parts):
+    rows = sum(part.shape[1] for part in parts)
+    width = parts[0].shape[0] * LANES
+    return pl.pallas_call(
+        assemble_rows_kernel,
+        out_shape=jax.ShapeDtypeStruct((rows, width), F32),
+        compiler_params=pltpu.CompilerParams(vmem_limit_bytes=48 * 2**20),
+        cost_estimate=SMALL,
+        name="assemble_rows",
+    )(*parts)
+
+
+def shard_gather(value):
+    return lax.all_gather(value, "wshard", axis=0, tiled=True)
+
+
+def shard_scatter(value):
+    return lax.psum_scatter(value, "wshard", scatter_dimension=0, tiled=True)
+
+
+def plain_body(
     tokens,
     starts,
     layer_index,
@@ -544,10 +1234,10 @@
     resid_in = tokens.reshape(rows, width).astype(F32)
     scale_in = lax.rsqrt(jnp.mean(resid_in * resid_in, axis=1, keepdims=True) + EPS)
     normed_own = (resid_in * scale_in * gain_mix).astype(BF)
-    normed_even, normed_odd = gather_seq(normed_own)
+    normed_even, normed_odd = plain_gather(normed_own)
     upstream_own = out_grad.reshape(rows, width)
 
-    rec_w = gather_shard(
+    rec_w = shard_gather(
         jnp.concatenate(
             [
                 own_columns(w_in, mix_run),
@@ -557,11 +1247,11 @@
             axis=1,
         )
     )
-    out_w = gather_shard(own_rows(w_out))
-    ff_w = gather_shard(
+    out_w = shard_gather(own_rows(w_out))
+    ff_w = shard_gather(
         jnp.concatenate([own_columns(w_ffgate, ffn_run), own_columns(w_ffup, ffn_run)], axis=1)
     )
-    down_w = gather_shard(own_rows(w_down))
+    down_w = shard_gather(own_rows(w_down))
 
     slots = lax.broadcasted_iota(jnp.int32, (groups, groups), 0)
     sources = lax.broadcasted_iota(jnp.int32, (groups, groups), 1)
@@ -591,12 +1281,12 @@
     square_own = scatter_small(square.reshape(groups, rows))
     scale_own = lax.rsqrt(square_own / width + EPS)
     scale_out = scale_own.reshape(rows, 1)
-    branch_mix = scale_out * scatter_seq(mix(gated_even), mix(gated_odd))
+    branch_mix = scale_out * plain_scatter(mix(gated_even), mix(gated_odd))
     resid = resid_in + branch_mix
     scale_ffn = lax.rsqrt(jnp.mean(resid * resid, axis=1, keepdims=True) + EPS)
-    ffn_even, ffn_odd = gather_seq((resid * scale_ffn * gain_ffn).astype(BF))
+    ffn_even, ffn_odd = plain_gather((resid * scale_ffn * gain_ffn).astype(BF))
     scale_all = gather_small(scale_own)
-    up_even, up_odd = gather_seq(upstream_own)
+    up_even, up_odd = plain_gather(upstream_own)
 
     def ffn(normed, upstream):
         ff = dot(normed, ff_w, "td,df->tf")
@@ -612,11 +1302,11 @@
 
     hidden_odd, grad_ff_odd = ffn(ffn_odd, up_odd)
     hidden_even, grad_ff_even = ffn(ffn_even, up_even)
-    grad_normed_ffn = scatter_seq(
+    grad_normed_ffn = plain_scatter(
         dot(grad_ff_even, ff_w, "tf,df->td").astype(BF),
         dot(grad_ff_odd, ff_w, "tf,df->td").astype(BF),
     )
-    branch_ffn = scatter_seq(
+    branch_ffn = plain_scatter(
         dot(hidden_even, down_w, "tf,fd->td").astype(BF),
         dot(hidden_odd, down_w, "tf,fd->td").astype(BF),
     )
@@ -632,12 +1322,12 @@
     grad_branch_own = grad_resid.astype(BF)
     overlap = jnp.sum(grad_branch_own.astype(F32) * branch_mix, axis=1)
     term_all = gather_small((scale_out[:, 0] ** 2 * overlap / width)[None])
-    branch_even, branch_odd = gather_seq(grad_branch_own)
+    branch_even, branch_odd = plain_gather(grad_branch_own)
     grad_gated_even = blocks(dot(branch_even, out_w, "td,cd->tc"))
     grad_gated_odd = blocks(dot(branch_odd, out_w, "td,cd->tc"))
 
     shape_one = (groups, seqs, seq_dev, 1)
-    grad_even, grad_odd, sum_bias, sum_theta, sum_gain = recur_backward(
+    grad_even, grad_odd, scaled_even, scaled_odd, sum_bias, sum_theta, sum_gain = recur_backward(
         place_one,
         floor,
         pre_even,
@@ -654,7 +1344,7 @@
     )
     grad_even = grad_even.reshape(half * rows, 5 * chan)
     grad_odd = grad_odd.reshape(half * rows, 5 * chan)
-    grad_normed_in = scatter_seq(
+    grad_normed_in = plain_scatter(
         dot(grad_even, rec_w, "tc,dc->td").astype(BF),
         dot(grad_odd, rec_w, "tc,dc->td").astype(BF),
     )
@@ -672,7 +1362,7 @@
     def to_owner(grad):
         run = grad.shape[0] // devices
         part = grad.astype(BF).reshape(groups, planes, run, -1).transpose(1, 0, 2, 3)
-        part = scatter_shard(part.reshape(grad.shape)).reshape(groups, run, -1)
+        part = shard_scatter(part.reshape(grad.shape)).reshape(groups, run, -1)
         return lax.all_to_all(part, "seq", split_axis=0, concat_axis=0, tiled=True)
 
     def columns(part, run):
@@ -680,8 +1370,8 @@
         split = part.reshape(source, count, cols // run, run)
         return split.transpose(1, 2, 0, 3).reshape(count, -1).astype(F32)
 
-    scaled_even = (gated_even.astype(F32) * scale_all[:half].reshape(-1, 1)).astype(BF)
-    scaled_odd = (gated_odd.astype(F32) * scale_all[half:].reshape(-1, 1)).astype(BF)
+    scaled_even = scaled_even.reshape(half * rows, 2 * chan)
+    scaled_odd = scaled_odd.reshape(half * rows, 2 * chan)
     ff_grad = to_owner(
         pair_dot((ffn_even, ffn_odd), (grad_ff_even, grad_ff_odd), "td,tf->df")
     )
@@ -697,7 +1387,7 @@
     ]
 
     def rows_to_owner(grad):
-        part = scatter_shard(grad.astype(BF))
+        part = shard_scatter(grad.astype(BF))
         return lax.ppermute(part, ("seq", "wshard"), pairs).astype(F32)
 
     grad_w_down = rows_to_owner(
@@ -706,6 +1396,354 @@
     grad_w_out = rows_to_owner(
         pair_dot((scaled_even, scaled_odd), (branch_even, branch_odd), "tc,td->cd")
     )
+
+    def spread(part):
+        count = part.shape[1] // mix_run
+        zero = jnp.zeros((count, groups, mix_run), F32)
+        zero = lax.dynamic_update_slice(zero, part.reshape(count, 1, mix_run), (0, place, 0))
+        return zero.reshape(-1)
+
+    pieces = [
+        spread(sum_bias),
+        spread(sum_theta),
+        spread(sum_gain),
+        grad_gain_ffn,
+        grad_gain_mix,
+        jnp.stack(
+            [
+                jnp.sum(resid_in * resid_in),
+                jnp.sum(branch_mix * branch_mix),
+                jnp.sum(branch_ffn * branch_ffn),
+            ]
+        ),
+    ]
+    sums = sum_all(jnp.concatenate(pieces))
+    cuts = []
+    offset = 0
+    for piece in pieces:
+        cuts.append(sums[offset : offset + piece.shape[0]])
+        offset += piece.shape[0]
+    grad_bias, grad_theta, grad_gain_out, grad_gain_ffn, grad_gain_mix, squares = cuts
+    rms_values = jnp.sqrt(squares / (rows * width * devices))
+    return (
+        result.reshape(seqs, seq_dev, width),
+        grad_tokens.reshape(seqs, seq_dev, width),
+        grad_gain_mix,
+        grad_w_in,
+        grad_w_forget,
+        grad_bias,
+        grad_theta,
+        grad_w_gate,
+        grad_gain_out,
+        grad_w_out,
+        grad_gain_ffn,
+        grad_w_ffgate,
+        grad_w_ffup,
+        grad_w_down,
+        rms_values,
+    )
+
+
+def body(
+    tokens,
+    starts,
+    layer_index,
+    gain_mix,
+    w_in,
+    w_forget,
+    bias_forget,
+    theta,
+    w_gate_out,
+    gain_out,
+    w_out,
+    gain_ffn,
+    w_ffgate,
+    w_ffup,
+    w_down,
+    out_grad,
+):
+    seqs, seq_dev, width = tokens.shape
+    rows = seqs * seq_dev
+    groups = lax.axis_size("seq")
+    planes = lax.axis_size("wshard")
+    half = groups // 2
+    devices = groups * planes
+    mix_run = w_out.shape[0] // groups
+    ffn_run = w_down.shape[0] // groups
+    chan = mix_run * planes // 2
+    shares = (ffn_run * 6 // 11, ffn_run - ffn_run * 6 // 11)
+    if not (
+        groups == 8
+        and seqs == 2
+        and chan % LANES == 0
+        and all(2 * planes * share % LANES == 0 and share % 16 == 0 for share in shares)
+    ):
+        return plain_body(
+            tokens,
+            starts,
+            layer_index,
+            gain_mix,
+            w_in,
+            w_forget,
+            bias_forget,
+            theta,
+            w_gate_out,
+            gain_out,
+            w_out,
+            gain_ffn,
+            w_ffgate,
+            w_ffup,
+            w_down,
+            out_grad,
+        )
+    place = lax.axis_index("seq")
+    floor = layer_index.astype(F32) / LAYERS
+    place_one = place.reshape(1)
+
+    first_bit, second_bit = chip_bits()
+
+    def own_columns(array, run, first, count):
+        blocks = array.shape[1] // (run * groups)
+        column = lax.broadcasted_iota(jnp.int32, (array.shape[1], blocks * count), 0)
+        index = lax.broadcasted_iota(jnp.int32, (array.shape[1], blocks * count), 1)
+        block = index // count
+        wanted = block * (run * groups) + place * run + first + (index - block * count)
+        return dot(array, (column == wanted).astype(BF), "rc,cj->rj").astype(BF)
+
+    def own_parts(vector):
+        count = vector.shape[0] // (mix_run * groups)
+        split = vector.reshape(count, groups, mix_run)
+        return lax.dynamic_slice_in_dim(split, place, 1, 1).reshape(1, count * mix_run)
+
+    def own_rows(array, first, count):
+        run = array.shape[0] // groups
+        return lax.dynamic_slice_in_dim(array, place * run + first, count, 0)
+
+    rec_own = jnp.concatenate(
+        [own_columns(array, mix_run, 0, mix_run) for array in (w_in, w_forget, w_gate_out)], axis=1
+    )
+    packs = [pack([rec_own[None], own_rows(w_out, 0, mix_run)[None]])]
+    first = 0
+    for share in shares:
+        ff_own = jnp.concatenate(
+            [own_columns(array, ffn_run, first, share) for array in (w_ffgate, w_ffup)], axis=1
+        )
+        packs.append(pack([ff_own[None], own_rows(w_down, first, share)[None]]))
+        first += share
+    rec_packed = gather_packed(packs[0])
+    packed = [gather_packed(item) for item in packs[1:]]
+
+    resid_in = after(tokens, packs[0]).reshape(rows, width).astype(F32)
+    scale_in = lax.rsqrt(jnp.mean(resid_in * resid_in, axis=1, keepdims=True) + EPS)
+    normed_own = (resid_in * scale_in * gain_mix).astype(BF)
+    normed_stage = gather_first(normed_own)
+    normed_far = gather_far(normed_own, normed_stage)
+    normed_even = (normed_own, *normed_stage, *normed_far)
+    normed_odd = cross(normed_even)
+    upstream_own = out_grad.reshape(rows, width)
+    up_gate = after(upstream_own, normed_far)
+    up_stage = gather_first(up_gate)
+    up_far = gather_far(up_gate, up_stage)
+    rec_packed, up_stage, _ = tied(rec_packed, up_stage, packs[1:])
+
+    slots = lax.broadcasted_iota(jnp.int32, (groups, groups), 0)
+    sources = lax.broadcasted_iota(jnp.int32, (groups, groups), 1)
+    keys = jnp.where(slots < half, 2 * slots, 2 * (slots - half) + 1)
+    chosen = ((place ^ keys) == sources).astype(F32)
+    marks = starts.astype(F32).reshape(seqs, groups, seq_dev).transpose(1, 0, 2)
+    flags = jnp.sum(chosen[:, :, None, None] * marks[None], axis=1)[..., None]
+    bias_own = own_parts(bias_forget)
+    theta_own = own_parts(theta)
+    gain_own = own_parts(gain_out)
+
+    pre_even, pre_odd, state, square, *mixes = mix_forward(
+        place_one,
+        floor,
+        normed_even,
+        normed_odd,
+        rec_packed,
+        flags,
+        bias_own,
+        theta_own,
+        gain_own,
+    )
+    mixes = tuple(item.reshape(rows, width) for item in mixes)
+    mix_even, mix_odd = mixes[:half], mixes[half:]
+    mix_odd, up_far = tied(mix_odd, up_far)
+    up_even = (up_gate, *up_stage, *up_far)
+    square = shrink(square.reshape(groups, rows), 1)
+    mix_crossed = cross(mix_odd)
+    mix_sums = joints(mix_even, mix_crossed)
+    square_next = shrink(square, second_bit)
+    mix_stage, square_next = tied(scatter_first(mix_sums), square_next)
+    up_odd = cross(up_even)
+    square_own = shrink(square_next, first_bit)
+    scale_own = lax.rsqrt(square_own / width + EPS)
+    scale_out = scale_own.reshape(rows, 1)
+    branch_mix = scale_out * scatter_last(mix_even, mix_crossed, mix_sums, mix_stage)
+    resid = resid_in + branch_mix
+    scale_ffn = lax.rsqrt(jnp.mean(resid * resid, axis=1, keepdims=True) + EPS)
+    ffn_own = (resid * scale_ffn * gain_ffn).astype(BF)
+    ffn_stage = gather_first(ffn_own)
+    ffn_far = gather_far(ffn_own, ffn_stage)
+    ffn_even = (ffn_own, *ffn_stage, *ffn_far)
+    ffn_odd = cross(ffn_even)
+    scale_all = gather_small(scale_own)
+
+    ff_even, ff_odd, ff_grads = [], [], []
+
+    def share_grads(index):
+        (hidden_e, grad_e), (hidden_o, grad_o) = ff_even[index], ff_odd[index]
+        return grads_call(
+            groups,
+            planes,
+            (ffn_even, ffn_odd),
+            (grad_e, grad_o),
+            (hidden_e, hidden_o),
+            (up_even, up_odd),
+        )
+
+    cols = [2 * planes * share for share in shares]
+    hidden, grad, back_odd = ffn_call(
+        ffn_odd, up_odd, packed[0], cols[0], None, False
+    )
+    ff_odd.append((hidden, grad))
+    hidden, grad, back_even = ffn_call(
+        ffn_even, up_even, packed[0], cols[0], None, False
+    )
+    ff_even.append((hidden, grad))
+    ff_grads.append(share_grads(0))
+    packed[1], ff_grads[0], back_even, scale_all = tied(
+        packed[1], ff_grads[0], back_even, scale_all
+    )
+    hidden, grad, *back_odd = ffn_call(
+        ffn_odd, up_odd, packed[1], cols[1], back_odd, True
+    )
+    ff_odd.append((hidden, grad))
+    hidden, grad, *back_even = ffn_call(
+        ffn_even, up_even, packed[1], cols[1], back_even, True
+    )
+    ff_even.append((hidden, grad))
+    back_crossed = cross(back_odd)
+    back_sums = joints(back_even, back_crossed)
+    back_stage = scatter_first(back_sums)
+    ff_even[1] = (ff_even[1][0], after(ff_even[1][1], back_sums))
+    ff_grads.append(share_grads(1))
+    back_stage, ff_grads[1] = tied(back_stage, ff_grads[1])
+    grad_normed_ffn = scatter_last(back_even, back_crossed, back_sums, back_stage)
+
+    scaled_ffn = grad_normed_ffn * gain_ffn
+    grad_resid = (
+        upstream_own.astype(F32)
+        + scale_ffn * scaled_ffn
+        - resid * scale_ffn**3 * jnp.mean(scaled_ffn * resid, axis=1, keepdims=True)
+    )
+    grad_gain_ffn = jnp.sum(grad_normed_ffn * resid * scale_ffn, axis=0)
+    grad_branch_own = grad_resid.astype(BF)
+    overlap = jnp.sum(grad_branch_own.astype(F32) * branch_mix, axis=1)
+    term_own = (scale_out[:, 0] ** 2 * overlap / width)[None]
+    branch_stage = gather_first(grad_branch_own)
+    term_near = grow(grow(term_own, 1), first_bit)
+    result_even, result_odd = (
+        result_call(
+                [after(share[0][0], grad_branch_own), share[1][0]],
+            packed,
+            width,
+        )
+        for share in (ff_even, ff_odd)
+    )
+    branch_stage, result_even, result_odd, term_near = tied(
+        branch_stage, tuple(result_even), tuple(result_odd), term_near
+    )
+    branch_far = gather_far(grad_branch_own, branch_stage)
+    result_crossed = cross(result_odd)
+    result_sums = joints(result_even, result_crossed)
+    term_all = grow(term_near, second_bit)
+    branch_far, result_sums, term_all = tied(branch_far, result_sums, term_all)
+    term_all = slot_rows(term_all)
+    branch_even = (grad_branch_own, *branch_stage, *branch_far)
+    branch_odd = cross(branch_even)
+    result_stage = scatter_first(result_sums)
+
+    pairs = [(s * planes + w, w * groups + s) for s in range(groups) for w in range(planes)]
+
+    def owned(grads, count):
+        part = scatter_packed(grads)
+        lines = count * width // (planes * LANES)
+        tiles = part[:lines].reshape(groups, -1, LANES)
+        tiles = lax.all_to_all(tiles, "seq", split_axis=0, concat_axis=0, tiled=True)
+        tiles = tiles.reshape(groups, count // LANES, -1, LANES)
+        moved = lax.ppermute(part[lines:], ("seq", "wshard"), pairs)
+        return tiles, moved.reshape(width // LANES, -1, LANES)
+
+    first_tiles, first_lines = owned(ff_grads[0], cols[0])
+
+    shape_one = (groups, seqs, seq_dev, 1)
+    (
+        grad_even,
+        grad_odd,
+        scaled_even,
+        scaled_odd,
+        sum_bias,
+        sum_theta,
+        sum_gain,
+        *backs,
+    ) = mix_backward(
+        place_one,
+        floor,
+        rec_packed,
+        pre_even,
+        pre_odd,
+        flags,
+        bias_own,
+        theta_own,
+        gain_own,
+        state,
+        scale_all.reshape(shape_one),
+        term_all.reshape(shape_one),
+        branch_even,
+        branch_odd,
+    )
+    grad_even = grad_even.reshape(half * rows, 5 * chan)
+    grad_odd = grad_odd.reshape(half * rows, 5 * chan)
+    scaled_even = scaled_even.reshape(half * rows, 2 * chan)
+    scaled_odd = scaled_odd.reshape(half * rows, 2 * chan)
+    backs = tuple(item.reshape(rows, width) for item in backs)
+    grad_even, result_stage, first_tiles = tied(grad_even, result_stage, first_tiles)
+    rec_grads = grads_call(
+        groups,
+        planes,
+        (normed_even, normed_odd),
+        (grad_even, grad_odd),
+        (scaled_even, scaled_odd),
+        (branch_even, branch_odd),
+    )
+    back_even, back_odd = backs[:half], backs[half:]
+    back_crossed = cross(back_odd)
+    back_crossed, rec_grads = tied(back_crossed, rec_grads)
+    branch_ffn = scatter_last(result_even, result_crossed, result_sums, result_stage)
+    result = (resid + branch_ffn).astype(BF)
+    back_sums = joints(back_even, back_crossed)
+    back_stage = tied(*scatter_first(back_sums))
+    grad_normed_in = scatter_last(back_even, back_crossed, back_sums, back_stage)
+    scaled_in = grad_normed_in * gain_mix
+    grad_tokens = (
+        grad_resid
+        + scale_in * scaled_in
+        - resid_in * scale_in**3 * jnp.mean(scaled_in * resid_in, axis=1, keepdims=True)
+    ).astype(BF)
+    grad_gain_mix = jnp.sum(grad_normed_in * resid_in * scale_in, axis=0)
+
+    hidden_all = w_ffgate.shape[1]
+    rec_widths = (w_in.shape[1], w_forget.shape[1], w_gate_out.shape[1])
+    second_tiles, second_lines = owned(ff_grads[1], cols[1])
+    grad_w_ffgate, grad_w_ffup = assemble_tiles(
+        [first_tiles, second_tiles], shares, (hidden_all, hidden_all)
+    )
+    grad_w_down = assemble_rows([first_lines, second_lines])
+    rec_tiles, rec_lines = owned(rec_grads, 5 * chan)
+    grad_w_in, grad_w_forget, grad_w_gate = assemble_tiles([rec_tiles], (mix_run,), rec_widths)
+    grad_w_out = assemble_rows([rec_lines])
 
     def spread(part):
         count = part.shape[1] // mix_run

time: 718 us -> 634 us (0.88)
  Pallas kernels: 28.3 us -> 204 us
  matrix products: 185 us -> 17.6 us
  waiting for transfers between devices: 268 us -> 186 us
  local copies, waits for them, and re-layouts: 94 us -> 43 us
  other arithmetic: 46.2 us -> 70.4 us
  starting transfers between devices: 73.1 us -> 87.4 us
    pallas_call x2 -> x15, Pallas kernels: 28.3 us -> 204 us  [the longest x4 68 us: ffn_call(): pl.pallas_call(functools.partial(ffn_kernel, base is not None, last), gri...]
    dot_general x29 -> x7, matrix products: 185 us -> 17.6 us  [dot(): return jnp.einsum(form, left, right, preferred_element_type=F32)]
    ppermute x60 -> x88, waiting for transfers between devices: 217 us -> 152 us  [swap(): return lax.ppermute(value, 'seq', [(i, i ^ bit) for i in range(size)])]
    all_gather x4 -> x3, waiting for transfers between devices: 34.2 us -> 0.04 us  [gather_packed(): return lax.all_gather(packed, 'wshard', axis=0, tiled=True)]
    convert_element_type x15 -> x0, local copies, waits for them, and re-layouts: 27.2 us -> none  [columns(): return split.transpose(1, 2, 0, 3).reshape(count, -1).astype(F32)]
    convert_element_type x9 -> x22, other arithmetic: 12.2 us -> 34.1 us  [the longest x12 18.7 us: joints(): sums.append(both.astype(BF))]
    ppermute x2 -> x3, waiting for transfers between devices: 13.3 us -> 29.7 us  [owned(): moved = lax.ppermute(part[lines:], ('seq', 'wshard'), pairs)]
    unnamed x102 -> x152, local copies, waits for them, and re-layouts: 23.4 us -> 8.87 us
  transfers between devices with their start and end apart: 74 -> 102, of which waited for: 32 -> 33; matrix products, arithmetic and copies ran while one was open for 40% -> 19% of each run, Pallas kernels for 4% -> 32%
where the time goes in v3:
time: 634 us; the launch traced here: 625 us
  Pallas kernels  204 us (32%)
  waiting for transfers between devices  186 us (29%)
  starting transfers between devices  87.4 us (14%)
  other arithmetic  70.4 us (11%)
  local copies, waits for them, and re-layouts  43 us (7%)
  matrix products  17.6 us (3%)
  between operations  16.6 us (3%)
    ppermute x88, waiting for transfers between devices, swap(): return lax.ppermute(value, 'seq', [(i, i ^ bit) for i in range(size)])  152 us
    pallas_call x4, Pallas kernels, ffn_call(): pl.pallas_call(functools.partial(ffn_kernel, base is not None, last), gri...  68 us
    ppermute x88, starting transfers between devices, swap(): return lax.ppermute(value, 'seq', [(i, i ^ bit) for i in range(size)])  65.4 us
    pallas_call x3, Pallas kernels, grads_call(): pl.pallas_call(functools.partial(grads_kernel, planes), grid=(groups,), i...  50.2 us
    pallas_call x1, Pallas kernels, mix_backward(): pl.pallas_call(mix_backward_kernel, grid=(seqs,), in_specs=[SCALAR, SCALA...  32.3 us
    ppermute x3, waiting for transfers between devices, owned(): moved = lax.ppermute(part[lines:], ('seq', 'wshard'), pairs)  29.7 us
    pallas_call x1, Pallas kernels, mix_forward(): pl.pallas_call(mix_forward_kernel, grid=(seqs,), in_specs=[SCALAR, SCALAR...  27.7 us
    pallas_call x2, Pallas kernels, result_call(): pl.pallas_call(functools.partial(result_kernel, firsts), grid=(slots,), i...  20.2 us
  transfers between devices with their start and end apart: 102, of which 33 were waited for; matrix products, arithmetic and copies ran while one was open for 19% of the time, Pallas kernels for 32%

profile of v3, /device:TPU:4, one launch (start us, length us, event | category | flops | bytes accessed | tf_op | source)
XLA Modules:
  0.0 624.8 jit_solution(11116096117312150928)
XLA Ops:
  20.6 5.5 fusion.50
  30.5 12.0 %collective-permute-done.refs_8_.refs_1_ = bf16[256,2048]{1,0:T(8,128)(2,1)} collective-permute-done((bf16[256,2048]{1,0:T(8,128)(2,1)}, bf16[256,2048]{1,0:T(8,128)(2,1)}, u32[]{:S(2)}, u32[]{:S(2)}) %collective-permute-start) | collective-permute-done | bytes 1048608 | tf_op jit(solution)/shard_map/ppermute | solution.py:22
  47.0 4.8 fusion.56
  51.9 4.9 collective-permute-done.1.refs_10_.refs_3_
  68.1 14.2 %collective-permute-done.4.refs_7_.refs_11_ = bf16[256,2048]{1,0:T(8,128)(2,1)S(1)} collective-permute-done((bf16[256,2048]{1,0:T(8,128)(2,1)}, bf16[256,2048]{1,0:T(8,128)(2,1)S(1)}, u32[]{:S(2)}, u32[]{:S(2)}) %collective-permute-start.4) | collective-permute-done | bytes 1048608 | tf_op jit(solution)/shard_map/ppermute | solution.py:22
  98.4 27.7 %mix_forward.1 = (f32[4,2,128,640]{3,2,1,0:T(8,128)}, f32[4,2,128,640]{3,2,1,0:T(8,128)}, f32[8,2,128,256]{3,2,1,0:T(8,128)}, f32[8,2,128,1]{3,2,1,0:T(8,128)}, ...) custom-call(s32[1]{0:T(128)} %bitcast.9.refs_0_, ...), custom_call_target="tpu_custom_call" | custom-call | flops 1024 | bytes 1024 | tf_op jit(solution)/shard_map/mix_forward/pallas_call | solution.py:950
  142.1 14.9 %collective-permute-done.21 = f32[2,256]{1,0:T(2,128)S(1)} collective-permute-done((f32[2,256]{1,0:T(2,128)S(1)}, f32[2,256]{1,0:T(2,128)S(1)}, u32[]{:S(2)}, u32[]{:S(2)}) %collective-permute-start.21) | collective-permute-done | bytes 2080 | tf_op jit(solution)/shard_map/ppermute | solution.py:22
  166.1 8.2 %collective-permute-done.22 = f32[1,256]{1,0:T(1,128)S(1)} collective-permute-done((f32[1,256]{1,0:T(1,128)S(1)}, f32[1,256]{1,0:T(1,128)S(1)}, u32[]{:S(2)}, u32[]{:S(2)}) %collective-permute-start.22) | collective-permute-done | bytes 1056 | tf_op jit(solution)/shard_map/ppermute | solution.py:22
  185.3 18.1 %collective-permute-done.41 = f32[2,256]{1,0:T(2,128)S(1)} collective-permute-done((f32[2,256]{1,0:T(2,128)S(1)}, f32[2,256]{1,0:T(2,128)S(1)}, u32[]{:S(2)}, u32[]{:S(2)}) %collective-permute-start.41) | collective-permute-done | bytes 2080 | tf_op jit(solution)/shard_map/ppermute | solution.py:22
  210.9 11.4 %collective-permute-done.28.refs_4_.refs_3_ = bf16[128,2048]{1,0:T(8,128)(2,1)} collective-permute-done((bf16[128,2048]{1,0:T(8,128)(2,1)S(1)}, bf16[128,2048]{1,0:T(8,128)(2,1)}, u32[]{:S(2)}, u32[]{:S(2)}) %collective-permute-start.28) | collective-permute-done | bytes 524320 | tf_op jit(solution)/shard_map/ppermute | solution.py:22
  224.0 16.7 %ffn.4 = (bf16[1024,384]{1,0:T(8,128)(2,1)}, bf16[1024,768]{1,0:T(8,128)(2,1)}, f32[1024,2048]{1,0:T(8,128)}) custom-call(bf16[4,4608,128]{2,1,0:T(8,128)(2,1)} %all-gather.8.cloned.1.call-done.refs_0_.refs_2_, bf16[256,2048]{1,0:T(8,128)(2,1)} %copy-done.10, bf16[256,2048]{1,0:T(8,128)(2,1)} %collective-permute-done.26.refs_2_.refs_1_, ...), custom_call_target="tpu_custom_call" | custom-call | flops 1024 | bytes 1024 | tf_op jit(solution)/shard_map/ffn/pallas_call | solution.py:718
  240.7 16.6 %ffn.5 = (bf16[1024,384]{1,0:T(8,128)(2,1)}, bf16[1024,768]{1,0:T(8,128)(2,1)}, f32[1024,2048]{1,0:T(8,128)}) custom-call(bf16[4,4608,128]{2,1,0:T(8,128)(2,1)} %all-gather.8.cloned.1.call-done.refs_0_.refs_2_, bf16[256,2048]{1,0:T(8,128)(2,1)} %collective-permute-done.30.refs_1_.refs_5_, bf16[256,2048]{1,0:T(8,128)(2,1)} %collective-permute-done.31.refs_2_.refs_6_, ...), custom_call_target="tpu_custom_call" | custom-call | flops 1024 | bytes 1024 | tf_op jit(solution)/shard_map/ffn/pallas_call | solution.py:718
  257.3 17.4 %weight_grads.3 = bf16[4,4608,128]{2,1,0:T(8,128)(2,1)} custom-call(bf16[256,2048]{1,0:T(8,128)(2,1)} %copy-done.10, bf16[256,2048]{1,0:T(8,128)(2,1)} %collective-permute-done.26.refs_2_.refs_1_, bf16[256,2048]{1,0:T(8,128)(2,1)} %collective-permute-done.27.refs_3_.refs_2_, bf16[128,2048]{1,0:T(8,128)(2,1)} %collective-permute-done.28.refs_4_.refs_3_, ...), custom_call_target="tpu_custom_call" | custom-call | flops 9663676416 | bytes 1024 | tf_op jit(solution)/shard_map/weight_grads/pallas_call | solution.py:792
  275.0 17.4 %ffn.7 = (bf16[1024,320]{1,0:T(8,128)(2,1)}, bf16[1024,640]{1,0:T(8,128)(2,1)}, bf16[256,2048]{1,0:T(8,128)(2,1)}, bf16[256,2048]{1,0:T(8,128)(2,1)}, bf16[256,2...) custom-call(bf16[4,3840,128]{2,1,0:T(8,128)(2,1)} %all-gather.6.cloned.1.call-done.refs_0_.refs_3_, ...), custom_call_target="tpu_custom_call" | custom-call | flops 1024 | bytes 1024 | tf_op jit(solution)/shard_map/ffn/pallas_call | solution.py:718
  293.5 17.4 %ffn.6 = (bf16[1024,320]{1,0:T(8,128)(2,1)}, bf16[1024,640]{1,0:T(8,128)(2,1)}, bf16[256,2048]{1,0:T(8,128)(2,1)}, bf16[256,2048]{1,0:T(8,128)(2,1)}, bf16[256,2...) custom-call(bf16[4,3840,128]{2,1,0:T(8,128)(2,1)} %all-gather.6.cloned.1.call-done.refs_0_.refs_3_, ...), custom_call_target="tpu_custom_call" | custom-call | flops 1024 | bytes 1024 | tf_op jit(solution)/shard_map/ffn/pallas_call | solution.py:718
  319.3 16.8 %weight_grads.4 = bf16[4,3840,128]{2,1,0:T(8,128)(2,1)} custom-call(bf16[256,2048]{1,0:T(8,128)(2,1)} %copy-done.10, bf16[256,2048]{1,0:T(8,128)(2,1)} %collective-permute-done.26.refs_2_.refs_1_, bf16[256,2048]{1,0:T(8,128)(2,1)} %collective-permute-done.27.refs_3_.refs_2_, bf16[128,2048]{1,0:T(8,128)(2,1)} %collective-permute-done.28.refs_4_.refs_3_, ...), custom_call_target="tpu_custom_call" | custom-call | flops 8053063680 | bytes 1024 | tf_op jit(solution)/shard_map/weight_grads/pallas_call | solution.py:792
  336.1 5.8 collective-permute-done.45
  346.5 10.0 %collective-permute-done.51 = bf16[128,2048]{1,0:T(8,128)(2,1)S(1)} collective-permute-done((bf16[128,2048]{1,0:T(8,128)(2,1)S(1)}, bf16[128,2048]{1,0:T(8,128)(2,1)S(1)}, u32[]{:S(2)}, u32[]{:S(2)}) %collective-permute-start.51) | collective-permute-done | bytes 524320 | tf_op jit(solution)/shard_map/ppermute | solution.py:22
  361.3 5.9 multiply_reduce_fusion.1
  368.8 10.5 %ffn_result.3 = (bf16[256,2048]{1,0:T(8,128)(2,1)S(1)}, bf16[256,2048]{1,0:T(8,128)(2,1)S(1)}, bf16[256,2048]{1,0:T(8,128)(2,1)S(1)}, bf16[256,2048]{1,0:T(8,128)(2,1)S(1)}) custom-call(bf16[1024,384]{1,0:T(8,128)(2,1)S(1)} %copy-done.3, bf16[1024,320]{1,0:T(8,128)(2,1)S(1)} %copy-done.4, bf16[4,4608,128]{2,1,0:T(8,128)(2,1)} %all-gather.8.cloned.1.call-done.refs_0_.refs_2_, ...), custom_call_target="tpu_custom_call" | custom-call | flops 2952790016 | bytes 1024 | tf_op jit(solution)/shard_map/ffn_result/pallas_call | solution.py:833
  380.4 9.7 %ffn_result.2 = (bf16[256,2048]{1,0:T(8,128)(2,1)S(1)}, bf16[256,2048]{1,0:T(8,128)(2,1)S(1)}, bf16[256,2048]{1,0:T(8,128)(2,1)S(1)}, bf16[256,2048]{1,0:T(8,128)(2,1)S(1)}) custom-call(bf16[1024,384]{1,0:T(8,128)(2,1)S(1)} %copy-done.2, bf16[1024,320]{1,0:T(8,128)(2,1)S(1)} %copy-done.5, bf16[4,4608,128]{2,1,0:T(8,128)(2,1)} %all-gather.8.cloned.1.call-done.refs_0_.refs_2_, ...), custom_call_target="tpu_custom_call" | custom-call | flops 2952790016 | bytes 1024 | tf_op jit(solution)/shard_map/ffn_result/pallas_call | solution.py:833
  401.5 9.5 %collective-permute-done.58.refs_15_.refs_13_ = bf16[128,2048]{1,0:T(8,128)(2,1)} collective-permute-done((bf16[128,2048]{1,0:T(8,128)(2,1)S(1)}, bf16[128,2048]{1,0:T(8,128)(2,1)}, u32[]{:S(2)}, u32[]{:S(2)}) %collective-permute-start.58) | collective-permute-done | bytes 524320 | tf_op jit(solution)/shard_map/ppermute | solution.py:22
  426.3 32.3 %mix_backward.1 = (bf16[4,2,128,640]{3,2,1,0:T(8,128)(2,1)}, bf16[4,2,128,640]{3,2,1,0:T(8,128)(2,1)}, bf16[4,2,128,256]{3,2,1,0:T(8,128)(2,1)}, bf16[4,2,128,25...) custom-call(s32[1]{0:T(128)} %bitcast.9.refs_0_, ...), custom_call_target="tpu_custom_call" | custom-call | flops 1024 | bytes 1024 | tf_op jit(solution)/shard_map/mix_backward/pallas_call | solution.py:1064
  459.6 16.1 %weight_grads.5 = bf16[4,3584,128]{2,1,0:T(8,128)(2,1)} custom-call(bf16[256,2048]{1,0:T(8,128)(2,1)} %fusion.30.refs_7_.refs_0_, bf16[256,2048]{1,0:T(8,128)(2,1)} %collective-permute-done.refs_8_.refs_1_, bf16[256,2048]{1,0:T(8,128)(2,1)} %collective-permute-done.2.refs_9_.refs_2_, bf16[128,2048]{1,0:T(8,128)(2,1)} %collective-permute-done.1.refs_10_.refs_3_, ...), custom_call_target="tpu_custom_call" | custom-call | flops 7516192768 | bytes 1024 | tf_op jit(solution)/shard_map/weight_grads/pallas_call | solution.py:792
  495.7 11.1 %collective-permute-done.79 = bf16[128,2048]{1,0:T(8,128)(2,1)S(1)} collective-permute-done((bf16[128,2048]{1,0:T(8,128)(2,1)S(1)}, bf16[128,2048]{1,0:T(8,128)(2,1)S(1)}, u32[]{:S(2)}, u32[]{:S(2)}) %collective-permute-start.79) | collective-permute-done | bytes 524320 | tf_op jit(solution)/shard_map/ppermute | solution.py:22
  519.8 5.0 all-to-all-start.2
  534.0 5.0 multiply_reduce_fusion
  551.4 4.7 collective-permute-done.86
  556.7 5.1 collective-permute-start.87
  561.8 6.6 %collective-permute-done.92 = bf16[1280,128]{1,0:T(8,128)(2,1)S(1)} collective-permute-done((bf16[1280,128]{1,0:T(8,128)(2,1)}, bf16[1280,128]{1,0:T(8,128)(2,1)S(1)}, u32[]{:S(2)}, u32[]{:S(2)}) %collective-permute-start.92) | collective-permute-done | bytes 327712 | tf_op jit(solution)/shard_map/ppermute | solution.py:1676
  568.4 8.3 %collective-permute-done.91 = bf16[1536,128]{1,0:T(8,128)(2,1)S(1)} collective-permute-done((bf16[1536,128]{1,0:T(8,128)(2,1)}, bf16[1536,128]{1,0:T(8,128)(2,1)S(1)}, u32[]{:S(2)}, u32[]{:S(2)}) %collective-permute-start.91) | collective-permute-done | bytes 393248 | tf_op jit(solution)/shard_map/ppermute | solution.py:1676
  600.5 14.7 %collective-permute-done.90 = bf16[1024,128]{1,0:T(8,128)(2,1)S(1)} collective-permute-done((bf16[1024,128]{1,0:T(8,128)(2,1)S(1)}, bf16[1024,128]{1,0:T(8,128)(2,1)S(1)}, u32[]{:S(2)}, u32[]{:S(2)}) %collective-permute-start.90) | collective-permute-done | bytes 262176 | tf_op jit(solution)/shard_map/ppermute | solution.py:1676
  (485 shorter events, 224.2 us)
Async XLA Ops:
  7.2 91.2 %all-gather.4.cloned.1.call-start = ((), (), s32[]{:S(2)}) async-start(), calls=%async_computation.6 | async-start | bytes 4587520 | tf_op jit(solution)/shard_map/all_gather | solution.py:179
  14.6 209.3 %all-gather.8.cloned.1.call-start = ((), (), s32[]{:S(2)}) async-start(), calls=%async_computation.8 | async-start | bytes 5898240 | tf_op jit(solution)/shard_map/all_gather | solution.py:179
  17.3 25.2 %collective-permute-start = (bf16[256,2048]{1,0:T(8,128)(2,1)}, bf16[256,2048]{1,0:T(8,128)(2,1)}, u32[]{:S(2)}, u32[]{:S(2)}) collective-permute-start(bf16[256,2048]{1,0:T(8,128)(2,1)} %fusion.30.refs_7_.refs_0_), channel_id=1, source_target_pairs={{0,8},{4,12},{8,0},{12,4},{16,24},{20,28},{24,16},{28,20},{1,9},{5... | collective-permute-start | bytes 3145736 | tf_op jit(solution)/shard_map/ppermute | solution.py:22
  18.8 25.3 %collective-permute-start.2 = (bf16[256,2048]{1,0:T(8,128)(2,1)}, bf16[256,2048]{1,0:T(8,128)(2,1)}, u32[]{:S(2)}, u32[]{:S(2)}) collective-permute-start(bf16[256,2048]{1,0:T(8,128)(2,1)} %fusion.30.refs_7_.refs_0_), channel_id=1, source_target_pairs={{0,16},{4,20},{8,24},{12,28},{16,0},{20,4},{24,8},{28,12},{1,17},{... | collective-permute-start | bytes 3145736 | tf_op jit(solution)/shard_map/ppermute | solution.py:22
  30.2 244.6 %all-gather.6.cloned.1.call-start = ((), (), s32[]{:S(2)}) async-start(), calls=%async_computation.7 | async-start | bytes 4915200 | tf_op jit(solution)/shard_map/all_gather | solution.py:179
  30.4 56.5 %collective-permute-start.6 = (bf16[256,2048]{1,0:T(8,128)(2,1)}, bf16[256,2048]{1,0:T(8,128)(2,1)}, u32[]{:S(2)}, u32[]{:S(2)}) collective-permute-start(bf16[256,2048]{1,0:T(8,128)(2,1)} %fusion.30.refs_7_.refs_0_), channel_id=1, source_target_pairs={{0,4},{4,0},{8,12},{12,8},{16,20},{20,16},{24,28},{28,24},{1,5},{5... | collective-permute-start | bytes 3145736 | tf_op jit(solution)/shard_map/ppermute | solution.py:22
  67.6 30.8 %collective-permute-start.7 = (bf16[256,2048]{1,0:T(8,128)(2,1)}, bf16[256,2048]{1,0:T(8,128)(2,1)}, u32[]{:S(2)}, u32[]{:S(2)}) collective-permute-start(bf16[256,2048]{1,0:T(8,128)(2,1)} %collective-permute-done.refs_8_.refs_1_), channel_id=1, source_target_pairs={{0,4},{4,0},{8,12},{12,8},{16,20},{20,16},{24,28},{28,24},{1,5},{5... | collective-permute-start | bytes 3145736 | tf_op jit(solution)/shard_map/ppermute | solution.py:22
  86.9 39.3 %collective-permute-start.11 = (bf16[128,2048]{1,0:T(8,128)(2,1)}, bf16[128,2048]{1,0:T(8,128)(2,1)}, u32[]{:S(2)}, u32[]{:S(2)}) collective-permute-start(bf16[128,2048]{1,0:T(8,128)(2,1)} %slice.318), channel_id=1, source_target_pairs={{0,16},{4,20},{8,24},{12,28},{16,0},{20,4},{24,8},{28,12},{1,17},{... | collective-permute-start | bytes 1572872 | tf_op jit(solution)/shard_map/ppermute | solution.py:22
  88.4 37.7 %collective-permute-start.12 = (bf16[128,2048]{1,0:T(8,128)(2,1)}, bf16[128,2048]{1,0:T(8,128)(2,1)}, u32[]{:S(2)}, u32[]{:S(2)}) collective-permute-start(bf16[128,2048]{1,0:T(8,128)(2,1)} %slice.319), channel_id=1, source_target_pairs={{0,8},{4,12},{8,0},{12,4},{16,24},{20,28},{24,16},{28,20},{1,9},{5... | collective-permute-start | bytes 1572872 | tf_op jit(solution)/shard_map/ppermute | solution.py:22
  131.4 25.6 %collective-permute-start.19 = (bf16[128,2048]{1,0:T(8,128)(2,1)}, bf16[128,2048]{1,0:T(8,128)(2,1)}, u32[]{:S(2)}, u32[]{:S(2)}) collective-permute-start(bf16[128,2048]{1,0:T(8,128)(2,1)} %fusion.73), channel_id=1, source_target_pairs={{0,16},{4,20},{8,24},{12,28},{16,0},{20,4},{24,8},{28,12},{1,17},{... | collective-permute-start | bytes 1572872 | tf_op jit(solution)/shard_map/ppermute | solution.py:22
  141.6 274.7 %reduce-scatter.4.cloned.1.call-start = ((), (), s32[]{:S(2)}) async-start(), calls=%async_computation.9 | async-start | bytes 5898240 | tf_op jit(solution)/shard_map/reduce_scatter | solution.py:183
  182.4 26.0 %collective-permute-start.36 = (bf16[256,2048]{1,0:T(8,128)(2,1)S(1)}, bf16[256,2048]{1,0:T(8,128)(2,1)S(1)}, u32[]{:S(2)}, u32[]{:S(2)}) collective-permute-start(bf16[256,2048]{1,0:T(8,128)(2,1)S(1)} %copy-done.13), channel_id=1, source_target_pairs={{0,4},{4,0},{8,12},{12,8},{16,20},{20,16},{24,28},{28,24},{1,5},{5... | collective-permute-start | bytes 3145736 | tf_op jit(solution)/shard_map/ppermute | solution.py:22
  183.6 25.0 %collective-permute-start.37 = (bf16[256,2048]{1,0:T(8,128)(2,1)S(1)}, bf16[256,2048]{1,0:T(8,128)(2,1)S(1)}, u32[]{:S(2)}, u32[]{:S(2)}) collective-permute-start(bf16[256,2048]{1,0:T(8,128)(2,1)S(1)} %copy-done.15), channel_id=1, source_target_pairs={{0,4},{4,0},{8,12},{12,8},{16,20},{20,16},{24,28},{28,24},{1,5},{5... | collective-permute-start | bytes 3145736 | tf_op jit(solution)/shard_map/ppermute | solution.py:22
  207.7 32.9 %collective-permute-start.30 = (bf16[256,2048]{1,0:T(8,128)(2,1)S(1)}, bf16[256,2048]{1,0:T(8,128)(2,1)}, u32[]{:S(2)}, u32[]{:S(2)}) collective-permute-start(bf16[256,2048]{1,0:T(8,128)(2,1)S(1)} %multiply_convert_fusion.refs_1_.refs_0_), channel_id=1, source_target_pairs={{0,4},{4,0},{8,12},{12,8},{16,20},{20,16},{24,28},{28,24},{1,5},{5... | collective-permute-start | bytes 3145736 | tf_op jit(solution)/shard_map/ppermute | solution.py:22
  208.4 32.2 %collective-permute-start.31 = (bf16[256,2048]{1,0:T(8,128)(2,1)}, bf16[256,2048]{1,0:T(8,128)(2,1)}, u32[]{:S(2)}, u32[]{:S(2)}) collective-permute-start(bf16[256,2048]{1,0:T(8,128)(2,1)} %collective-permute-done.26.refs_2_.refs_1_), channel_id=1, source_target_pairs={{0,4},{4,0},{8,12},{12,8},{16,20},{20,16},{24,28},{28,24},{1,5},{5... | collective-permute-start | bytes 3145736 | tf_op jit(solution)/shard_map/ppermute | solution.py:22
  208.6 32.1 %collective-permute-start.32 = (bf16[256,2048]{1,0:T(8,128)(2,1)}, bf16[256,2048]{1,0:T(8,128)(2,1)}, u32[]{:S(2)}, u32[]{:S(2)}) collective-permute-start(bf16[256,2048]{1,0:T(8,128)(2,1)} %collective-permute-done.27.refs_3_.refs_2_), channel_id=1, source_target_pairs={{0,4},{4,0},{8,12},{12,8},{16,20},{20,16},{24,28},{28,24},{1,5},{5... | collective-permute-start | bytes 3145736 | tf_op jit(solution)/shard_map/ppermute | solution.py:22
  274.8 243.0 %reduce-scatter.8.cloned.1.call-start = ((), (), s32[]{:S(2)}) async-start(), calls=%async_computation.11 | async-start | bytes 4915200 | tf_op jit(solution)/shard_map/reduce_scatter | solution.py:183
  293.4 53.1 %collective-permute-start.43 = (bf16[256,2048]{1,0:T(8,128)(2,1)}, bf16[256,2048]{1,0:T(8,128)(2,1)S(1)}, u32[]{:S(2)}, u32[]{:S(2)}) collective-permute-start(bf16[256,2048]{1,0:T(8,128)(2,1)} %get-tuple-element.170), channel_id=1, source_target_pairs={{0,4},{4,0},{8,12},{12,8},{16,20},{20,16},{24,28},{28,24},{1,5},{5... | collective-permute-start | bytes 3145736 | tf_op jit(solution)/shard_map/ppermute | solution.py:22
  412.2 46.5 %collective-permute-start.69 = (bf16[128,2048]{1,0:T(8,128)(2,1)}, bf16[128,2048]{1,0:T(8,128)(2,1)}, u32[]{:S(2)}, u32[]{:S(2)}) collective-permute-start(bf16[128,2048]{1,0:T(8,128)(2,1)} %get-tuple-element.215), channel_id=1, source_target_pairs={{0,8},{4,12},{8,0},{12,4},{16,24},{20,28},{24,16},{28,20},{1,9},{5... | collective-permute-start | bytes 1572872 | tf_op jit(solution)/shard_map/ppermute | solution.py:22
  413.1 46.0 %collective-permute-start.70 = (bf16[128,2048]{1,0:T(8,128)(2,1)}, bf16[128,2048]{1,0:T(8,128)(2,1)}, u32[]{:S(2)}, u32[]{:S(2)}) collective-permute-start(bf16[128,2048]{1,0:T(8,128)(2,1)} %get-tuple-element.216), channel_id=1, source_target_pairs={{0,16},{4,20},{8,24},{12,28},{16,0},{20,4},{24,8},{28,12},{1,17},{... | collective-permute-start | bytes 1572872 | tf_op jit(solution)/shard_map/ppermute | solution.py:22
  415.7 43.5 %collective-permute-start.71 = (bf16[128,2048]{1,0:T(8,128)(2,1)}, bf16[128,2048]{1,0:T(8,128)(2,1)}, u32[]{:S(2)}, u32[]{:S(2)}) collective-permute-start(bf16[128,2048]{1,0:T(8,128)(2,1)} %get-tuple-element.217), channel_id=1, source_target_pairs={{0,8},{4,12},{8,0},{12,4},{16,24},{20,28},{24,16},{28,20},{1,9},{5... | collective-permute-start | bytes 1572872 | tf_op jit(solution)/shard_map/ppermute | solution.py:22
  418.4 41.3 %all-to-all-start = ((bf16[8,384,128]{2,1,0:T(8,128)(2,1)}), bf16[8,384,128]{2,1,0:T(8,128)(2,1)S(1)}, u32[]{:S(2)}, u32[]{:S(2)}) async-start(bf16[8,384,128]{2,1,0:T(8,128)(2,1)} %bitcast.204), calls=%async_computation.1 | async-start | bytes 1572864 | tf_op jit(solution)/shard_map/all_to_all | solution.py:1674
  422.8 167.4 %reduce-scatter.6.cloned.1.call-start = ((), (), s32[]{:S(2)}) async-start(), calls=%async_computation.10 | async-start | bytes 4587520 | tf_op jit(solution)/shard_map/reduce_scatter | solution.py:183
  422.8 36.8 %collective-permute-start.72 = (bf16[128,2048]{1,0:T(8,128)(2,1)}, bf16[128,2048]{1,0:T(8,128)(2,1)}, u32[]{:S(2)}, u32[]{:S(2)}) collective-permute-start(bf16[128,2048]{1,0:T(8,128)(2,1)} %get-tuple-element.218), channel_id=1, source_target_pairs={{0,16},{4,20},{8,24},{12,28},{16,0},{20,4},{24,8},{28,12},{1,17},{... | collective-permute-start | bytes 1572872 | tf_op jit(solution)/shard_map/ppermute | solution.py:22
  475.8 52.5 %collective-permute-start.57 = (bf16[256,2048]{1,0:T(8,128)(2,1)S(1)}, bf16[256,2048]{1,0:T(8,128)(2,1)}, u32[]{:S(2)}, u32[]{:S(2)}) collective-permute-start(bf16[256,2048]{1,0:T(8,128)(2,1)S(1)} %get-tuple-element.197), channel_id=1, source_target_pairs={{0,4},{4,0},{8,12},{12,8},{16,20},{20,16},{24,28},{28,24},{1,5},{5... | collective-permute-start | bytes 3145736 | tf_op jit(solution)/shard_map/ppermute | solution.py:22
  492.1 38.4 %collective-permute-start.73 = (bf16[128,2048]{1,0:T(8,128)(2,1)}, bf16[128,2048]{1,0:T(8,128)(2,1)}, u32[]{:S(2)}, u32[]{:S(2)}) collective-permute-start(bf16[128,2048]{1,0:T(8,128)(2,1)} %add_convert_fusion.4), channel_id=1, source_target_pairs={{0,8},{4,12},{8,0},{12,4},{16,24},{20,28},{24,16},{28,20},{1,9},{5... | collective-permute-start | bytes 1572872 | tf_op jit(solution)/shard_map/ppermute | solution.py:22
  495.5 38.5 %collective-permute-start.74 = (bf16[128,2048]{1,0:T(8,128)(2,1)}, bf16[128,2048]{1,0:T(8,128)(2,1)}, u32[]{:S(2)}, u32[]{:S(2)}) collective-permute-start(bf16[128,2048]{1,0:T(8,128)(2,1)} %add_convert_fusion.3), channel_id=1, source_target_pairs={{0,16},{4,20},{8,24},{12,28},{16,0},{20,4},{24,8},{28,12},{1,17},{... | collective-permute-start | bytes 1572872 | tf_op jit(solution)/shard_map/ppermute | solution.py:22
  508.9 30.1 %collective-permute-start.83 = (bf16[128,2048]{1,0:T(8,128)(2,1)}, bf16[128,2048]{1,0:T(8,128)(2,1)}, u32[]{:S(2)}, u32[]{:S(2)}) collective-permute-start(bf16[128,2048]{1,0:T(8,128)(2,1)} %add_convert_fusion.2), channel_id=1, source_target_pairs={{0,8},{4,12},{8,0},{12,4},{16,24},{20,28},{24,16},{28,20},{1,9},{5... | collective-permute-start | bytes 1572872 | tf_op jit(solution)/shard_map/ppermute | solution.py:22
  512.4 26.6 %collective-permute-start.84 = (bf16[128,2048]{1,0:T(8,128)(2,1)}, bf16[128,2048]{1,0:T(8,128)(2,1)}, u32[]{:S(2)}, u32[]{:S(2)}) collective-permute-start(bf16[128,2048]{1,0:T(8,128)(2,1)} %add_convert_fusion.1), channel_id=1, source_target_pairs={{0,16},{4,20},{8,24},{12,28},{16,0},{20,4},{24,8},{28,12},{1,17},{... | collective-permute-start | bytes 1572872 | tf_op jit(solution)/shard_map/ppermute | solution.py:22
  519.8 58.2 %all-to-all-start.2 = ((bf16[8,320,128]{2,1,0:T(8,128)(2,1)}), bf16[8,320,128]{2,1,0:T(8,128)(2,1)S(1)}, u32[]{:S(2)}, u32[]{:S(2)}) async-start(bf16[8,320,128]{2,1,0:T(8,128)(2,1)} %bitcast.208), calls=%async_computation.5 | async-start | bytes 1310720 | tf_op jit(solution)/shard_map/all_to_all | solution.py:1674
  528.3 40.1 %collective-permute-start.92 = (bf16[1280,128]{1,0:T(8,128)(2,1)}, bf16[1280,128]{1,0:T(8,128)(2,1)S(1)}, u32[]{:S(2)}, u32[]{:S(2)}) collective-permute-start(bf16[1280,128]{1,0:T(8,128)(2,1)} %slice.352), channel_id=1, source_target_pairs={{0,0},{1,8},{2,16},{3,24},{4,1},{5,9},{6,17},{7,25},{8,2},{9,10},{... | collective-permute-start | bytes 983048 | tf_op jit(solution)/shard_map/ppermute | solution.py:1676
  530.6 46.2 %collective-permute-start.91 = (bf16[1536,128]{1,0:T(8,128)(2,1)}, bf16[1536,128]{1,0:T(8,128)(2,1)S(1)}, u32[]{:S(2)}, u32[]{:S(2)}) collective-permute-start(bf16[1536,128]{1,0:T(8,128)(2,1)} %slice.351), channel_id=1, source_target_pairs={{0,0},{1,8},{2,16},{3,24},{4,1},{5,9},{6,17},{7,25},{8,2},{9,10},{... | collective-permute-start | bytes 1179656 | tf_op jit(solution)/shard_map/ppermute | solution.py:1676
  (142 other events, 2027.5 us)
Sparse Core Ops, SparseCore 0:
  14.7 73.3 all-gather.3
  90.3 88.0 all-gather.7
  179.9 74.9 all-gather.5
  274.9 86.1 reduce-scatter.3
  363.2 73.2 reduce-scatter.7
  475.9 78.8 reduce-scatter.5

commit v4 on v3

--- a/solution.py
+++ b/solution.py
@@ -92,29 +92,102 @@
     return tuple(swap(piece, 1) for piece in pieces)
 
 
+def scatter_far(even, crossed):
+    half = even.shape[0] // 2
+    bits = chip_bits()
+    return tuple(
+        swap((even[rows].astype(F32) + crossed[rows].astype(F32)).astype(BF), bit)
+        for rows, bit in zip((slice(0, half), slice(half, None)), bits)
+    )
+
+
+def onward_kernel(first_even, first_cross, far_low, second_even, second_cross, far_top, *outs):
+    half = far_low.shape[0]
+    first_out, second_out = outs
+    both = first_even[...].astype(F32) + first_cross[...].astype(F32)
+    first_out[:half, :] = both[:half].astype(BF)
+    first_out[half:, :] = (both[half:] + far_low[...].astype(F32)).astype(BF)
+    both = second_even[...].astype(F32) + second_cross[...].astype(F32)
+    second_out[:half, :] = (both[:half] + far_top[...].astype(F32)).astype(BF)
+    second_out[half:, :] = both[half:].astype(BF)
+
+
+def near_sums(even, crossed, far):
+    rows, width = even[0].shape
+    step = width // 4
+    whole = pl.BlockSpec((rows, step), lambda i: (0, i))
+    part = pl.BlockSpec((rows // 2, step), lambda i: (0, i))
+    return pl.pallas_call(
+        onward_kernel,
+        grid=(width // step,),
+        in_specs=[whole, whole, part] * 2,
+        out_specs=[whole] * 2,
+        out_shape=[jax.ShapeDtypeStruct((rows, width), BF)] * 2,
+        cost_estimate=SMALL,
+        name="onward_sums",
+    )(even[0], crossed[0], far[1], even[1], crossed[1], far[0])
+
+
+def to_neighbours(sums):
+    return tuple(swap(item, bit) for item, bit in zip(sums, chip_bits()))
+
+
+def scatter_near(even, crossed, far):
+    return to_neighbours(near_sums(even, crossed, far))
+
+
+def joint_kernel(*refs):
+    count = len(refs) // 3
+    for index in range(count):
+        both = refs[index][...].astype(F32) + refs[count + index][...].astype(F32)
+        refs[2 * count + index][...] = both.astype(BF)
+
+
+FIRST_SUMS = ((3, 0), (3, 1), (1, 0), (2, 1))
+
+
 def joints(even, crossed):
-    half = even[0].shape[0] // 2
-    sums = []
-    for index in (1, 2, 3):
-        for rows in (slice(0, half), slice(half, None)):
-            both = even[index][rows].astype(F32) + crossed[index][rows].astype(F32)
-            sums.append(both.astype(BF))
-    return tuple(sums)
+    rows, width = even[0].shape
+    half = rows // 2
+    step = width // 4
+
+    def spec(part):
+        return pl.BlockSpec((half, step), lambda i, part=part: (part, i))
+
+    return pl.pallas_call(
+        joint_kernel,
+        grid=(width // step,),
+        in_specs=[spec(part) for _, part in FIRST_SUMS] * 2,
+        out_specs=[spec(0)] * len(FIRST_SUMS),
+        out_shape=[jax.ShapeDtypeStruct((half, width), BF)] * len(FIRST_SUMS),
+        cost_estimate=SMALL,
+        name="chip_sums",
+    )(*[even[index] for index, _ in FIRST_SUMS], *[crossed[index] for index, _ in FIRST_SUMS])
 
 
 def scatter_first(sums):
     first, second = chip_bits()
-    return swap(sums[4], first), swap(sums[5], second), swap(sums[0], first), swap(sums[3], second)
-
-
-def scatter_last(even, crossed, sums, stage):
+    return tuple(swap(item, bit) for item, bit in zip(sums, (first, second, first, second)))
+
+
+def scatter_last(even, crossed, stage):
     first, second = chip_bits()
+    half = even[0].shape[0] // 2
     far_top, far_low, first_top, second_low = stage
-    first_low = swap((sums[1].astype(F32) + far_low.astype(F32)).astype(BF), first)
-    second_top = swap((sums[2].astype(F32) + far_top.astype(F32)).astype(BF), second)
+
+    def onward(index, rows, far):
+        both = even[index][rows].astype(F32) + crossed[index][rows].astype(F32)
+        return (both + far.astype(F32)).astype(BF)
+
+    first_low = swap(onward(1, slice(half, None), far_low), first)
+    second_top = swap(onward(2, slice(0, half), far_top), second)
     first_all = jnp.concatenate([first_top, first_low], axis=0).astype(F32)
     second_all = jnp.concatenate([second_top, second_low], axis=0).astype(F32)
     return even[0].astype(F32) + crossed[0].astype(F32) + first_all + second_all
+
+
+def scatter_sum(even, crossed, near):
+    return (even.astype(F32) + crossed.astype(F32)) + (near[0].astype(F32) + near[1].astype(F32))
 
 
 def tied(*values):
@@ -147,15 +220,24 @@
     return blocks
 
 
-def sum_all(value):
+def sum_seq(value):
     for bit in [1] + chip_bits():
         value = value + swap(value, bit)
+    return value
+
+
+def others(value):
     planes = lax.axis_size("wshard")
-    bit = 1
-    while bit < planes:
-        value = value + lax.ppermute(value, "wshard", [(i, i ^ bit) for i in range(planes)])
-        bit *= 2
-    return value
+    return [
+        lax.ppermute(value, "wshard", [(i, i ^ key) for i in range(planes)])
+        for key in range(1, planes)
+    ]
+
+
+def sum_tree(values):
+    while len(values) > 1:
+        values = [values[i] + values[i + 1] for i in range(0, len(values), 2)]
+    return values[0]
 
 
 LANES = 128
@@ -633,218 +715,252 @@
 SCALAR = pl.BlockSpec(memory_space=pltpu.SMEM)
 
 
-def slot_copies(pieces, held, sems, slot):
-    if slot < 3:
-        return [pltpu.make_async_copy(pieces[slot], held.at[slot], sems.at[slot])]
-    half = held.shape[1] // 2
-    return [
-        pltpu.make_async_copy(
-            pieces[3 + part], held.at[3, part * half : (part + 1) * half], sems.at[3 + part]
-        )
-        for part in range(2)
-    ]
-
-
-def ffn_kernel(based, last, *refs):
-    packed_ref = refs[0]
-    normed, up = refs[1 : 1 + PIECES], refs[1 + PIECES : 1 + 2 * PIECES]
-    rest = list(refs[1 + 2 * PIECES :])
-    base_ref = rest.pop(0) if based else None
-    hidden_ref, grad_ref = rest[:2]
-    backs = rest[2 : 6 if last else 3]
-    ff_s, down_s, normed_s, up_s, normed_sems, up_sems = rest[6 if last else 3 :]
+def block_copies(pieces, held, sems):
+    copies = []
+    index = 0
+    for block, parts in enumerate(pieces):
+        copies.append([])
+        rows = held.shape[1] // len(parts)
+        for part, (ref, offset) in enumerate(parts):
+            source = ref if offset is None else ref.at[offset : offset + rows]
+            target = held.at[block, part * rows : (part + 1) * rows]
+            copies[-1].append(pltpu.make_async_copy(source, target, sems.at[index]))
+            index += 1
+    return copies
+
+
+def ffn_kernel(counts, offsets, last, *refs):
+    refs = list(refs)
+
+    def take(count):
+        taken = refs[:count]
+        del refs[:count]
+        return taken
+
+    (packed_ref,) = take(1)
+    blocks = len(counts)
+    normed = [[(ref, None) for ref in take(count)] for count in counts]
+    up = [[(ref, None) for ref in take(count)] for count in counts]
+    groups = [normed, up]
+    if offsets:
+        groups.append([[(ref, offset)] for ref, offset in zip(take(blocks), offsets)])
+    hidden_ref, grad_ref = take(2)
+    backs = take(blocks if last else 1)
+    ff_s, down_s = take(2)
+    helds = take(len(groups))
+    sems = take(len(groups))
+    copies = [block_copies(*item) for item in zip(groups, helds, sems)]
     hidden = down_s.shape[0]
     step = pl.program_id(0)
-    slots = normed_s.shape[0]
 
     @pl.when(step == 0)
     def _():
-        for slot in range(slots):
-            for copy in slot_copies(normed, normed_s, normed_sems, slot):
-                copy.start()
-            for copy in slot_copies(up, up_s, up_sems, slot):
-                copy.start()
+        for block in range(blocks):
+            for group in copies:
+                for copy in group[block]:
+                    copy.start()
         first = ff_s.shape[0] // packed_ref.shape[0] * (ff_s.shape[1] // LANES)
         unpack_columns(packed_ref, ff_s)
         unpack_rows(packed_ref, first, down_s)
 
-    for slot in range(slots):
-
-        @pl.when(step == slot)
-        def _(slot=slot):
-            for copy in slot_copies(normed, normed_s, normed_sems, slot):
-                copy.wait()
-            for copy in slot_copies(up, up_s, up_sems, slot):
-                copy.wait()
-
-    ff = dot_nn(normed_s[step], ff_s[...])
+    for block in range(blocks):
+
+        @pl.when(step == block)
+        def _(block=block):
+            for group in copies:
+                for copy in group[block]:
+                    copy.wait()
+
+    ff = dot_nn(helds[0][step], ff_s[...])
     gate, value = ff[:, :hidden], ff[:, hidden:]
     sig = jax.nn.sigmoid(gate)
     silu = gate * sig
     hidden_ref[...] = (silu * value).astype(BF)
-    grad = dot_nt(up_s[step], down_s[...])
+    grad = dot_nt(helds[1][step], down_s[...])
     grad_ref[:, :hidden] = (grad * value * sig * (1.0 + gate * (1.0 - sig))).astype(BF)
     grad_ref[:, hidden:] = (grad * silu).astype(BF)
     back = dot_nt(grad_ref[...], ff_s[...])
-    if based:
-        back = back + base_ref[...]
+    if offsets:
+        back = back + helds[2][step]
     if last:
-        for slot in range(slots):
-
-            @pl.when(step == slot)
-            def _(slot=slot):
-                backs[slot][...] = back.astype(BF)
+        for block in range(blocks):
+
+            @pl.when(step == block)
+            def _(block=block):
+                backs[block][...] = back.astype(BF)
     else:
         backs[0][...] = back
 
 
-def ffn_call(normed, upstream, packed, ff_cols, base, last):
-    rows, width = normed[0].shape
-    slots = 4
-    tokens = slots * rows
+def ffn_call(blocks, packed, ff_cols, bases=None, fills=False):
+    rows = sum(piece.shape[0] for piece in blocks[0][0])
+    width = blocks[0][0][0].shape[1]
+    count = len(blocks)
+    tokens = count * rows
     hidden = ff_cols // 2
-    wide = pl.BlockSpec((rows, width), lambda i: (i, 0))
-    whole = pl.BlockSpec((rows, width), lambda i: (0, 0))
-    operands = [packed, *normed, *upstream]
-    in_specs = [
-        pl.BlockSpec(packed.shape, lambda i: (0, 0, 0), pipeline_mode=pl.Buffered(1)),
-    ] + [ANYWHERE] * (2 * PIECES)
-    if base is not None:
-        operands.append(base)
-        in_specs.append(wide)
+    last = bases is not None
+    counts = tuple(len(block[0]) for block in blocks)
+    pieces = sum(counts)
+    operands = [packed]
+    for index in range(2):
+        for block in blocks:
+            operands += block[index]
+    held = pltpu.VMEM((count, rows, width), BF)
+    helds = [held, held]
+    sems = [pltpu.SemaphoreType.DMA((pieces,))] * 2
+    if last:
+        operands += [array for array, _ in bases]
+        helds.append(pltpu.VMEM((count, rows, width), F32))
+        sems.append(pltpu.SemaphoreType.DMA((count,)))
     backs = [jax.ShapeDtypeStruct((tokens, width), F32)]
+    back_specs = [pl.BlockSpec((rows, width), lambda i: (i, 0))]
     if last:
-        backs = [jax.ShapeDtypeStruct((rows, width), BF)] * slots
+        backs = [jax.ShapeDtypeStruct((rows, width), BF)] * count
+        back_specs = [pl.BlockSpec((rows, width), lambda i: (0, 0))] * count
+    offsets = tuple(offset for _, offset in bases) if last else ()
     return pl.pallas_call(
-        functools.partial(ffn_kernel, base is not None, last),
-        grid=(slots,),
-        in_specs=in_specs,
+        functools.partial(ffn_kernel, counts, offsets, last),
+        grid=(count,),
+        in_specs=[pl.BlockSpec(packed.shape, lambda i: (0, 0, 0), pipeline_mode=pl.Buffered(1))]
+        + [ANYWHERE] * (len(operands) - 1),
         out_specs=[
             pl.BlockSpec((rows, hidden), lambda i: (i, 0)),
             pl.BlockSpec((rows, ff_cols), lambda i: (i, 0)),
         ]
-        + ([whole] * slots if last else [wide]),
+        + back_specs,
         out_shape=[
             jax.ShapeDtypeStruct((tokens, hidden), BF),
             jax.ShapeDtypeStruct((tokens, ff_cols), BF),
             *backs,
         ],
-        scratch_shapes=[
-            pltpu.VMEM((width, ff_cols), BF),
-            pltpu.VMEM((hidden, width), BF),
-            pltpu.VMEM((slots, rows, width), BF),
-            pltpu.VMEM((slots, rows, width), BF),
-            pltpu.SemaphoreType.DMA((PIECES,)),
-            pltpu.SemaphoreType.DMA((PIECES,)),
-        ],
-        compiler_params=pltpu.CompilerParams(vmem_limit_bytes=56 * 2**20),
-        cost_estimate=SMALL,
+        scratch_shapes=[pltpu.VMEM((width, ff_cols), BF), pltpu.VMEM((hidden, width), BF)]
+        + helds
+        + sems,
+        compiler_params=pltpu.CompilerParams(vmem_limit_bytes=60 * 2**20),
+        cost_estimate=filler(5 * tokens * width * ff_cols if fills else 1024),
         name="ffn",
     )(*operands)
 
 
-def grads_kernel(planes, *refs):
-    left = refs[: 2 * PIECES]
-    up = refs[2 * PIECES : 4 * PIECES]
-    cols_even, cols_odd, rows_even, rows_odd, out_ref = refs[4 * PIECES :]
+def grads_kernel(planes, counts, turn_ref, *refs):
+    refs = list(refs)
+    out_ref = refs.pop()
+
+    def take(count):
+        taken = refs[:count]
+        del refs[:count]
+        return taken
+
+    groups = [(take(count), take(count), *take(2)) for count in counts]
     step = pl.program_id(0)
     steps = pl.num_programs(0)
-    block = left[0].shape[1]
+    block = groups[0][0][0].shape[1]
     run = block // planes
-    tiles = cols_even.shape[1] // LANES
-    count = rows_even.shape[1] // planes
+    tiles = groups[0][2].shape[1] // LANES
+    count = groups[0][3].shape[1] // planes
 
     def joined(pieces):
         return jnp.concatenate([piece[...] for piece in pieces], axis=0)
 
-    grad = dot_tn(joined(left[:PIECES]), cols_even[...])
-    grad = (grad + dot_tn(joined(left[PIECES:]), cols_odd[...])).astype(BF)
+    grad = sum(dot_tn(joined(left), cols[...]) for left, _, cols, _ in groups).astype(BF)
     for plane in range(planes):
         for tile in range(tiles):
             lines = pl.ds(pl.multiple_of((step * tiles + tile) * run, run), run)
             out_ref[plane, lines, :] = grad[
                 plane * run : (plane + 1) * run, tile * LANES : (tile + 1) * LANES
             ]
-    grad = dot_tn(rows_even[...], joined(up[:PIECES]))
-    grad = (grad + dot_tn(rows_odd[...], joined(up[PIECES:]))).astype(BF)
+    grad = sum(dot_tn(rows[...], joined(up)) for _, up, _, rows in groups).astype(BF)
     first = block // planes * tiles * steps
-    for plane in range(planes):
+    for index in range(planes):
+        plane = lax.rem(turn_ref[0] + index, planes)
         for tile in range(block // LANES):
             base = first + (step * (block // LANES) + tile) * count
             lines = pl.ds(pl.multiple_of(base, 16), count)
             out_ref[plane, lines, :] = grad[
-                plane * count : (plane + 1) * count, tile * LANES : (tile + 1) * LANES
+                index * count : (index + 1) * count, tile * LANES : (tile + 1) * LANES
             ]
 
 
-def grads_call(groups, planes, left, cols, rows, up):
-    width = left[0][0].shape[1]
-    tokens = cols[0].shape[0]
-    block = width // groups
-    col_count = cols[0].shape[1]
-    row_count = rows[0].shape[1]
+def grads_call(steps, planes, turn, groups):
+    width = groups[0][0][0].shape[1]
+    block = width // steps
+    col_count = groups[0][2].shape[1]
+    row_count = groups[0][3].shape[1]
+    tokens = sum(group[2].shape[0] for group in groups)
     lines = (col_count * width + row_count * width) // (planes * LANES)
-    pieces = [*left[0], *left[1], *up[0], *up[1]]
-
-    def whole(array):
-        return pl.BlockSpec(array.shape, lambda i: (0, 0), pipeline_mode=pl.Buffered(1))
-
+    operands, specs = [turn], [SCALAR]
+    for left, up, cols, rows in groups:
+        for piece in (*left, *up):
+            operands.append(piece)
+            specs.append(pl.BlockSpec((piece.shape[0], block), lambda i: (0, i)))
+        for array in (cols, rows):
+            operands.append(array)
+            specs.append(
+                pl.BlockSpec(array.shape, lambda i: (0, 0), pipeline_mode=pl.Buffered(1))
+            )
     return pl.pallas_call(
-        functools.partial(grads_kernel, planes),
-        grid=(groups,),
-        in_specs=[pl.BlockSpec((piece.shape[0], block), lambda i: (0, i)) for piece in pieces]
-        + [whole(cols[0]), whole(cols[1]), whole(rows[0]), whole(rows[1])],
+        functools.partial(grads_kernel, planes, tuple(len(group[0]) for group in groups)),
+        grid=(steps,),
+        in_specs=specs,
         out_specs=pl.BlockSpec((planes, lines, LANES), lambda i: (0, 0, 0)),
         out_shape=jax.ShapeDtypeStruct((planes, lines, LANES), BF),
-        compiler_params=pltpu.CompilerParams(vmem_limit_bytes=56 * 2**20),
+        compiler_params=pltpu.CompilerParams(vmem_limit_bytes=60 * 2**20),
         cost_estimate=filler(4 * tokens * width * (col_count + row_count)),
         name="weight_grads",
-    )(*pieces, *cols, *rows)
-
-
-def result_kernel(firsts, *refs):
-    hidden_first, hidden_second, packed_first, packed_second = refs[:4]
-    outs, down_s = refs[4:-1], refs[-1]
-    rows = hidden_first.shape[1]
+    )(*operands)
+
+
+def result_kernel(firsts, places, counts, *refs):
+    hiddens = (refs[: counts[0]], refs[counts[0] : sum(counts)])
+    refs = refs[sum(counts) :]
+    outs, down_s = refs[2:-1], refs[-1]
     step = pl.program_id(0)
+    first_rows = hiddens[0][0].shape[1]
 
     @pl.when(step == 0)
     def _():
-        unpack_rows(packed_first, firsts[0], down_s.at[:rows])
-        unpack_rows(packed_second, firsts[1], down_s.at[rows:])
-
-    out = dot_nn(hidden_first[...], down_s[:rows, :]) + dot_nn(hidden_second[...], down_s[rows:, :])
-    for slot in range(len(outs)):
+        unpack_rows(refs[0], firsts[0], down_s.at[:first_rows])
+        unpack_rows(refs[1], firsts[1], down_s.at[first_rows:])
+
+    for slot, out in enumerate(outs):
 
         @pl.when(step == slot)
-        def _(slot=slot):
-            outs[slot][...] = out.astype(BF)
-
-
-def result_call(hidden, packed, width):
-    slots = 4
-    tokens = hidden[0].shape[0]
-    rows = tokens // slots
-    total = sum(item.shape[1] for item in hidden)
+        def _(slot=slot, out=out):
+            rows = out.shape[0]
+            parts = []
+            for arrays, (index, offset) in zip(hiddens, places[slot]):
+                parts.append(arrays[index][offset : offset + rows, :])
+            total = dot_nn(parts[0], down_s[:first_rows, :])
+            total = total + dot_nn(parts[1], down_s[first_rows:, :])
+            out[...] = total.astype(BF)
+
+
+def result_call(hiddens, places, packed, rows, width):
+    slots = len(places)
+    total = hiddens[0][0].shape[1] + hiddens[1][0].shape[1]
     firsts = tuple(
-        part.shape[1] - item.shape[1] // part.shape[0] * width // LANES
-        for part, item in zip(packed, hidden)
-    )
+        part.shape[1] - arrays[0].shape[1] // part.shape[0] * width // LANES
+        for part, arrays in zip(packed, hiddens)
+    )
+    arrays = [*hiddens[0], *hiddens[1]]
+
+    def whole(array):
+        zeros = (0,) * array.ndim
+        return pl.BlockSpec(array.shape, lambda i: zeros, pipeline_mode=pl.Buffered(1))
+
     return pl.pallas_call(
-        functools.partial(result_kernel, firsts),
+        functools.partial(
+            result_kernel, firsts, places, (len(hiddens[0]), len(hiddens[1]))
+        ),
         grid=(slots,),
-        in_specs=[pl.BlockSpec((rows, item.shape[1]), lambda i: (i, 0)) for item in hidden]
-        + [
-            pl.BlockSpec(part.shape, lambda i: (0, 0, 0), pipeline_mode=pl.Buffered(1))
-            for part in packed
-        ],
+        in_specs=[whole(array) for array in arrays] + [whole(part) for part in packed],
         out_specs=[pl.BlockSpec((rows, width), lambda i: (0, 0))] * slots,
         out_shape=[jax.ShapeDtypeStruct((rows, width), BF)] * slots,
         scratch_shapes=[pltpu.VMEM((total, width), BF)],
         compiler_params=pltpu.CompilerParams(vmem_limit_bytes=48 * 2**20),
-        cost_estimate=filler(2 * tokens * width * total),
+        cost_estimate=filler(2 * slots * rows * width * total),
         name="ffn_result",
-    )(*hidden, *packed)
+    )(*arrays, *packed)
 
 
 def seq_copies(pieces, held, sems, seq):
@@ -1120,7 +1236,7 @@
     )
 
 
-def assemble_tiles_kernel(shares, *refs):
+def assemble_tiles_kernel(shares, planes, *refs):
     sources, outs = refs[: len(shares)], refs[len(shares) :]
     groups = sources[0].shape[0]
     run = sum(shares)
@@ -1134,7 +1250,10 @@
         firsts = [0] * len(shares)
         for out in outs:
             for block in range(out.shape[1] // (groups * run)):
-                base = (block * groups + group) * run
+                where = group
+                if planes:
+                    where = (block + group) % planes + planes * (group // planes)
+                base = (block * groups + where) * run
                 for index, share in enumerate(shares):
                     first = firsts[index]
                     out[:, base : base + share] = wides[index][:, first : first + share]
@@ -1142,10 +1261,10 @@
                     base += share
 
 
-def assemble_tiles(parts, shares, widths):
+def assemble_tiles(parts, shares, planes, widths):
     rows = parts[0].shape[2]
     return pl.pallas_call(
-        functools.partial(assemble_tiles_kernel, shares),
+        functools.partial(assemble_tiles_kernel, shares, planes),
         out_shape=[jax.ShapeDtypeStruct((rows, width), F32) for width in widths],
         compiler_params=pltpu.CompilerParams(vmem_limit_bytes=48 * 2**20),
         cost_estimate=SMALL,
@@ -1417,7 +1536,8 @@
             ]
         ),
     ]
-    sums = sum_all(jnp.concatenate(pieces))
+    sums = sum_seq(jnp.concatenate(pieces))
+    sums = sum_tree([sums, *others(sums)])
     cuts = []
     offset = 0
     for piece in pieces:
@@ -1474,6 +1594,7 @@
     shares = (ffn_run * 6 // 11, ffn_run - ffn_run * 6 // 11)
     if not (
         groups == 8
+        and groups % planes == 0
         and seqs == 2
         and chan % LANES == 0
         and all(2 * planes * share % LANES == 0 and share % 16 == 0 for share in shares)
@@ -1502,12 +1623,15 @@
 
     first_bit, second_bit = chip_bits()
 
-    def own_columns(array, run, first, count):
+    def turned(block):
+        return lax.rem(block + place, planes) + planes * (place // planes)
+
+    def own_columns(array, run, first, count, where):
         blocks = array.shape[1] // (run * groups)
         column = lax.broadcasted_iota(jnp.int32, (array.shape[1], blocks * count), 0)
         index = lax.broadcasted_iota(jnp.int32, (array.shape[1], blocks * count), 1)
         block = index // count
-        wanted = block * (run * groups) + place * run + first + (index - block * count)
+        wanted = (block * groups + where(block)) * run + first + (index - block * count)
         return dot(array, (column == wanted).astype(BF), "rc,cj->rj").astype(BF)
 
     def own_parts(vector):
@@ -1515,36 +1639,40 @@
         split = vector.reshape(count, groups, mix_run)
         return lax.dynamic_slice_in_dim(split, place, 1, 1).reshape(1, count * mix_run)
 
-    def own_rows(array, first, count):
+    def own_rows(array, first, count, where):
         run = array.shape[0] // groups
-        return lax.dynamic_slice_in_dim(array, place * run + first, count, 0)
+        return lax.dynamic_slice_in_dim(array, where * run + first, count, 0)
 
     rec_own = jnp.concatenate(
-        [own_columns(array, mix_run, 0, mix_run) for array in (w_in, w_forget, w_gate_out)], axis=1
-    )
-    packs = [pack([rec_own[None], own_rows(w_out, 0, mix_run)[None]])]
+        [
+            own_columns(array, mix_run, 0, mix_run, lambda block: place)
+            for array in (w_in, w_forget, w_gate_out)
+        ],
+        axis=1,
+    )
+    packs = [pack([rec_own[None], own_rows(w_out, 0, mix_run, place)[None]])]
     first = 0
     for share in shares:
         ff_own = jnp.concatenate(
-            [own_columns(array, ffn_run, first, share) for array in (w_ffgate, w_ffup)], axis=1
+            [own_columns(array, ffn_run, first, share, turned) for array in (w_ffgate, w_ffup)], axis=1
         )
-        packs.append(pack([ff_own[None], own_rows(w_down, first, share)[None]]))
+        packs.append(pack([ff_own[None], own_rows(w_down, first, share, turned(lax.axis_index("wshard")))[None]]))
         first += share
     rec_packed = gather_packed(packs[0])
-    packed = [gather_packed(item) for item in packs[1:]]
-
-    resid_in = after(tokens, packs[0]).reshape(rows, width).astype(F32)
+
+    upstream_own = out_grad.reshape(rows, width)
+    up_stage = gather_first(upstream_own)
+    tokens_, up_stage = tied(after(tokens, packs[0]), up_stage)
+    resid_in = tokens_.reshape(rows, width).astype(F32)
     scale_in = lax.rsqrt(jnp.mean(resid_in * resid_in, axis=1, keepdims=True) + EPS)
     normed_own = (resid_in * scale_in * gain_mix).astype(BF)
     normed_stage = gather_first(normed_own)
+    normed_stage, packs[1], packs[2] = tied(normed_stage, packs[1], packs[2])
     normed_far = gather_far(normed_own, normed_stage)
     normed_even = (normed_own, *normed_stage, *normed_far)
     normed_odd = cross(normed_even)
-    upstream_own = out_grad.reshape(rows, width)
-    up_gate = after(upstream_own, normed_far)
-    up_stage = gather_first(up_gate)
-    up_far = gather_far(up_gate, up_stage)
-    rec_packed, up_stage, _ = tied(rec_packed, up_stage, packs[1:])
+    up_far = gather_far(upstream_own, up_stage)
+    packed = [gather_packed(item) for item in packs[1:]]
 
     slots = lax.broadcasted_iota(jnp.int32, (groups, groups), 0)
     sources = lax.broadcasted_iota(jnp.int32, (groups, groups), 1)
@@ -1570,67 +1698,95 @@
     mixes = tuple(item.reshape(rows, width) for item in mixes)
     mix_even, mix_odd = mixes[:half], mixes[half:]
     mix_odd, up_far = tied(mix_odd, up_far)
-    up_even = (up_gate, *up_stage, *up_far)
+    up_even = (upstream_own, *up_stage, *up_far)
     square = shrink(square.reshape(groups, rows), 1)
     mix_crossed = cross(mix_odd)
-    mix_sums = joints(mix_even, mix_crossed)
+    mix_far = scatter_far(mix_even[3], mix_crossed[3])
     square_next = shrink(square, second_bit)
-    mix_stage, square_next = tied(scatter_first(mix_sums), square_next)
+    mix_far, square_next = tied(mix_far, square_next)
+    mix_near = scatter_near(mix_even[1:3], mix_crossed[1:3], mix_far)
     up_odd = cross(up_even)
     square_own = shrink(square_next, first_bit)
     scale_own = lax.rsqrt(square_own / width + EPS)
     scale_out = scale_own.reshape(rows, 1)
-    branch_mix = scale_out * scatter_last(mix_even, mix_crossed, mix_sums, mix_stage)
+    branch_mix = scale_out * scatter_sum(mix_even[0], mix_crossed[0], mix_near)
     resid = resid_in + branch_mix
     scale_ffn = lax.rsqrt(jnp.mean(resid * resid, axis=1, keepdims=True) + EPS)
     ffn_own = (resid * scale_ffn * gain_ffn).astype(BF)
     ffn_stage = gather_first(ffn_own)
     ffn_far = gather_far(ffn_own, ffn_stage)
-    ffn_even = (ffn_own, *ffn_stage, *ffn_far)
-    ffn_odd = cross(ffn_even)
     scale_all = gather_small(scale_own)
 
-    ff_even, ff_odd, ff_grads = [], [], []
-
-    def share_grads(index):
-        (hidden_e, grad_e), (hidden_o, grad_o) = ff_even[index], ff_odd[index]
-        return grads_call(
-            groups,
-            planes,
-            (ffn_even, ffn_odd),
-            (grad_e, grad_o),
-            (hidden_e, hidden_o),
-            (up_even, up_odd),
+    cols = [2 * planes * share for share in shares]
+
+    def block(normed, up, slot):
+        cut = slice(slot, slot + 1) if slot < 3 else slice(3, None)
+        return normed[cut], up[cut]
+
+    def grouped(blocks, out):
+        return (
+            [piece for item in blocks for piece in item[0]],
+            [piece for item in blocks for piece in item[1]],
+            out[1],
+            out[0],
         )
 
-    cols = [2 * planes * share for share in shares]
-    hidden, grad, back_odd = ffn_call(
-        ffn_odd, up_odd, packed[0], cols[0], None, False
-    )
-    ff_odd.append((hidden, grad))
-    hidden, grad, back_even = ffn_call(
-        ffn_even, up_even, packed[0], cols[0], None, False
-    )
-    ff_even.append((hidden, grad))
-    ff_grads.append(share_grads(0))
-    packed[1], ff_grads[0], back_even, scale_all = tied(
-        packed[1], ff_grads[0], back_even, scale_all
-    )
-    hidden, grad, *back_odd = ffn_call(
-        ffn_odd, up_odd, packed[1], cols[1], back_odd, True
-    )
-    ff_odd.append((hidden, grad))
-    hidden, grad, *back_even = ffn_call(
-        ffn_even, up_even, packed[1], cols[1], back_even, True
-    )
-    ff_even.append((hidden, grad))
-    back_crossed = cross(back_odd)
-    back_sums = joints(back_even, back_crossed)
-    back_stage = scatter_first(back_sums)
-    ff_even[1] = (ff_even[1][0], after(ff_even[1][1], back_sums))
-    ff_grads.append(share_grads(1))
-    back_stage, ff_grads[1] = tied(back_stage, ff_grads[1])
-    grad_normed_ffn = scatter_last(back_even, back_crossed, back_sums, back_stage)
+    def gradients(groups_, turn):
+        return grads_call(groups, planes, turn, groups_)
+
+    ffn_near = (ffn_own, *ffn_stage)
+    even_blocks = [block(ffn_near, up_even, slot) for slot in range(3)]
+    even_out = ffn_call(even_blocks, packed[0], cols[0], fills=True)
+    odd_near = cross(ffn_near)
+    odd_blocks = [block(odd_near, up_odd, slot) for slot in range(3)]
+    odd_out = ffn_call(odd_blocks, packed[0], cols[0], fills=True)
+    ffn_far, odd_out = tied(ffn_far, odd_out)
+    odd_far = cross(ffn_far)
+    ffn_even = (*ffn_near, *ffn_far)
+    ffn_odd = (*odd_near, *odd_far)
+    far_blocks = [block(ffn_even, up_even, 3), block(ffn_odd, up_odd, 3)]
+    far_out = ffn_call(far_blocks, packed[0], cols[0])
+    firsts = [
+        (even_blocks, even_out),
+        (odd_blocks, odd_out),
+        (far_blocks, far_out),
+    ]
+    ff_grads = [gradients([grouped(*item) for item in firsts], place_one)]
+    even_place = [(0, 0), (0, rows), (0, 2 * rows), (2, 0)]
+    odd_place = [(1, 0), (1, rows), (1, 2 * rows), (2, rows)]
+
+    def base(place_):
+        return firsts[place_[0]][1][2], place_[1]
+
+    packed[1], ff_grads[0], scale_all, _ = tied(packed[1], ff_grads[0], scale_all, far_out)
+    far_blocks = [block(ffn_odd, up_odd, 3), block(ffn_even, up_even, 3)]
+    far_out = ffn_call(far_blocks, packed[1], cols[1], [base(odd_place[3]), base(even_place[3])])
+    (far_crossed,) = cross([far_out[2]])
+    back_far = scatter_far(far_out[3], far_crossed)
+    near_packed, _ = tied(packed[1], far_crossed)
+    near_blocks = [block(ffn_odd, up_odd, slot) for slot in (1, 2)]
+    near_blocks += [block(ffn_even, up_even, slot) for slot in (1, 2)]
+    near_out = ffn_call(
+        near_blocks,
+        near_packed,
+        cols[1],
+        [base(odd_place[1]), base(odd_place[2]), base(even_place[1]), base(even_place[2])],
+        True,
+    )
+    back_far, near_out = tied(back_far, near_out)
+    near_crossed = cross(near_out[2:4])
+    back_sums = near_sums(near_out[4:6], near_crossed, back_far)
+    back_near = to_neighbours(back_sums)
+    own_packed, _ = tied(packed[1], back_sums)
+    own_blocks = [block(ffn_odd, up_odd, 0), block(ffn_even, up_even, 0)]
+    own_out = ffn_call(
+        own_blocks, own_packed, cols[1], [base(odd_place[0]), base(even_place[0])], True
+    )
+    (own_crossed,) = cross([own_out[2]])
+    seconds = [(far_blocks, far_out), (near_blocks, near_out), (own_blocks, own_out)]
+    ff_grads.append(gradients([grouped(*item) for item in seconds], place_one))
+    back_near, ff_grads[1], own_crossed = tied(back_near, ff_grads[1], own_crossed)
+    grad_normed_ffn = scatter_sum(own_out[3], own_crossed, back_near)
 
     scaled_ffn = grad_normed_ffn * gain_ffn
     grad_resid = (
@@ -1644,39 +1800,44 @@
     term_own = (scale_out[:, 0] ** 2 * overlap / width)[None]
     branch_stage = gather_first(grad_branch_own)
     term_near = grow(grow(term_own, 1), first_bit)
-    result_even, result_odd = (
-        result_call(
-                [after(share[0][0], grad_branch_own), share[1][0]],
-            packed,
-            width,
-        )
-        for share in (ff_even, ff_odd)
+    hiddens = [[item[1][0] for item in firsts], [item[1][0] for item in seconds]]
+    hiddens[1][2] = after(hiddens[1][2], grad_branch_own)
+    odd_second = [(2, 0), (1, 0), (1, rows), (0, 0)]
+    even_second = [(2, rows), (1, 2 * rows), (1, 3 * rows), (0, rows)]
+    result_odd = result_call(
+        hiddens, tuple(zip(odd_place, odd_second)), packed, rows, width
+    )
+    result_even = result_call(
+        hiddens, tuple(zip(even_place, even_second)), packed, rows, width
     )
     branch_stage, result_even, result_odd, term_near = tied(
         branch_stage, tuple(result_even), tuple(result_odd), term_near
     )
     branch_far = gather_far(grad_branch_own, branch_stage)
     result_crossed = cross(result_odd)
-    result_sums = joints(result_even, result_crossed)
     term_all = grow(term_near, second_bit)
-    branch_far, result_sums, term_all = tied(branch_far, result_sums, term_all)
+    branch_far, result_crossed, term_all = tied(branch_far, result_crossed, term_all)
+    result_stage = scatter_first(joints(result_even, result_crossed))
     term_all = slot_rows(term_all)
     branch_even = (grad_branch_own, *branch_stage, *branch_far)
     branch_odd = cross(branch_even)
-    result_stage = scatter_first(result_sums)
-
-    pairs = [(s * planes + w, w * groups + s) for s in range(groups) for w in range(planes)]
-
-    def owned(grads, count):
-        part = scatter_packed(grads)
+
+    mix_pairs = [(s * planes + w, w * groups + s) for s in range(groups) for w in range(planes)]
+    down_pairs = []
+    for s in range(groups):
+        for w in range(planes):
+            owner = (w - s) % planes * (groups // planes) + s // planes
+            down_pairs.append((s * planes + w, owner * planes + w))
+
+    scattered = [scatter_packed(grads) for grads in ff_grads]
+
+    def owned(part, count, pairs):
         lines = count * width // (planes * LANES)
         tiles = part[:lines].reshape(groups, -1, LANES)
         tiles = lax.all_to_all(tiles, "seq", split_axis=0, concat_axis=0, tiled=True)
         tiles = tiles.reshape(groups, count // LANES, -1, LANES)
         moved = lax.ppermute(part[lines:], ("seq", "wshard"), pairs)
         return tiles, moved.reshape(width // LANES, -1, LANES)
-
-    first_tiles, first_lines = owned(ff_grads[0], cols[0])
 
     shape_one = (groups, seqs, seq_dev, 1)
     (
@@ -1709,23 +1870,28 @@
     scaled_even = scaled_even.reshape(half * rows, 2 * chan)
     scaled_odd = scaled_odd.reshape(half * rows, 2 * chan)
     backs = tuple(item.reshape(rows, width) for item in backs)
-    grad_even, result_stage, first_tiles = tied(grad_even, result_stage, first_tiles)
-    rec_grads = grads_call(
-        groups,
-        planes,
-        (normed_even, normed_odd),
-        (grad_even, grad_odd),
-        (scaled_even, scaled_odd),
-        (branch_even, branch_odd),
+    grad_even, result_stage, scattered = tied(grad_even, result_stage, scattered)
+    rec_grads = gradients(
+        [
+            (normed_even, branch_even, grad_even, scaled_even),
+            (normed_odd, branch_odd, grad_odd, scaled_odd),
+        ],
+        jnp.zeros((1,), jnp.int32),
     )
     back_even, back_odd = backs[:half], backs[half:]
     back_crossed = cross(back_odd)
     back_crossed, rec_grads = tied(back_crossed, rec_grads)
-    branch_ffn = scatter_last(result_even, result_crossed, result_sums, result_stage)
+    back_far = scatter_far(back_even[3], back_crossed[3])
+    branch_ffn = scatter_last(result_even, result_crossed, after(result_stage, rec_grads))
+    back_far, branch_ffn = tied(back_far, branch_ffn)
+    back_near = scatter_near(back_even[1:3], back_crossed[1:3], back_far)
+    grad_normed_in = scatter_sum(back_even[0], back_crossed[0], back_near)
+    _, *scattered = tied(back_near, *scattered)
+    second_tiles, second_lines = owned(scattered[1], cols[1], down_pairs)
+    rec_part = after(scatter_packed(rec_grads), second_tiles)
+    rec_tiles, rec_lines = owned(rec_part, 5 * chan, mix_pairs)
+    first_tiles, first_lines = owned(after(scattered[0], rec_tiles), cols[0], down_pairs)
     result = (resid + branch_ffn).astype(BF)
-    back_sums = joints(back_even, back_crossed)
-    back_stage = tied(*scatter_first(back_sums))
-    grad_normed_in = scatter_last(back_even, back_crossed, back_sums, back_stage)
     scaled_in = grad_normed_in * gain_mix
     grad_tokens = (
         grad_resid
@@ -1736,13 +1902,11 @@
 
     hidden_all = w_ffgate.shape[1]
     rec_widths = (w_in.shape[1], w_forget.shape[1], w_gate_out.shape[1])
-    second_tiles, second_lines = owned(ff_grads[1], cols[1])
     grad_w_ffgate, grad_w_ffup = assemble_tiles(
-        [first_tiles, second_tiles], shares, (hidden_all, hidden_all)
+        [first_tiles, second_tiles], shares, planes, (hidden_all, hidden_all)
     )
     grad_w_down = assemble_rows([first_lines, second_lines])
-    rec_tiles, rec_lines = owned(rec_grads, 5 * chan)
-    grad_w_in, grad_w_forget, grad_w_gate = assemble_tiles([rec_tiles], (mix_run,), rec_widths)
+    grad_w_in, grad_w_forget, grad_w_gate = assemble_tiles([rec_tiles], (mix_run,), 0, rec_widths)
     grad_w_out = assemble_rows([rec_lines])
 
     def spread(part):
@@ -1765,7 +1929,9 @@
             ]
         ),
     ]
-    sums = sum_all(jnp.concatenate(pieces))
+    sums = sum_seq(jnp.concatenate(pieces))
+    sums = tied(rec_part, sums, *others(sums))[1:]
+    sums = sum_tree(list(sums))
     cuts = []
     offset = 0
     for piece in pieces:

time: 634 us -> 614 us (0.968)
  Pallas kernels: 204 us -> 233 us
  waiting for transfers between devices: 186 us -> 159 us
  other arithmetic: 70.4 us -> 44 us
  local copies, waits for them, and re-layouts: 43 us -> 55.8 us
  starting transfers between devices: 87.4 us -> 79.6 us
    pallas_call x11 -> x17, Pallas kernels: 142 us -> 171 us  [the longest x6 78.8 us: ffn_call(): pl.pallas_call(functools.partial(ffn_kernel, counts, offsets, last), grid...]
    convert_element_type x20 -> x5, other arithmetic: 32.6 us -> 8.44 us  [the longest x3 5.58 us: scatter_far(): (even[rows].astype(F32) + crossed[rows].astype(F32)).astype(BF)]
    ppermute x3, waiting for transfers between devices: 29.7 us -> 6.27 us  [owned(): moved = lax.ppermute(part[lines:], ('seq', 'wshard'), pairs)]
    ppermute x88 -> x82, starting transfers between devices: 65.4 us -> 51 us  [swap(): return lax.ppermute(value, 'seq', [(i, i ^ bit) for i in range(size)])]
    unnamed x152 -> x172, local copies, waits for them, and re-layouts: 8.87 us -> 19.2 us
    slice x8, local copies, waits for them, and re-layouts: 6.29 us -> 13.5 us  [gather_far(): return (swap(stage[0][:half], second), swap(stage[1][half:], first))]
    ppermute x88 -> x82, waiting for transfers between devices: 152 us -> 150 us  [swap(): return lax.ppermute(value, 'seq', [(i, i ^ bit) for i in range(size)])]
  transfers between devices with their start and end apart: 102 -> 97, of which waited for: 33 -> 30; matrix products, arithmetic and copies ran while one was open for 19% -> 17% of each run, Pallas kernels for 32% -> 38%
where the time goes in v4:
time: 614 us; the launch traced here: 608 us
  Pallas kernels  233 us (38%)
  waiting for transfers between devices  159 us (26%)
  starting transfers between devices  79.6 us (13%)
  local copies, waits for them, and re-layouts  55.8 us (9%)
  other arithmetic  44 us (7%)
  matrix products  19.6 us (3%)
  between operations  16.5 us (3%)
    ppermute x82, waiting for transfers between devices, swap(): return lax.ppermute(value, 'seq', [(i, i ^ bit) for i in range(size)])  150 us
    pallas_call x6, Pallas kernels, ffn_call(): pl.pallas_call(functools.partial(ffn_kernel, counts, offsets, last), grid...  78.8 us
    ppermute x82, starting transfers between devices, swap(): return lax.ppermute(value, 'seq', [(i, i ^ bit) for i in range(size)])  51 us
    pallas_call x3, Pallas kernels, grads_call(): pl.pallas_call(functools.partial(grads_kernel, planes, tuple((len(group[0...  50.2 us
    pallas_call x1, Pallas kernels, mix_backward(): pl.pallas_call(mix_backward_kernel, grid=(seqs,), in_specs=[SCALAR, SCALA...  32.2 us
    pallas_call x1, Pallas kernels, mix_forward(): pl.pallas_call(mix_forward_kernel, grid=(seqs,), in_specs=[SCALAR, SCALAR...  27.4 us
    pallas_call x2, Pallas kernels, result_call(): pl.pallas_call(functools.partial(result_kernel, firsts, places, (len(hidd...  20.1 us
    dot_general x7, matrix products, dot(): return jnp.einsum(form, left, right, preferred_element_type=F32)  19.6 us
  transfers between devices with their start and end apart: 97, of which 30 were waited for; matrix products, arithmetic and copies ran while one was open for 17% of the time, Pallas kernels for 38%

profile of v4, /device:TPU:4, one launch (start us, length us, event | category | flops | bytes accessed | tf_op | source)
XLA Modules:
  0.0 608.0 jit_solution(5029238422836449605)
XLA Ops:
  18.2 5.3 fusion.70
  28.1 5.1 fusion.64
  33.2 5.1 fusion.61
  45.4 20.2 %collective-permute-done.3.refs_9_.refs_2_ = bf16[256,2048]{1,0:T(8,128)(2,1)} collective-permute-done((bf16[256,2048]{1,0:T(8,128)(2,1)S(1)}, bf16[256,2048]{1,0:T(8,128)(2,1)}, u32[]{:S(2)}, u32[]{:S(2)}) %collective-permute-start.3) | collective-permute-done | bytes 1048608 | tf_op jit(solution)/shard_map/ppermute | solution.py:22
  78.5 6.3 %collective-permute-done.5.refs_11_.refs_4_ = bf16[128,2048]{1,0:T(8,128)(2,1)} collective-permute-done((bf16[128,2048]{1,0:T(8,128)(2,1)}, bf16[128,2048]{1,0:T(8,128)(2,1)}, u32[]{:S(2)}, u32[]{:S(2)}) %collective-permute-start.5) | collective-permute-done | bytes 524320 | tf_op jit(solution)/shard_map/ppermute | solution.py:22
  91.1 27.4 %mix_forward.1 = (f32[4,2,128,640]{3,2,1,0:T(8,128)}, f32[4,2,128,640]{3,2,1,0:T(8,128)}, f32[8,2,128,256]{3,2,1,0:T(8,128)}, f32[8,2,128,1]{3,2,1,0:T(8,128)}, ...) custom-call(s32[1]{0:T(128)} %bitcast.10.refs_0_.turn_ref, ...), custom_call_target="tpu_custom_call" | custom-call | flops 1024 | bytes 1024 | tf_op jit(solution)/shard_map/mix_forward/pallas_call | solution.py:1066
  129.4 8.7 %collective-permute-done.17 = f32[2,256]{1,0:T(2,128)S(1)} collective-permute-done((f32[2,256]{1,0:T(2,128)S(1)}, f32[2,256]{1,0:T(2,128)S(1)}, u32[]{:S(2)}, u32[]{:S(2)}) %collective-permute-start.17) | collective-permute-done | bytes 2080 | tf_op jit(solution)/shard_map/ppermute | solution.py:22
  140.7 4.5 onward_sums.3
  148.3 22.0 %collective-permute-done.18 = f32[1,256]{1,0:T(1,128)S(1)} collective-permute-done((f32[1,256]{1,0:T(1,128)S(1)}, f32[1,256]{1,0:T(1,128)S(1)}, u32[]{:S(2)}, u32[]{:S(2)}) %collective-permute-start.18) | collective-permute-done | bytes 1056 | tf_op jit(solution)/shard_map/ppermute | solution.py:22
  181.2 21.5 %collective-permute-done.39 = f32[2,256]{1,0:T(2,128)S(1)} collective-permute-done((f32[2,256]{1,0:T(2,128)S(1)}, f32[2,256]{1,0:T(2,128)S(1)}, u32[]{:S(2)}, u32[]{:S(2)}) %collective-permute-start.39) | collective-permute-done | bytes 2080 | tf_op jit(solution)/shard_map/ppermute | solution.py:22
  213.3 14.0 %ffn.7 = (bf16[768,384]{1,0:T(8,128)(2,1)}, bf16[768,768]{1,0:T(8,128)(2,1)}, f32[768,2048]{1,0:T(8,128)}) custom-call(bf16[4,4608,128]{2,1,0:T(8,128)(2,1)} %all-gather.8.cloned.1.call-done.refs_0_.refs_6_, bf16[256,2048]{1,0:T(8,128)(2,1)} %collective-permute-done.26.refs_1_.refs_8_.refs_20_, ...), custom_call_target="tpu_custom_call" | custom-call | flops 6039797760 | bytes 1024 | tf_op jit(solution)/shard_map/ffn/pallas_call | solution.py:821
  228.0 13.7 %ffn.6 = (bf16[768,384]{1,0:T(8,128)(2,1)}, bf16[768,768]{1,0:T(8,128)(2,1)}, f32[768,2048]{1,0:T(8,128)}) custom-call(bf16[4,4608,128]{2,1,0:T(8,128)(2,1)} %all-gather.8.cloned.1.call-done.refs_0_.refs_6_, bf16[256,2048]{1,0:T(8,128)(2,1)} %copy-done.19, bf16[256,2048]{1,0:T(8,128)(2,1)} %collective-permute-done.24.refs_2_.refs_1_.refs_3_.refs_12_, ...), custom_call_target="tpu_custom_call" | custom-call | flops 6039797760 | bytes 1024 | tf_op jit(solution)/shard_map/ffn/pallas_call | solution.py:821
  243.3 10.9 %ffn.8 = (bf16[512,384]{1,0:T(8,128)(2,1)}, bf16[512,768]{1,0:T(8,128)(2,1)}, f32[512,2048]{1,0:T(8,128)}) custom-call(bf16[4,4608,128]{2,1,0:T(8,128)(2,1)} %all-gather.8.cloned.1.call-done.refs_0_.refs_6_, bf16[128,2048]{1,0:T(8,128)(2,1)} %collective-permute-done.32.refs_1_.refs_16_.refs_3_.refs_2_, ...), custom_call_target="tpu_custom_call" | custom-call | flops 1024 | bytes 1024 | tf_op jit(solution)/shard_map/ffn/pallas_call | solution.py:821
  254.2 17.3 %weight_grads.3 = bf16[4,4608,128]{2,1,0:T(8,128)(2,1)} custom-call(s32[1]{0:T(128)} %bitcast.10.refs_0_.turn_ref, bf16[256,2048]{1,0:T(8,128)(2,1)} %copy-done.19, bf16[256,2048]{1,0:T(8,128)(2,1)} %collective-permute-done.24.refs_2_.refs_1_.refs_3_.refs_12_, bf16[256,2048]{1,0:T(8,128)(2,1)} %collective-permute-done.25.refs_3_.refs_2_.refs_4_.refs_13_, ...), custom_call_target="tpu_custom_call" | custom-call | flops 19327352832 | bytes 1024 | tf_op jit(solution)/shard_map/weight_grads/pallas_call | solution.py:901
  271.6 11.6 %ffn.9 = (bf16[512,320]{1,0:T(8,128)(2,1)}, bf16[512,640]{1,0:T(8,128)(2,1)}, bf16[256,2048]{1,0:T(8,128)(2,1)}, bf16[256,2048]{1,0:T(8,128)(2,1)}) custom-call(bf16[4,3840,128]{2,1,0:T(8,128)(2,1)} %all-gather.6.cloned.1.call-done.refs_0_.refs_7_, bf16[128,2048]{1,0:T(8,128)(2,1)} %copy-done.31, bf16[128,2048]{1,0:T(8,128)(2,1)} %copy-done.32, ...), custom_call_target="tpu_custom_call" | custom-call | flops 1024 | bytes 1024 | tf_op jit(solution)/shard_map/ffn/pallas_call | solution.py:821
  290.7 17.3 %ffn.10 = (bf16[1024,320]{1,0:T(8,128)(2,1)}, bf16[1024,640]{1,0:T(8,128)(2,1)}, bf16[256,2048]{1,0:T(8,128)(2,1)}, bf16[256,2048]{1,0:T(8,128)(2,1)}, bf16[256,...) custom-call(bf16[4,3840,128]{2,1,0:T(8,128)(2,1)} %all-gather.6.cloned.1.call-done.refs_0_.refs_7_, ...), custom_call_target="tpu_custom_call" | custom-call | flops 6710886400 | bytes 1024 | tf_op jit(solution)/shard_map/ffn/pallas_call | solution.py:821
  320.6 11.3 %ffn.11 = (bf16[512,320]{1,0:T(8,128)(2,1)}, bf16[512,640]{1,0:T(8,128)(2,1)}, bf16[256,2048]{1,0:T(8,128)(2,1)}, bf16[256,2048]{1,0:T(8,128)(2,1)}) custom-call(bf16[4,3840,128]{2,1,0:T(8,128)(2,1)} %all-gather.6.cloned.1.call-done.refs_0_.refs_7_, bf16[256,2048]{1,0:T(8,128)(2,1)} %collective-permute-done.26.refs_1_.refs_8_.refs_20_, ...), custom_call_target="tpu_custom_call" | custom-call | flops 3355443200 | bytes 1024 | tf_op jit(solution)/shard_map/ffn/pallas_call | solution.py:821
  332.0 16.7 %weight_grads.4 = bf16[4,3840,128]{2,1,0:T(8,128)(2,1)} custom-call(s32[1]{0:T(128)} %bitcast.10.refs_0_.turn_ref, bf16[128,2048]{1,0:T(8,128)(2,1)} %copy-done.31, bf16[128,2048]{1,0:T(8,128)(2,1)} %copy-done.32, bf16[128,2048]{1,0:T(8,128)(2,1)} %collective-permute-done.32.refs_1_.refs_16_.refs_3_.refs_2_, ...), custom_call_target="tpu_custom_call" | custom-call | flops 16106127360 | bytes 1024 | tf_op jit(solution)/shard_map/weight_grads/pallas_call | solution.py:901
  352.2 5.8 multiply_reduce_fusion.1
  360.2 10.1 %ffn_result.3 = (bf16[256,2048]{1,0:T(8,128)(2,1)S(1)}, bf16[256,2048]{1,0:T(8,128)(2,1)S(1)}, bf16[256,2048]{1,0:T(8,128)(2,1)}, bf16[256,2048]{1,0:T(8,128)(2,1)}) custom-call(bf16[768,384]{1,0:T(8,128)(2,1)S(1)} %copy-done.6, bf16[768,384]{1,0:T(8,128)(2,1)S(1)} %copy-done.5, bf16[512,384]{1,0:T(8,128)(2,1)S(1)} %copy-done.9, ...), custom_call_target="tpu_custom_call" | custom-call | flops 2952790016 | bytes 1024 | tf_op jit(solution)/shard_map/ffn_result/pallas_call | solution.py:951
  371.0 10.1 %ffn_result.2 = (bf16[256,2048]{1,0:T(8,128)(2,1)S(1)}, bf16[256,2048]{1,0:T(8,128)(2,1)S(1)}, bf16[256,2048]{1,0:T(8,128)(2,1)}, bf16[256,2048]{1,0:T(8,128)(2,1)}) custom-call(bf16[768,384]{1,0:T(8,128)(2,1)S(1)} %copy-done.6, bf16[768,384]{1,0:T(8,128)(2,1)S(1)} %copy-done.5, bf16[512,384]{1,0:T(8,128)(2,1)S(1)} %copy-done.9, ...), custom_call_target="tpu_custom_call" | custom-call | flops 2952790016 | bytes 1024 | tf_op jit(solution)/shard_map/ffn_result/pallas_call | solution.py:951
  390.7 9.2 %collective-permute-done.54.refs_16_.refs_9_ = bf16[128,2048]{1,0:T(8,128)(2,1)} collective-permute-done((bf16[128,2048]{1,0:T(8,128)(2,1)S(1)}, bf16[128,2048]{1,0:T(8,128)(2,1)}, u32[]{:S(2)}, u32[]{:S(2)}) %collective-permute-start.54) | collective-permute-done | bytes 524320 | tf_op jit(solution)/shard_map/ppermute | solution.py:22
  417.0 32.2 %mix_backward.1 = (bf16[4,2,128,640]{3,2,1,0:T(8,128)(2,1)}, bf16[4,2,128,640]{3,2,1,0:T(8,128)(2,1)}, bf16[4,2,128,256]{3,2,1,0:T(8,128)(2,1)}, bf16[4,2,128,25...) custom-call(s32[1]{0:T(128)} %bitcast.10.refs_0_.turn_ref, ...), custom_call_target="tpu_custom_call" | custom-call | flops 1024 | bytes 1024 | tf_op jit(solution)/shard_map/mix_backward/pallas_call | solution.py:1180
  451.9 16.2 %weight_grads.5 = bf16[4,3584,128]{2,1,0:T(8,128)(2,1)} custom-call(s32[1]{0:T(128)} %constant.147.clone.1.turn_ref, bf16[256,2048]{1,0:T(8,128)(2,1)} %copy-done.20, bf16[256,2048]{1,0:T(8,128)(2,1)} %collective-permute-done.2.refs_8_.refs_1_, bf16[256,2048]{1,0:T(8,128)(2,1)} %collective-permute-done.3.refs_9_.refs_2_, ...), custom_call_target="tpu_custom_call" | custom-call | flops 15032385536 | bytes 1024 | tf_op jit(solution)/shard_map/weight_grads/pallas_call | solution.py:901
  478.5 9.0 %collective-permute-done.75 = bf16[128,2048]{1,0:T(8,128)(2,1)S(1)} collective-permute-done((bf16[128,2048]{1,0:T(8,128)(2,1)S(1)}, bf16[128,2048]{1,0:T(8,128)(2,1)S(1)}, u32[]{:S(2)}, u32[]{:S(2)}) %collective-permute-start.75) | collective-permute-done | bytes 524320 | tf_op jit(solution)/shard_map/ppermute | solution.py:22
  490.9 8.1 %collective-permute-done.74.far_low = bf16[128,2048]{1,0:T(8,128)(2,1)S(1)} collective-permute-done((bf16[128,2048]{1,0:T(8,128)(2,1)S(1)}, bf16[128,2048]{1,0:T(8,128)(2,1)S(1)}, u32[]{:S(2)}, u32[]{:S(2)}) %collective-permute-start.74) | collective-permute-done | bytes 524320 | tf_op jit(solution)/shard_map/ppermute | solution.py:22
  500.0 4.6 onward_sums.5
  513.5 15.6 %collective-permute-done.77 = bf16[256,2048]{1,0:T(8,128)(2,1)} collective-permute-done((bf16[256,2048]{1,0:T(8,128)(2,1)}, bf16[256,2048]{1,0:T(8,128)(2,1)}, u32[]{:S(2)}, u32[]{:S(2)}) %collective-permute-start.77) | collective-permute-done | bytes 1048608 | tf_op jit(solution)/shard_map/ppermute | solution.py:22
  530.3 4.9 all-to-all-start
  557.1 6.5 %all-to-all-start.1 = ((bf16[8,320,128]{2,1,0:T(8,128)(2,1)}), bf16[8,320,128]{2,1,0:T(8,128)(2,1)S(1)}, u32[]{:S(2)}, u32[]{:S(2)}) async-start(bf16[8,320,128]{2,1,0:T(8,128)(2,1)} %bitcast.186), calls=%async_computation.4 | async-start | bytes 1310720 | tf_op jit(solution)/shard_map/all_to_all | solution.py:1837
  575.6 5.0 all-to-all-start.2
  591.5 4.9 collective-permute-done.86
  (485 shorter events, 210.3 us)
Async XLA Ops:
  7.2 83.0 %all-gather.4.cloned.1.call-start = ((), (), s32[]{:S(2)}) async-start(), calls=%async_computation.6 | async-start | bytes 4587520 | tf_op jit(solution)/shard_map/all_gather | solution.py:261
  7.2 31.6 %collective-permute-start.1 = (bf16[256,2048]{1,0:T(8,128)(2,1)}, bf16[256,2048]{1,0:T(8,128)(2,1)}, u32[]{:S(2)}, u32[]{:S(2)}) collective-permute-start(bf16[256,2048]{1,0:T(8,128)(2,1)} %bitcast.8.refs_4_.refs_3_.refs_23_), channel_id=1, source_target_pairs={{0,16},{4,20},{8,24},{12,28},{16,0},{20,4},{24,8},{28,12},{1,17},{... | collective-permute-start | bytes 3145736 | tf_op jit(solution)/shard_map/ppermute | solution.py:22
  7.3 31.5 %collective-permute-start = (bf16[256,2048]{1,0:T(8,128)(2,1)}, bf16[256,2048]{1,0:T(8,128)(2,1)}, u32[]{:S(2)}, u32[]{:S(2)}) collective-permute-start(bf16[256,2048]{1,0:T(8,128)(2,1)} %bitcast.8.refs_4_.refs_3_.refs_23_), channel_id=1, source_target_pairs={{0,8},{4,12},{8,0},{12,4},{16,24},{20,28},{24,16},{28,20},{1,9},{5... | collective-permute-start | bytes 3145736 | tf_op jit(solution)/shard_map/ppermute | solution.py:22
  15.7 197.7 %all-gather.8.cloned.1.call-start = ((), (), s32[]{:S(2)}) async-start(), calls=%async_computation.8 | async-start | bytes 5898240 | tf_op jit(solution)/shard_map/all_gather | solution.py:261
  41.2 24.5 %collective-permute-start.3 = (bf16[256,2048]{1,0:T(8,128)(2,1)S(1)}, bf16[256,2048]{1,0:T(8,128)(2,1)}, u32[]{:S(2)}, u32[]{:S(2)}) collective-permute-start(bf16[256,2048]{1,0:T(8,128)(2,1)S(1)} %fusion.41.refs_7_.refs_0_), channel_id=1, source_target_pairs={{0,16},{4,20},{8,24},{12,28},{16,0},{20,4},{24,8},{28,12},{1,17},{... | collective-permute-start | bytes 3145736 | tf_op jit(solution)/shard_map/ppermute | solution.py:22
  42.7 24.2 %collective-permute-start.2 = (bf16[256,2048]{1,0:T(8,128)(2,1)S(1)}, bf16[256,2048]{1,0:T(8,128)(2,1)}, u32[]{:S(2)}, u32[]{:S(2)}) collective-permute-start(bf16[256,2048]{1,0:T(8,128)(2,1)S(1)} %fusion.41.refs_7_.refs_0_), channel_id=1, source_target_pairs={{0,8},{4,12},{8,0},{12,4},{16,24},{20,28},{24,16},{28,20},{1,9},{5... | collective-permute-start | bytes 3145736 | tf_op jit(solution)/shard_map/ppermute | solution.py:22
  67.0 204.5 %all-gather.6.cloned.1.call-start = ((), (), s32[]{:S(2)}) async-start(), calls=%async_computation.7 | async-start | bytes 4915200 | tf_op jit(solution)/shard_map/all_gather | solution.py:261
  78.0 40.6 %collective-permute-start.12 = (bf16[128,2048]{1,0:T(8,128)(2,1)}, bf16[128,2048]{1,0:T(8,128)(2,1)}, u32[]{:S(2)}, u32[]{:S(2)}) collective-permute-start(bf16[128,2048]{1,0:T(8,128)(2,1)} %slice.140), channel_id=1, source_target_pairs={{0,8},{4,12},{8,0},{12,4},{16,24},{20,28},{24,16},{28,20},{1,9},{5... | collective-permute-start | bytes 1572872 | tf_op jit(solution)/shard_map/ppermute | solution.py:22
  84.8 33.8 %collective-permute-start.11 = (bf16[128,2048]{1,0:T(8,128)(2,1)}, bf16[128,2048]{1,0:T(8,128)(2,1)}, u32[]{:S(2)}, u32[]{:S(2)}) collective-permute-start(bf16[128,2048]{1,0:T(8,128)(2,1)} %slice.139), channel_id=1, source_target_pairs={{0,16},{4,20},{8,24},{12,28},{16,0},{20,4},{24,8},{28,12},{1,17},{... | collective-permute-start | bytes 1572872 | tf_op jit(solution)/shard_map/ppermute | solution.py:22
  138.2 32.1 %collective-permute-start.19 = (bf16[256,2048]{1,0:T(8,128)(2,1)}, bf16[256,2048]{1,0:T(8,128)(2,1)S(1)}, u32[]{:S(2)}, u32[]{:S(2)}) collective-permute-start(bf16[256,2048]{1,0:T(8,128)(2,1)} %bitcast.29), channel_id=1, source_target_pairs={{0,4},{4,0},{8,12},{12,8},{16,20},{20,16},{24,28},{28,24},{1,5},{5... | collective-permute-start | bytes 3145736 | tf_op jit(solution)/shard_map/ppermute | solution.py:22
  145.2 25.1 %collective-permute-start.22 = (bf16[256,2048]{1,0:T(8,128)(2,1)}, bf16[256,2048]{1,0:T(8,128)(2,1)S(1)}, u32[]{:S(2)}, u32[]{:S(2)}) collective-permute-start(bf16[256,2048]{1,0:T(8,128)(2,1)} %get-tuple-element.195), channel_id=1, source_target_pairs={{0,8},{4,12},{8,0},{12,4},{16,24},{20,28},{24,16},{28,20},{1,9},{5... | collective-permute-start | bytes 3145736 | tf_op jit(solution)/shard_map/ppermute | solution.py:22
  146.1 25.6 %collective-permute-start.23 = (bf16[256,2048]{1,0:T(8,128)(2,1)}, bf16[256,2048]{1,0:T(8,128)(2,1)}, u32[]{:S(2)}, u32[]{:S(2)}) collective-permute-start(bf16[256,2048]{1,0:T(8,128)(2,1)} %get-tuple-element.196), channel_id=1, source_target_pairs={{0,16},{4,20},{8,24},{12,28},{16,0},{20,4},{24,8},{28,12},{1,17},{... | collective-permute-start | bytes 3145736 | tf_op jit(solution)/shard_map/ppermute | solution.py:22
  148.2 54.9 %collective-permute-start.29 = (bf16[256,2048]{1,0:T(8,128)(2,1)}, bf16[256,2048]{1,0:T(8,128)(2,1)}, u32[]{:S(2)}, u32[]{:S(2)}) collective-permute-start(bf16[256,2048]{1,0:T(8,128)(2,1)} %bitcast.8.refs_4_.refs_3_.refs_23_), channel_id=1, source_target_pairs={{0,4},{4,0},{8,12},{12,8},{16,20},{20,16},{24,28},{28,24},{1,5},{5... | collective-permute-start | bytes 3145736 | tf_op jit(solution)/shard_map/ppermute | solution.py:22
  148.3 302.9 %reduce-scatter.4.cloned.1.call-start = ((), (), s32[]{:S(2)}) async-start(), calls=%async_computation.9 | async-start | bytes 5898240 | tf_op jit(solution)/shard_map/reduce_scatter | solution.py:265
  176.3 30.1 %collective-permute-start.25 = (bf16[256,2048]{1,0:T(8,128)(2,1)S(1)}, bf16[256,2048]{1,0:T(8,128)(2,1)}, u32[]{:S(2)}, u32[]{:S(2)}) collective-permute-start(bf16[256,2048]{1,0:T(8,128)(2,1)S(1)} %multiply_convert_fusion.refs_1_.refs_0_.refs_2_.refs_21_), channel_id=1, source_target_pairs={{0,16},{4,20},{8,24},{12,28},{16,0},{20,4},{24,8},{28,12},{1,17},{... | collective-permute-start | bytes 3145736 | tf_op jit(solution)/shard_map/ppermute | solution.py:22
  178.0 28.9 %collective-permute-start.24 = (bf16[256,2048]{1,0:T(8,128)(2,1)S(1)}, bf16[256,2048]{1,0:T(8,128)(2,1)}, u32[]{:S(2)}, u32[]{:S(2)}) collective-permute-start(bf16[256,2048]{1,0:T(8,128)(2,1)S(1)} %multiply_convert_fusion.refs_1_.refs_0_.refs_2_.refs_21_), channel_id=1, source_target_pairs={{0,8},{4,12},{8,0},{12,4},{16,24},{20,28},{24,16},{28,20},{1,9},{5... | collective-permute-start | bytes 3145736 | tf_op jit(solution)/shard_map/ppermute | solution.py:22
  210.8 30.9 %collective-permute-start.36 = (bf16[128,2048]{1,0:T(8,128)(2,1)}, bf16[128,2048]{1,0:T(8,128)(2,1)}, u32[]{:S(2)}, u32[]{:S(2)}) collective-permute-start(bf16[128,2048]{1,0:T(8,128)(2,1)} %collective-permute-done.11.refs_5_.refs_20_.refs_7_.refs_6_), channel_id=1, source_target_pairs={{0,4},{4,0},{8,12},{12,8},{16,20},{20,16},{24,28},{28,24},{1,5},{5... | collective-permute-start | bytes 1572872 | tf_op jit(solution)/shard_map/ppermute | solution.py:22
  211.3 30.4 %collective-permute-start.37 = (bf16[128,2048]{1,0:T(8,128)(2,1)}, bf16[128,2048]{1,0:T(8,128)(2,1)}, u32[]{:S(2)}, u32[]{:S(2)}) collective-permute-start(bf16[128,2048]{1,0:T(8,128)(2,1)} %collective-permute-done.12.refs_6_.refs_21_.refs_8_.refs_7_), channel_id=1, source_target_pairs={{0,4},{4,0},{8,12},{12,8},{16,20},{20,16},{24,28},{28,24},{1,5},{5... | collective-permute-start | bytes 1572872 | tf_op jit(solution)/shard_map/ppermute | solution.py:22
  271.5 179.6 %reduce-scatter.6.cloned.1.call-start = ((), (), s32[]{:S(2)}) async-start(), calls=%async_computation.10 | async-start | bytes 4915200 | tf_op jit(solution)/shard_map/reduce_scatter | solution.py:265
  318.6 30.1 %collective-permute-start.46 = (bf16[256,2048]{1,0:T(8,128)(2,1)}, bf16[256,2048]{1,0:T(8,128)(2,1)S(1)}, u32[]{:S(2)}, u32[]{:S(2)}) collective-permute-start(bf16[256,2048]{1,0:T(8,128)(2,1)} %get-tuple-element.235), channel_id=1, source_target_pairs={{0,8},{4,12},{8,0},{12,4},{16,24},{20,28},{24,16},{28,20},{1,9},{5... | collective-permute-start | bytes 3145736 | tf_op jit(solution)/shard_map/ppermute | solution.py:22
  319.3 29.4 %collective-permute-start.47 = (bf16[256,2048]{1,0:T(8,128)(2,1)}, bf16[256,2048]{1,0:T(8,128)(2,1)}, u32[]{:S(2)}, u32[]{:S(2)}) collective-permute-start(bf16[256,2048]{1,0:T(8,128)(2,1)} %get-tuple-element.236), channel_id=1, source_target_pairs={{0,16},{4,20},{8,24},{12,28},{16,0},{20,4},{24,8},{28,12},{1,17},{... | collective-permute-start | bytes 3145736 | tf_op jit(solution)/shard_map/ppermute | solution.py:22
  348.8 206.4 %reduce-scatter.8.cloned.1.call-start = ((), (), s32[]{:S(2)}) async-start(), calls=%async_computation.11 | async-start | bytes 4587520 | tf_op jit(solution)/shard_map/reduce_scatter | solution.py:265
  358.0 26.3 %collective-permute-start.50 = (bf16[256,2048]{1,0:T(8,128)(2,1)S(1)}, bf16[256,2048]{1,0:T(8,128)(2,1)}, u32[]{:S(2)}, u32[]{:S(2)}) collective-permute-start(bf16[256,2048]{1,0:T(8,128)(2,1)S(1)} %get-tuple-element.341.refs_12_.refs_5_), channel_id=1, source_target_pairs={{0,16},{4,20},{8,24},{12,28},{16,0},{20,4},{24,8},{28,12},{1,17},{... | collective-permute-start | bytes 3145736 | tf_op jit(solution)/shard_map/ppermute | solution.py:22
  358.7 25.6 %collective-permute-start.49 = (bf16[256,2048]{1,0:T(8,128)(2,1)S(1)}, bf16[256,2048]{1,0:T(8,128)(2,1)}, u32[]{:S(2)}, u32[]{:S(2)}) collective-permute-start(bf16[256,2048]{1,0:T(8,128)(2,1)S(1)} %get-tuple-element.341.refs_12_.refs_5_), channel_id=1, source_target_pairs={{0,8},{4,12},{8,0},{12,4},{16,24},{20,28},{24,16},{28,20},{1,9},{5... | collective-permute-start | bytes 3145736 | tf_op jit(solution)/shard_map/ppermute | solution.py:22
  409.6 39.7 %collective-permute-start.69 = (bf16[128,2048]{1,0:T(8,128)(2,1)}, bf16[128,2048]{1,0:T(8,128)(2,1)S(1)}, u32[]{:S(2)}, u32[]{:S(2)}) collective-permute-start(bf16[128,2048]{1,0:T(8,128)(2,1)} %get-tuple-element.280), channel_id=1, source_target_pairs={{0,8},{4,12},{8,0},{12,4},{16,24},{20,28},{24,16},{28,20},{1,9},{5... | collective-permute-start | bytes 1572872 | tf_op jit(solution)/shard_map/ppermute | solution.py:22
  411.0 39.6 %collective-permute-start.70 = (bf16[128,2048]{1,0:T(8,128)(2,1)}, bf16[128,2048]{1,0:T(8,128)(2,1)}, u32[]{:S(2)}, u32[]{:S(2)}) collective-permute-start(bf16[128,2048]{1,0:T(8,128)(2,1)} %get-tuple-element.281), channel_id=1, source_target_pairs={{0,16},{4,20},{8,24},{12,28},{16,0},{20,4},{24,8},{28,12},{1,17},{... | collective-permute-start | bytes 1572872 | tf_op jit(solution)/shard_map/ppermute | solution.py:22
  411.7 38.9 %collective-permute-start.71 = (bf16[128,2048]{1,0:T(8,128)(2,1)}, bf16[128,2048]{1,0:T(8,128)(2,1)S(1)}, u32[]{:S(2)}, u32[]{:S(2)}) collective-permute-start(bf16[128,2048]{1,0:T(8,128)(2,1)} %get-tuple-element.282), channel_id=1, source_target_pairs={{0,8},{4,12},{8,0},{12,4},{16,24},{20,28},{24,16},{28,20},{1,9},{5... | collective-permute-start | bytes 1572872 | tf_op jit(solution)/shard_map/ppermute | solution.py:22
  413.1 38.0 %collective-permute-start.72 = (bf16[128,2048]{1,0:T(8,128)(2,1)}, bf16[128,2048]{1,0:T(8,128)(2,1)S(1)}, u32[]{:S(2)}, u32[]{:S(2)}) collective-permute-start(bf16[128,2048]{1,0:T(8,128)(2,1)} %get-tuple-element.283), channel_id=1, source_target_pairs={{0,16},{4,20},{8,24},{12,28},{16,0},{20,4},{24,8},{28,12},{1,17},{... | collective-permute-start | bytes 1572872 | tf_op jit(solution)/shard_map/ppermute | solution.py:22
  504.6 24.5 %collective-permute-start.77 = (bf16[256,2048]{1,0:T(8,128)(2,1)}, bf16[256,2048]{1,0:T(8,128)(2,1)}, u32[]{:S(2)}, u32[]{:S(2)}) collective-permute-start(bf16[256,2048]{1,0:T(8,128)(2,1)} %get-tuple-element.311), channel_id=1, source_target_pairs={{0,8},{4,12},{8,0},{12,4},{16,24},{20,28},{24,16},{28,20},{1,9},{5... | collective-permute-start | bytes 3145736 | tf_op jit(solution)/shard_map/ppermute | solution.py:22
  505.2 24.2 %collective-permute-start.78 = (bf16[256,2048]{1,0:T(8,128)(2,1)}, bf16[256,2048]{1,0:T(8,128)(2,1)}, u32[]{:S(2)}, u32[]{:S(2)}) collective-permute-start(bf16[256,2048]{1,0:T(8,128)(2,1)} %get-tuple-element.312), channel_id=1, source_target_pairs={{0,16},{4,20},{8,24},{12,28},{16,0},{20,4},{24,8},{28,12},{1,17},{... | collective-permute-start | bytes 3145736 | tf_op jit(solution)/shard_map/ppermute | solution.py:22
  530.3 24.8 %all-to-all-start = ((bf16[8,320,128]{2,1,0:T(8,128)(2,1)}), bf16[8,320,128]{2,1,0:T(8,128)(2,1)S(1)}, u32[]{:S(2)}, u32[]{:S(2)}) async-start(bf16[8,320,128]{2,1,0:T(8,128)(2,1)} %bitcast.60), calls=%async_computation.3 | async-start | bytes 1310720 | tf_op jit(solution)/shard_map/all_to_all | solution.py:1837
  548.0 43.5 %collective-permute-start.87 = (bf16[1280,128]{1,0:T(8,128)(2,1)}, bf16[1280,128]{1,0:T(8,128)(2,1)}, u32[]{:S(2)}, u32[]{:S(2)}) collective-permute-start(bf16[1280,128]{1,0:T(8,128)(2,1)} %slice.178), channel_id=1, source_target_pairs={{0,0},{1,9},{2,18},{3,27},{4,24},{5,1},{6,10},{7,19},{8,16},{9,25}... | collective-permute-start | bytes 983048 | tf_op jit(solution)/shard_map/ppermute | solution.py:1839
  (147 other events, 1621.1 us)
Sparse Core Ops, SparseCore 0:
  15.8 72.7 all-gather.3
  90.7 88.0 all-gather.7
  180.4 74.8 all-gather.5
  271.7 85.8 reduce-scatter.3
  359.7 73.1 reduce-scatter.5
  469.3 69.7 reduce-scatter.7

commit v5 on v4

--- a/solution.py
+++ b/solution.py
@@ -842,7 +842,7 @@
     )(*operands)
 
 
-def grads_kernel(planes, counts, turn_ref, *refs):
+def grads_kernel(planes, owners, counts, turn_ref, *refs):
     refs = list(refs)
     out_ref = refs.pop()
 
@@ -855,7 +855,8 @@
     step = pl.program_id(0)
     steps = pl.num_programs(0)
     block = groups[0][0][0].shape[1]
-    run = block // planes
+    subs = owners // steps
+    run = block // subs // planes
     tiles = groups[0][2].shape[1] // LANES
     count = groups[0][3].shape[1] // planes
 
@@ -863,14 +864,17 @@
         return jnp.concatenate([piece[...] for piece in pieces], axis=0)
 
     grad = sum(dot_tn(joined(left), cols[...]) for left, _, cols, _ in groups).astype(BF)
-    for plane in range(planes):
-        for tile in range(tiles):
-            lines = pl.ds(pl.multiple_of((step * tiles + tile) * run, run), run)
-            out_ref[plane, lines, :] = grad[
-                plane * run : (plane + 1) * run, tile * LANES : (tile + 1) * LANES
-            ]
+    for sub in range(subs):
+        for plane in range(planes):
+            first = (sub * planes + plane) * run
+            for tile in range(tiles):
+                base = ((step * subs + sub) * tiles + tile) * run
+                lines = pl.ds(pl.multiple_of(base, 16), run)
+                out_ref[plane, lines, :] = grad[
+                    first : first + run, tile * LANES : (tile + 1) * LANES
+                ]
     grad = sum(dot_tn(rows[...], joined(up)) for _, up, _, rows in groups).astype(BF)
-    first = block // planes * tiles * steps
+    first = run * tiles * owners
     for index in range(planes):
         plane = lax.rem(turn_ref[0] + index, planes)
         for tile in range(block // LANES):
@@ -881,8 +885,9 @@
             ]
 
 
-def grads_call(steps, planes, turn, groups):
+def grads_call(owners, planes, turn, groups):
     width = groups[0][0][0].shape[1]
+    steps = owners // 2
     block = width // steps
     col_count = groups[0][2].shape[1]
     row_count = groups[0][3].shape[1]
@@ -899,7 +904,9 @@
                 pl.BlockSpec(array.shape, lambda i: (0, 0), pipeline_mode=pl.Buffered(1))
             )
     return pl.pallas_call(
-        functools.partial(grads_kernel, planes, tuple(len(group[0]) for group in groups)),
+        functools.partial(
+            grads_kernel, planes, owners, tuple(len(group[0]) for group in groups)
+        ),
         grid=(steps,),
         in_specs=specs,
         out_specs=pl.BlockSpec((planes, lines, LANES), lambda i: (0, 0, 0)),
@@ -1883,14 +1890,15 @@
     back_crossed, rec_grads = tied(back_crossed, rec_grads)
     back_far = scatter_far(back_even[3], back_crossed[3])
     branch_ffn = scatter_last(result_even, result_crossed, after(result_stage, rec_grads))
-    back_far, branch_ffn = tied(back_far, branch_ffn)
+    first_tiles, first_lines = owned(scattered[0], cols[0], down_pairs)
+    second_tiles, second_lines = owned(scattered[1], cols[1], down_pairs)
+    back_far, branch_ffn, first_tiles, second_tiles = tied(
+        back_far, branch_ffn, first_tiles, second_tiles
+    )
     back_near = scatter_near(back_even[1:3], back_crossed[1:3], back_far)
+    back_near, rec_part = tied(back_near, scatter_packed(rec_grads))
     grad_normed_in = scatter_sum(back_even[0], back_crossed[0], back_near)
-    _, *scattered = tied(back_near, *scattered)
-    second_tiles, second_lines = owned(scattered[1], cols[1], down_pairs)
-    rec_part = after(scatter_packed(rec_grads), second_tiles)
     rec_tiles, rec_lines = owned(rec_part, 5 * chan, mix_pairs)
-    first_tiles, first_lines = owned(after(scattered[0], rec_tiles), cols[0], down_pairs)
     result = (resid + branch_ffn).astype(BF)
     scaled_in = grad_normed_in * gain_mix
     grad_tokens = (
@@ -1906,7 +1914,6 @@
         [first_tiles, second_tiles], shares, planes, (hidden_all, hidden_all)
     )
     grad_w_down = assemble_rows([first_lines, second_lines])
-    grad_w_in, grad_w_forget, grad_w_gate = assemble_tiles([rec_tiles], (mix_run,), 0, rec_widths)
     grad_w_out = assemble_rows([rec_lines])
 
     def spread(part):
@@ -1929,9 +1936,9 @@
             ]
         ),
     ]
-    sums = sum_seq(jnp.concatenate(pieces))
-    sums = tied(rec_part, sums, *others(sums))[1:]
-    sums = sum_tree(list(sums))
+    sums, rec_tiles = tied(sum_seq(jnp.concatenate(pieces)), rec_tiles)
+    sums = sum_tree([sums, *others(sums)])
+    grad_w_in, grad_w_forget, grad_w_gate = assemble_tiles([rec_tiles], (mix_run,), 0, rec_widths)
     cuts = []
     offset = 0
     for piece in pieces:

time: 614 us -> 608 us (level)
  waiting for transfers between devices: 159 us -> 148 us
  starting transfers between devices: 79.6 us -> 88.3 us
    ppermute x82, waiting for transfers between devices: 150 us -> 138 us  [swap(): return lax.ppermute(value, 'seq', [(i, i ^ bit) for i in range(size)])]
    ppermute x3, starting transfers between devices: 4.45 us -> 11.7 us  [others(): lax.ppermute(value, 'wshard', [(i, i ^ key) for i in range(planes)])]
    unnamed x172 -> x138, local copies, waits for them, and re-layouts: 19.2 us -> 15.7 us
  transfers between devices with their start and end apart: 97 -> 97, of which waited for: 30 -> 28; matrix products, arithmetic and copies ran while one was open for 17% -> 17% of each run, Pallas kernels for 38% -> 38%
where the time goes in v5:
time: 608 us; the launch traced here: 604 us
  Pallas kernels  230 us (38%)
  waiting for transfers between devices  148 us (24%)
  starting transfers between devices  88.3 us (15%)
  local copies, waits for them, and re-layouts  51.9 us (9%)
  other arithmetic  49.2 us (8%)
  matrix products  19.6 us (3%)
  between operations  16.5 us (3%)
    ppermute x82, waiting for transfers between devices, swap(): return lax.ppermute(value, 'seq', [(i, i ^ bit) for i in range(size)])  138 us
    pallas_call x6, Pallas kernels, ffn_call(): pl.pallas_call(functools.partial(ffn_kernel, counts, offsets, last), grid...  78.9 us
    ppermute x82, starting transfers between devices, swap(): return lax.ppermute(value, 'seq', [(i, i ^ bit) for i in range(size)])  51.3 us
    pallas_call x3, Pallas kernels, grads_call(): pl.pallas_call(functools.partial(grads_kernel, planes, owners, tuple((len...  47.7 us
    pallas_call x1, Pallas kernels, mix_backward(): pl.pallas_call(mix_backward_kernel, grid=(seqs,), in_specs=[SCALAR, SCALA...  32.3 us
    pallas_call x1, Pallas kernels, mix_forward(): pl.pallas_call(mix_forward_kernel, grid=(seqs,), in_specs=[SCALAR, SCALAR...  27.4 us
    pallas_call x2, Pallas kernels, result_call(): pl.pallas_call(functools.partial(result_kernel, firsts, places, (len(hidd...  20.1 us
    dot_general x7, matrix products, dot(): return jnp.einsum(form, left, right, preferred_element_type=F32)  19.6 us
  transfers between devices with their start and end apart: 97, of which 28 were waited for; matrix products, arithmetic and copies ran while one was open for 17% of the time, Pallas kernels for 38%

profile of v5, /device:TPU:4, one launch (start us, length us, event | category | flops | bytes accessed | tf_op | source)
XLA Modules:
  0.0 603.7 jit_solution(9396200111652352814)
XLA Ops:
  18.2 5.3 fusion.70
  28.1 5.1 fusion.64
  33.2 5.1 fusion.61
  45.3 20.2 %collective-permute-done.3.refs_9_.refs_2_ = bf16[256,2048]{1,0:T(8,128)(2,1)} collective-permute-done((bf16[256,2048]{1,0:T(8,128)(2,1)S(1)}, bf16[256,2048]{1,0:T(8,128)(2,1)}, u32[]{:S(2)}, u32[]{:S(2)}) %collective-permute-start.3) | collective-permute-done | bytes 1048608 | tf_op jit(solution)/shard_map/ppermute | solution.py:22
  78.4 6.2 %collective-permute-done.5.refs_11_.refs_4_ = bf16[128,2048]{1,0:T(8,128)(2,1)} collective-permute-done((bf16[128,2048]{1,0:T(8,128)(2,1)}, bf16[128,2048]{1,0:T(8,128)(2,1)}, u32[]{:S(2)}, u32[]{:S(2)}) %collective-permute-start.5) | collective-permute-done | bytes 524320 | tf_op jit(solution)/shard_map/ppermute | solution.py:22
  91.1 27.4 %mix_forward.1 = (f32[4,2,128,640]{3,2,1,0:T(8,128)}, f32[4,2,128,640]{3,2,1,0:T(8,128)}, f32[8,2,128,256]{3,2,1,0:T(8,128)}, f32[8,2,128,1]{3,2,1,0:T(8,128)}, ...) custom-call(s32[1]{0:T(128)} %bitcast.10.refs_0_.turn_ref, ...), custom_call_target="tpu_custom_call" | custom-call | flops 1024 | bytes 1024 | tf_op jit(solution)/shard_map/mix_forward/pallas_call | solution.py:1073
  129.3 8.7 %collective-permute-done.17 = f32[2,256]{1,0:T(2,128)S(1)} collective-permute-done((f32[2,256]{1,0:T(2,128)S(1)}, f32[2,256]{1,0:T(2,128)S(1)}, u32[]{:S(2)}, u32[]{:S(2)}) %collective-permute-start.17) | collective-permute-done | bytes 2080 | tf_op jit(solution)/shard_map/ppermute | solution.py:22
  140.6 4.6 onward_sums.3
  148.3 22.0 %collective-permute-done.18 = f32[1,256]{1,0:T(1,128)S(1)} collective-permute-done((f32[1,256]{1,0:T(1,128)S(1)}, f32[1,256]{1,0:T(1,128)S(1)}, u32[]{:S(2)}, u32[]{:S(2)}) %collective-permute-start.18) | collective-permute-done | bytes 1056 | tf_op jit(solution)/shard_map/ppermute | solution.py:22
  181.2 21.5 %collective-permute-done.39 = f32[2,256]{1,0:T(2,128)S(1)} collective-permute-done((f32[2,256]{1,0:T(2,128)S(1)}, f32[2,256]{1,0:T(2,128)S(1)}, u32[]{:S(2)}, u32[]{:S(2)}) %collective-permute-start.39) | collective-permute-done | bytes 2080 | tf_op jit(solution)/shard_map/ppermute | solution.py:22
  213.3 14.0 %ffn.7 = (bf16[768,384]{1,0:T(8,128)(2,1)}, bf16[768,768]{1,0:T(8,128)(2,1)}, f32[768,2048]{1,0:T(8,128)}) custom-call(bf16[4,4608,128]{2,1,0:T(8,128)(2,1)} %all-gather.8.cloned.1.call-done.refs_0_.refs_6_, bf16[256,2048]{1,0:T(8,128)(2,1)} %collective-permute-done.26.refs_1_.refs_8_.refs_20_, ...), custom_call_target="tpu_custom_call" | custom-call | flops 6039797760 | bytes 1024 | tf_op jit(solution)/shard_map/ffn/pallas_call | solution.py:821
  227.9 13.7 %ffn.6 = (bf16[768,384]{1,0:T(8,128)(2,1)}, bf16[768,768]{1,0:T(8,128)(2,1)}, f32[768,2048]{1,0:T(8,128)}) custom-call(bf16[4,4608,128]{2,1,0:T(8,128)(2,1)} %all-gather.8.cloned.1.call-done.refs_0_.refs_6_, bf16[256,2048]{1,0:T(8,128)(2,1)} %copy-done.13, bf16[256,2048]{1,0:T(8,128)(2,1)} %collective-permute-done.24.refs_2_.refs_1_.refs_3_.refs_12_, ...), custom_call_target="tpu_custom_call" | custom-call | flops 6039797760 | bytes 1024 | tf_op jit(solution)/shard_map/ffn/pallas_call | solution.py:821
  243.3 10.8 %ffn.8 = (bf16[512,384]{1,0:T(8,128)(2,1)}, bf16[512,768]{1,0:T(8,128)(2,1)}, f32[512,2048]{1,0:T(8,128)}) custom-call(bf16[4,4608,128]{2,1,0:T(8,128)(2,1)} %all-gather.8.cloned.1.call-done.refs_0_.refs_6_, bf16[128,2048]{1,0:T(8,128)(2,1)} %collective-permute-done.32.refs_1_.refs_16_.refs_3_.refs_2_, ...), custom_call_target="tpu_custom_call" | custom-call | flops 1024 | bytes 1024 | tf_op jit(solution)/shard_map/ffn/pallas_call | solution.py:821
  254.1 16.6 %weight_grads.3 = bf16[4,4608,128]{2,1,0:T(8,128)(2,1)} custom-call(s32[1]{0:T(128)} %bitcast.10.refs_0_.turn_ref, bf16[256,2048]{1,0:T(8,128)(2,1)} %copy-done.13, bf16[256,2048]{1,0:T(8,128)(2,1)} %collective-permute-done.24.refs_2_.refs_1_.refs_3_.refs_12_, bf16[256,2048]{1,0:T(8,128)(2,1)} %collective-permute-done.25.refs_3_.refs_2_.refs_4_.refs_13_, ...), custom_call_target="tpu_custom_call" | custom-call | flops 19327352832 | bytes 1024 | tf_op jit(solution)/shard_map/weight_grads/pallas_call | solution.py:906
  270.9 11.6 %ffn.9 = (bf16[512,320]{1,0:T(8,128)(2,1)}, bf16[512,640]{1,0:T(8,128)(2,1)}, bf16[256,2048]{1,0:T(8,128)(2,1)}, bf16[256,2048]{1,0:T(8,128)(2,1)}) custom-call(bf16[4,3840,128]{2,1,0:T(8,128)(2,1)} %all-gather.6.cloned.1.call-done.refs_0_.refs_7_, bf16[128,2048]{1,0:T(8,128)(2,1)} %copy-done.22, bf16[128,2048]{1,0:T(8,128)(2,1)} %copy-done.23, ...), custom_call_target="tpu_custom_call" | custom-call | flops 1024 | bytes 1024 | tf_op jit(solution)/shard_map/ffn/pallas_call | solution.py:821
  290.0 17.4 %ffn.10 = (bf16[1024,320]{1,0:T(8,128)(2,1)}, bf16[1024,640]{1,0:T(8,128)(2,1)}, bf16[256,2048]{1,0:T(8,128)(2,1)}, bf16[256,2048]{1,0:T(8,128)(2,1)}, bf16[256,...) custom-call(bf16[4,3840,128]{2,1,0:T(8,128)(2,1)} %all-gather.6.cloned.1.call-done.refs_0_.refs_7_, ...), custom_call_target="tpu_custom_call" | custom-call | flops 6710886400 | bytes 1024 | tf_op jit(solution)/shard_map/ffn/pallas_call | solution.py:821
  320.0 11.3 %ffn.11 = (bf16[512,320]{1,0:T(8,128)(2,1)}, bf16[512,640]{1,0:T(8,128)(2,1)}, bf16[256,2048]{1,0:T(8,128)(2,1)}, bf16[256,2048]{1,0:T(8,128)(2,1)}) custom-call(bf16[4,3840,128]{2,1,0:T(8,128)(2,1)} %all-gather.6.cloned.1.call-done.refs_0_.refs_7_, bf16[256,2048]{1,0:T(8,128)(2,1)} %collective-permute-done.26.refs_1_.refs_8_.refs_20_, ...), custom_call_target="tpu_custom_call" | custom-call | flops 3355443200 | bytes 1024 | tf_op jit(solution)/shard_map/ffn/pallas_call | solution.py:821
  331.4 16.1 %weight_grads.4 = bf16[4,3840,128]{2,1,0:T(8,128)(2,1)} custom-call(s32[1]{0:T(128)} %bitcast.10.refs_0_.turn_ref, bf16[128,2048]{1,0:T(8,128)(2,1)} %copy-done.22, bf16[128,2048]{1,0:T(8,128)(2,1)} %copy-done.23, bf16[128,2048]{1,0:T(8,128)(2,1)} %collective-permute-done.32.refs_1_.refs_16_.refs_3_.refs_2_, ...), custom_call_target="tpu_custom_call" | custom-call | flops 16106127360 | bytes 1024 | tf_op jit(solution)/shard_map/weight_grads/pallas_call | solution.py:906
  350.9 5.8 multiply_reduce_fusion.1
  358.9 10.1 %ffn_result.3 = (bf16[256,2048]{1,0:T(8,128)(2,1)S(1)}, bf16[256,2048]{1,0:T(8,128)(2,1)S(1)}, bf16[256,2048]{1,0:T(8,128)(2,1)}, bf16[256,2048]{1,0:T(8,128)(2,1)}) custom-call(bf16[768,384]{1,0:T(8,128)(2,1)S(1)} %copy-done.4, bf16[768,384]{1,0:T(8,128)(2,1)S(1)} %copy-done.3, bf16[512,384]{1,0:T(8,128)(2,1)S(1)} %copy-done.7, ...), custom_call_target="tpu_custom_call" | custom-call | flops 2952790016 | bytes 1024 | tf_op jit(solution)/shard_map/ffn_result/pallas_call | solution.py:958
  369.6 10.0 %ffn_result.2 = (bf16[256,2048]{1,0:T(8,128)(2,1)S(1)}, bf16[256,2048]{1,0:T(8,128)(2,1)S(1)}, bf16[256,2048]{1,0:T(8,128)(2,1)}, bf16[256,2048]{1,0:T(8,128)(2,1)}) custom-call(bf16[768,384]{1,0:T(8,128)(2,1)S(1)} %copy-done.4, bf16[768,384]{1,0:T(8,128)(2,1)S(1)} %copy-done.3, bf16[512,384]{1,0:T(8,128)(2,1)S(1)} %copy-done.7, ...), custom_call_target="tpu_custom_call" | custom-call | flops 2952790016 | bytes 1024 | tf_op jit(solution)/shard_map/ffn_result/pallas_call | solution.py:958
  389.3 9.2 %collective-permute-done.54.refs_16_.refs_9_ = bf16[128,2048]{1,0:T(8,128)(2,1)} collective-permute-done((bf16[128,2048]{1,0:T(8,128)(2,1)S(1)}, bf16[128,2048]{1,0:T(8,128)(2,1)}, u32[]{:S(2)}, u32[]{:S(2)}) %collective-permute-start.54) | collective-permute-done | bytes 524320 | tf_op jit(solution)/shard_map/ppermute | solution.py:22
  415.6 32.3 %mix_backward.1 = (bf16[4,2,128,640]{3,2,1,0:T(8,128)(2,1)}, bf16[4,2,128,640]{3,2,1,0:T(8,128)(2,1)}, bf16[4,2,128,256]{3,2,1,0:T(8,128)(2,1)}, bf16[4,2,128,25...) custom-call(s32[1]{0:T(128)} %bitcast.10.refs_0_.turn_ref, ...), custom_call_target="tpu_custom_call" | custom-call | flops 1024 | bytes 1024 | tf_op jit(solution)/shard_map/mix_backward/pallas_call | solution.py:1187
  449.8 15.0 %weight_grads.5 = bf16[4,3584,128]{2,1,0:T(8,128)(2,1)} custom-call(s32[1]{0:T(128)} %constant.147.clone.1.turn_ref, bf16[256,2048]{1,0:T(8,128)(2,1)} %copy-done.14, bf16[256,2048]{1,0:T(8,128)(2,1)} %collective-permute-done.2.refs_8_.refs_1_, bf16[256,2048]{1,0:T(8,128)(2,1)} %collective-permute-done.3.refs_9_.refs_2_, ...), custom_call_target="tpu_custom_call" | custom-call | flops 15032385536 | bytes 1024 | tf_op jit(solution)/shard_map/weight_grads/pallas_call | solution.py:906
  467.9 4.7 all-to-all-start.1
  482.8 5.0 all-to-all-start
  497.7 15.5 %collective-permute-done.74.far_low = bf16[128,2048]{1,0:T(8,128)(2,1)S(1)} collective-permute-done((bf16[128,2048]{1,0:T(8,128)(2,1)S(1)}, bf16[128,2048]{1,0:T(8,128)(2,1)S(1)}, u32[]{:S(2)}, u32[]{:S(2)}) %collective-permute-start.74) | collective-permute-done | bytes 524320 | tf_op jit(solution)/shard_map/ppermute | solution.py:22
  537.0 6.4 %collective-permute-done.77 = bf16[256,2048]{1,0:T(8,128)(2,1)} collective-permute-done((bf16[256,2048]{1,0:T(8,128)(2,1)}, bf16[256,2048]{1,0:T(8,128)(2,1)}, u32[]{:S(2)}, u32[]{:S(2)}) %collective-permute-start.77) | collective-permute-done | bytes 1048608 | tf_op jit(solution)/shard_map/ppermute | solution.py:22
  545.9 5.8 all-to-all-start.2
  568.1 11.1 %collective-permute-start.84 = (f32[8195]{0:T(1024)S(1)}, f32[8195]{0:T(1024)S(1)}, u32[]{:S(2)}, u32[]{:S(2)}) collective-permute-start(f32[8195]{0:T(1024)S(1)} %add.324), channel_id=1, source_target_pairs={{0,3},{1,2},{2,1},{3,0},{4,7},{5,6},{6,5},{7,4},{8,11},{9,10},{10,... | collective-permute-start | bytes 98348 | tf_op jit(solution)/shard_map/ppermute | solution.py:232
  579.8 5.2 fusion.44
  585.1 7.5 %collective-permute-done.85 = bf16[1024,128]{1,0:T(8,128)(2,1)S(1)} collective-permute-done((bf16[1024,128]{1,0:T(8,128)(2,1)S(1)}, bf16[1024,128]{1,0:T(8,128)(2,1)S(1)}, u32[]{:S(2)}, u32[]{:S(2)}) %collective-permute-start.85) | collective-permute-done | bytes 262176 | tf_op jit(solution)/shard_map/ppermute | solution.py:1846
  (451 shorter events, 206.0 us)
Async XLA Ops:
  7.2 82.9 %all-gather.4.cloned.1.call-start = ((), (), s32[]{:S(2)}) async-start(), calls=%async_computation.6 | async-start | bytes 4587520 | tf_op jit(solution)/shard_map/all_gather | solution.py:261
  7.2 31.6 %collective-permute-start.1 = (bf16[256,2048]{1,0:T(8,128)(2,1)}, bf16[256,2048]{1,0:T(8,128)(2,1)}, u32[]{:S(2)}, u32[]{:S(2)}) collective-permute-start(bf16[256,2048]{1,0:T(8,128)(2,1)} %bitcast.8.refs_4_.refs_3_.refs_23_), channel_id=1, source_target_pairs={{0,16},{4,20},{8,24},{12,28},{16,0},{20,4},{24,8},{28,12},{1,17},{... | collective-permute-start | bytes 3145736 | tf_op jit(solution)/shard_map/ppermute | solution.py:22
  7.3 31.5 %collective-permute-start = (bf16[256,2048]{1,0:T(8,128)(2,1)}, bf16[256,2048]{1,0:T(8,128)(2,1)}, u32[]{:S(2)}, u32[]{:S(2)}) collective-permute-start(bf16[256,2048]{1,0:T(8,128)(2,1)} %bitcast.8.refs_4_.refs_3_.refs_23_), channel_id=1, source_target_pairs={{0,8},{4,12},{8,0},{12,4},{16,24},{20,28},{24,16},{28,20},{1,9},{5... | collective-permute-start | bytes 3145736 | tf_op jit(solution)/shard_map/ppermute | solution.py:22
  15.7 197.6 %all-gather.8.cloned.1.call-start = ((), (), s32[]{:S(2)}) async-start(), calls=%async_computation.8 | async-start | bytes 5898240 | tf_op jit(solution)/shard_map/all_gather | solution.py:261
  66.9 203.9 %all-gather.6.cloned.1.call-start = ((), (), s32[]{:S(2)}) async-start(), calls=%async_computation.7 | async-start | bytes 4915200 | tf_op jit(solution)/shard_map/all_gather | solution.py:261
  77.9 40.6 %collective-permute-start.12 = (bf16[128,2048]{1,0:T(8,128)(2,1)}, bf16[128,2048]{1,0:T(8,128)(2,1)}, u32[]{:S(2)}, u32[]{:S(2)}) collective-permute-start(bf16[128,2048]{1,0:T(8,128)(2,1)} %slice.140), channel_id=1, source_target_pairs={{0,8},{4,12},{8,0},{12,4},{16,24},{20,28},{24,16},{28,20},{1,9},{5... | collective-permute-start | bytes 1572872 | tf_op jit(solution)/shard_map/ppermute | solution.py:22
  84.7 33.8 %collective-permute-start.11 = (bf16[128,2048]{1,0:T(8,128)(2,1)}, bf16[128,2048]{1,0:T(8,128)(2,1)}, u32[]{:S(2)}, u32[]{:S(2)}) collective-permute-start(bf16[128,2048]{1,0:T(8,128)(2,1)} %slice.139), channel_id=1, source_target_pairs={{0,16},{4,20},{8,24},{12,28},{16,0},{20,4},{24,8},{28,12},{1,17},{... | collective-permute-start | bytes 1572872 | tf_op jit(solution)/shard_map/ppermute | solution.py:22
  138.1 32.2 %collective-permute-start.19 = (bf16[256,2048]{1,0:T(8,128)(2,1)}, bf16[256,2048]{1,0:T(8,128)(2,1)S(1)}, u32[]{:S(2)}, u32[]{:S(2)}) collective-permute-start(bf16[256,2048]{1,0:T(8,128)(2,1)} %bitcast.29), channel_id=1, source_target_pairs={{0,4},{4,0},{8,12},{12,8},{16,20},{20,16},{24,28},{28,24},{1,5},{5... | collective-permute-start | bytes 3145736 | tf_op jit(solution)/shard_map/ppermute | solution.py:22
  145.2 25.1 %collective-permute-start.22 = (bf16[256,2048]{1,0:T(8,128)(2,1)}, bf16[256,2048]{1,0:T(8,128)(2,1)S(1)}, u32[]{:S(2)}, u32[]{:S(2)}) collective-permute-start(bf16[256,2048]{1,0:T(8,128)(2,1)} %get-tuple-element.194), channel_id=1, source_target_pairs={{0,8},{4,12},{8,0},{12,4},{16,24},{20,28},{24,16},{28,20},{1,9},{5... | collective-permute-start | bytes 3145736 | tf_op jit(solution)/shard_map/ppermute | solution.py:22
  146.0 25.6 %collective-permute-start.23 = (bf16[256,2048]{1,0:T(8,128)(2,1)}, bf16[256,2048]{1,0:T(8,128)(2,1)}, u32[]{:S(2)}, u32[]{:S(2)}) collective-permute-start(bf16[256,2048]{1,0:T(8,128)(2,1)} %get-tuple-element.195), channel_id=1, source_target_pairs={{0,16},{4,20},{8,24},{12,28},{16,0},{20,4},{24,8},{28,12},{1,17},{... | collective-permute-start | bytes 3145736 | tf_op jit(solution)/shard_map/ppermute | solution.py:22
  148.2 55.0 %collective-permute-start.29 = (bf16[256,2048]{1,0:T(8,128)(2,1)}, bf16[256,2048]{1,0:T(8,128)(2,1)}, u32[]{:S(2)}, u32[]{:S(2)}) collective-permute-start(bf16[256,2048]{1,0:T(8,128)(2,1)} %bitcast.8.refs_4_.refs_3_.refs_23_), channel_id=1, source_target_pairs={{0,4},{4,0},{8,12},{12,8},{16,20},{20,16},{24,28},{28,24},{1,5},{5... | collective-permute-start | bytes 3145736 | tf_op jit(solution)/shard_map/ppermute | solution.py:22
  148.2 301.5 %reduce-scatter.4.cloned.1.call-start = ((), (), s32[]{:S(2)}) async-start(), calls=%async_computation.9 | async-start | bytes 5898240 | tf_op jit(solution)/shard_map/reduce_scatter | solution.py:265
  176.3 30.1 %collective-permute-start.25 = (bf16[256,2048]{1,0:T(8,128)(2,1)S(1)}, bf16[256,2048]{1,0:T(8,128)(2,1)}, u32[]{:S(2)}, u32[]{:S(2)}) collective-permute-start(bf16[256,2048]{1,0:T(8,128)(2,1)S(1)} %multiply_convert_fusion.refs_1_.refs_0_.refs_2_.refs_21_), channel_id=1, source_target_pairs={{0,16},{4,20},{8,24},{12,28},{16,0},{20,4},{24,8},{28,12},{1,17},{... | collective-permute-start | bytes 3145736 | tf_op jit(solution)/shard_map/ppermute | solution.py:22
  178.0 28.9 %collective-permute-start.24 = (bf16[256,2048]{1,0:T(8,128)(2,1)S(1)}, bf16[256,2048]{1,0:T(8,128)(2,1)}, u32[]{:S(2)}, u32[]{:S(2)}) collective-permute-start(bf16[256,2048]{1,0:T(8,128)(2,1)S(1)} %multiply_convert_fusion.refs_1_.refs_0_.refs_2_.refs_21_), channel_id=1, source_target_pairs={{0,8},{4,12},{8,0},{12,4},{16,24},{20,28},{24,16},{28,20},{1,9},{5... | collective-permute-start | bytes 3145736 | tf_op jit(solution)/shard_map/ppermute | solution.py:22
  210.8 30.8 %collective-permute-start.36 = (bf16[128,2048]{1,0:T(8,128)(2,1)}, bf16[128,2048]{1,0:T(8,128)(2,1)}, u32[]{:S(2)}, u32[]{:S(2)}) collective-permute-start(bf16[128,2048]{1,0:T(8,128)(2,1)} %collective-permute-done.11.refs_5_.refs_20_.refs_7_.refs_6_), channel_id=1, source_target_pairs={{0,4},{4,0},{8,12},{12,8},{16,20},{20,16},{24,28},{28,24},{1,5},{5... | collective-permute-start | bytes 1572872 | tf_op jit(solution)/shard_map/ppermute | solution.py:22
  211.3 30.4 %collective-permute-start.37 = (bf16[128,2048]{1,0:T(8,128)(2,1)}, bf16[128,2048]{1,0:T(8,128)(2,1)}, u32[]{:S(2)}, u32[]{:S(2)}) collective-permute-start(bf16[128,2048]{1,0:T(8,128)(2,1)} %collective-permute-done.12.refs_6_.refs_21_.refs_8_.refs_7_), channel_id=1, source_target_pairs={{0,4},{4,0},{8,12},{12,8},{16,20},{20,16},{24,28},{28,24},{1,5},{5... | collective-permute-start | bytes 1572872 | tf_op jit(solution)/shard_map/ppermute | solution.py:22
  270.8 178.9 %reduce-scatter.6.cloned.1.call-start = ((), (), s32[]{:S(2)}) async-start(), calls=%async_computation.10 | async-start | bytes 4915200 | tf_op jit(solution)/shard_map/reduce_scatter | solution.py:265
  318.1 29.4 %collective-permute-start.46 = (bf16[256,2048]{1,0:T(8,128)(2,1)}, bf16[256,2048]{1,0:T(8,128)(2,1)S(1)}, u32[]{:S(2)}, u32[]{:S(2)}) collective-permute-start(bf16[256,2048]{1,0:T(8,128)(2,1)} %get-tuple-element.234), channel_id=1, source_target_pairs={{0,8},{4,12},{8,0},{12,4},{16,24},{20,28},{24,16},{28,20},{1,9},{5... | collective-permute-start | bytes 3145736 | tf_op jit(solution)/shard_map/ppermute | solution.py:22
  318.7 28.8 %collective-permute-start.47 = (bf16[256,2048]{1,0:T(8,128)(2,1)}, bf16[256,2048]{1,0:T(8,128)(2,1)}, u32[]{:S(2)}, u32[]{:S(2)}) collective-permute-start(bf16[256,2048]{1,0:T(8,128)(2,1)} %get-tuple-element.235), channel_id=1, source_target_pairs={{0,16},{4,20},{8,24},{12,28},{16,0},{20,4},{24,8},{28,12},{1,17},{... | collective-permute-start | bytes 3145736 | tf_op jit(solution)/shard_map/ppermute | solution.py:22
  347.5 196.5 %reduce-scatter.8.cloned.1.call-start = ((), (), s32[]{:S(2)}) async-start(), calls=%async_computation.11 | async-start | bytes 4587520 | tf_op jit(solution)/shard_map/reduce_scatter | solution.py:265
  356.7 26.1 %collective-permute-start.50 = (bf16[256,2048]{1,0:T(8,128)(2,1)S(1)}, bf16[256,2048]{1,0:T(8,128)(2,1)}, u32[]{:S(2)}, u32[]{:S(2)}) collective-permute-start(bf16[256,2048]{1,0:T(8,128)(2,1)S(1)} %get-tuple-element.339.refs_12_.refs_5_), channel_id=1, source_target_pairs={{0,16},{4,20},{8,24},{12,28},{16,0},{20,4},{24,8},{28,12},{1,17},{... | collective-permute-start | bytes 3145736 | tf_op jit(solution)/shard_map/ppermute | solution.py:22
  357.4 25.4 %collective-permute-start.49 = (bf16[256,2048]{1,0:T(8,128)(2,1)S(1)}, bf16[256,2048]{1,0:T(8,128)(2,1)}, u32[]{:S(2)}, u32[]{:S(2)}) collective-permute-start(bf16[256,2048]{1,0:T(8,128)(2,1)S(1)} %get-tuple-element.339.refs_12_.refs_5_), channel_id=1, source_target_pairs={{0,8},{4,12},{8,0},{12,4},{16,24},{20,28},{24,16},{28,20},{1,9},{5... | collective-permute-start | bytes 3145736 | tf_op jit(solution)/shard_map/ppermute | solution.py:22
  408.2 39.8 %collective-permute-start.69 = (bf16[128,2048]{1,0:T(8,128)(2,1)}, bf16[128,2048]{1,0:T(8,128)(2,1)S(1)}, u32[]{:S(2)}, u32[]{:S(2)}) collective-permute-start(bf16[128,2048]{1,0:T(8,128)(2,1)} %get-tuple-element.279), channel_id=1, source_target_pairs={{0,8},{4,12},{8,0},{12,4},{16,24},{20,28},{24,16},{28,20},{1,9},{5... | collective-permute-start | bytes 1572872 | tf_op jit(solution)/shard_map/ppermute | solution.py:22
  409.4 39.8 %collective-permute-start.70 = (bf16[128,2048]{1,0:T(8,128)(2,1)}, bf16[128,2048]{1,0:T(8,128)(2,1)}, u32[]{:S(2)}, u32[]{:S(2)}) collective-permute-start(bf16[128,2048]{1,0:T(8,128)(2,1)} %get-tuple-element.280), channel_id=1, source_target_pairs={{0,16},{4,20},{8,24},{12,28},{16,0},{20,4},{24,8},{28,12},{1,17},{... | collective-permute-start | bytes 1572872 | tf_op jit(solution)/shard_map/ppermute | solution.py:22
  410.1 39.2 %collective-permute-start.71 = (bf16[128,2048]{1,0:T(8,128)(2,1)}, bf16[128,2048]{1,0:T(8,128)(2,1)}, u32[]{:S(2)}, u32[]{:S(2)}) collective-permute-start(bf16[128,2048]{1,0:T(8,128)(2,1)} %get-tuple-element.281), channel_id=1, source_target_pairs={{0,8},{4,12},{8,0},{12,4},{16,24},{20,28},{24,16},{28,20},{1,9},{5... | collective-permute-start | bytes 1572872 | tf_op jit(solution)/shard_map/ppermute | solution.py:22
  411.5 38.2 %collective-permute-start.72 = (bf16[128,2048]{1,0:T(8,128)(2,1)}, bf16[128,2048]{1,0:T(8,128)(2,1)}, u32[]{:S(2)}, u32[]{:S(2)}) collective-permute-start(bf16[128,2048]{1,0:T(8,128)(2,1)} %get-tuple-element.282), channel_id=1, source_target_pairs={{0,16},{4,20},{8,24},{12,28},{16,0},{20,4},{24,8},{28,12},{1,17},{... | collective-permute-start | bytes 1572872 | tf_op jit(solution)/shard_map/ppermute | solution.py:22
  482.8 31.2 %all-to-all-start = ((bf16[8,384,128]{2,1,0:T(8,128)(2,1)}), bf16[8,384,128]{2,1,0:T(8,128)(2,1)S(1)}, u32[]{:S(2)}, u32[]{:S(2)}) async-start(bf16[8,384,128]{2,1,0:T(8,128)(2,1)} %bitcast.184), calls=%async_computation.2 | async-start | bytes 1572864 | tf_op jit(solution)/shard_map/all_to_all | solution.py:1844
  518.8 25.2 %collective-permute-start.78 = (bf16[256,2048]{1,0:T(8,128)(2,1)}, bf16[256,2048]{1,0:T(8,128)(2,1)}, u32[]{:S(2)}, u32[]{:S(2)}) collective-permute-start(bf16[256,2048]{1,0:T(8,128)(2,1)} %get-tuple-element.313), channel_id=1, source_target_pairs={{0,16},{4,20},{8,24},{12,28},{16,0},{20,4},{24,8},{28,12},{1,17},{... | collective-permute-start | bytes 3145736 | tf_op jit(solution)/shard_map/ppermute | solution.py:22
  526.3 34.0 %collective-permute-start.87 = (bf16[1280,128]{1,0:T(8,128)(2,1)}, bf16[1280,128]{1,0:T(8,128)(2,1)S(1)}, u32[]{:S(2)}, u32[]{:S(2)}) collective-permute-start(bf16[1280,128]{1,0:T(8,128)(2,1)} %slice.178), channel_id=1, source_target_pairs={{0,0},{1,9},{2,18},{3,27},{4,24},{5,1},{6,10},{7,19},{8,16},{9,25}... | collective-permute-start | bytes 983048 | tf_op jit(solution)/shard_map/ppermute | solution.py:1846
  528.2 32.1 %collective-permute-start.86 = (bf16[1536,128]{1,0:T(8,128)(2,1)S(1)}, bf16[1536,128]{1,0:T(8,128)(2,1)S(1)}, u32[]{:S(2)}, u32[]{:S(2)}) collective-permute-start(bf16[1536,128]{1,0:T(8,128)(2,1)S(1)} %slice.177), channel_id=1, source_target_pairs={{0,0},{1,9},{2,18},{3,27},{4,24},{5,1},{6,10},{7,19},{8,16},{9,25}... | collective-permute-start | bytes 1179656 | tf_op jit(solution)/shard_map/ppermute | solution.py:1846
  565.7 26.9 %collective-permute-start.85 = (bf16[1024,128]{1,0:T(8,128)(2,1)S(1)}, bf16[1024,128]{1,0:T(8,128)(2,1)S(1)}, u32[]{:S(2)}, u32[]{:S(2)}) collective-permute-start(bf16[1024,128]{1,0:T(8,128)(2,1)S(1)} %slice.175), channel_id=1, source_target_pairs={{0,0},{1,8},{2,16},{3,24},{4,1},{5,9},{6,17},{7,25},{8,2},{9,10},{... | collective-permute-start | bytes 786440 | tf_op jit(solution)/shard_map/ppermute | solution.py:1846
  568.1 26.6 %collective-permute-start.84 = (f32[8195]{0:T(1024)S(1)}, f32[8195]{0:T(1024)S(1)}, u32[]{:S(2)}, u32[]{:S(2)}) collective-permute-start(f32[8195]{0:T(1024)S(1)} %add.324), channel_id=1, source_target_pairs={{0,3},{1,2},{2,1},{3,0},{4,7},{5,6},{6,5},{7,4},{8,11},{9,10},{10,... | collective-permute-start | bytes 98348 | tf_op jit(solution)/shard_map/ppermute | solution.py:232
  (130 other events, 1500.0 us)
Sparse Core Ops, SparseCore 0:
  15.8 72.7 all-gather.3
  90.7 88.0 all-gather.7
  180.4 74.8 all-gather.5
  270.9 85.8 reduce-scatter.3
  359.0 73.2 reduce-scatter.5
  466.0 69.5 reduce-scatter.7

commit v6 on v5

--- a/solution.py
+++ b/solution.py
@@ -1598,7 +1598,7 @@
     mix_run = w_out.shape[0] // groups
     ffn_run = w_down.shape[0] // groups
     chan = mix_run * planes // 2
-    shares = (ffn_run * 6 // 11, ffn_run - ffn_run * 6 // 11)
+    shares = (ffn_run * 5 // 11, ffn_run - ffn_run * 5 // 11)
     if not (
         groups == 8
         and groups % planes == 0
@@ -1914,7 +1914,6 @@
         [first_tiles, second_tiles], shares, planes, (hidden_all, hidden_all)
     )
     grad_w_down = assemble_rows([first_lines, second_lines])
-    grad_w_out = assemble_rows([rec_lines])
 
     def spread(part):
         count = part.shape[1] // mix_run
@@ -1936,8 +1935,9 @@
             ]
         ),
     ]
-    sums, rec_tiles = tied(sum_seq(jnp.concatenate(pieces)), rec_tiles)
+    sums, rec_tiles, rec_lines = tied(sum_seq(jnp.concatenate(pieces)), rec_tiles, rec_lines)
     sums = sum_tree([sums, *others(sums)])
+    grad_w_out = assemble_rows([rec_lines])
     grad_w_in, grad_w_forget, grad_w_gate = assemble_tiles([rec_tiles], (mix_run,), 0, rec_widths)
     cuts = []
     offset = 0

time: 608 us -> 601 us (0.988)
    ppermute x82, starting transfers between devices: 51.3 us -> 59.4 us  [swap(): return lax.ppermute(value, 'seq', [(i, i ^ bit) for i in range(size)])]
    ppermute x3, starting transfers between devices: 11.7 us -> 4.39 us  [others(): lax.ppermute(value, 'wshard', [(i, i ^ key) for i in range(planes)])]
    unnamed x138 -> x152, local copies, waits for them, and re-layouts: 15.7 us -> 16.3 us
  transfers between devices with their start and end apart: 97 -> 97, of which waited for: 28 -> 30; matrix products, arithmetic and copies ran while one was open for 17% -> 17% of each run, Pallas kernels for 38% -> 39%
where the time goes in v6:
time: 601 us; the launch traced here: 596 us
  Pallas kernels  229 us (38%)
  waiting for transfers between devices  144 us (24%)
  starting transfers between devices  88.1 us (15%)
  local copies, waits for them, and re-layouts  50.7 us (8%)
  other arithmetic  49.3 us (8%)
  matrix products  17.1 us (3%)
  between operations  16.5 us (3%)
    ppermute x82, waiting for transfers between devices, swap(): return lax.ppermute(value, 'seq', [(i, i ^ bit) for i in range(size)])  138 us
    pallas_call x6, Pallas kernels, ffn_call(): pl.pallas_call(functools.partial(ffn_kernel, counts, offsets, last), grid...  78.1 us
    ppermute x82, starting transfers between devices, swap(): return lax.ppermute(value, 'seq', [(i, i ^ bit) for i in range(size)])  59.4 us
    pallas_call x3, Pallas kernels, grads_call(): pl.pallas_call(functools.partial(grads_kernel, planes, owners, tuple((len...  48.1 us
    pallas_call x1, Pallas kernels, mix_backward(): pl.pallas_call(mix_backward_kernel, grid=(seqs,), in_specs=[SCALAR, SCALA...  32.1 us
    pallas_call x1, Pallas kernels, mix_forward(): pl.pallas_call(mix_forward_kernel, grid=(seqs,), in_specs=[SCALAR, SCALAR...  27.4 us
    pallas_call x2, Pallas kernels, result_call(): pl.pallas_call(functools.partial(result_kernel, firsts, places, (len(hidd...  20.2 us
    dot_general x7, matrix products, dot(): return jnp.einsum(form, left, right, preferred_element_type=F32)  17.1 us
  transfers between devices with their start and end apart: 97, of which 30 were waited for; matrix products, arithmetic and copies ran while one was open for 17% of the time, Pallas kernels for 39%

profile of v6, /device:TPU:4, one launch (start us, length us, event | category | flops | bytes accessed | tf_op | source)
XLA Modules:
  0.0 595.5 jit_solution(13924888322236133627)
XLA Ops:
  17.9 5.3 fusion.70
  27.7 5.3 fusion.64
  42.5 20.3 %collective-permute-done.3.refs_9_.refs_2_ = bf16[256,2048]{1,0:T(8,128)(2,1)} collective-permute-done((bf16[256,2048]{1,0:T(8,128)(2,1)S(1)}, bf16[256,2048]{1,0:T(8,128)(2,1)}, u32[]{:S(2)}, u32[]{:S(2)}) %collective-permute-start.3) | collective-permute-done | bytes 1048608 | tf_op jit(solution)/shard_map/ppermute | solution.py:22
  75.7 6.2 %collective-permute-done.5.refs_11_.refs_4_ = bf16[128,2048]{1,0:T(8,128)(2,1)} collective-permute-done((bf16[128,2048]{1,0:T(8,128)(2,1)}, bf16[128,2048]{1,0:T(8,128)(2,1)}, u32[]{:S(2)}, u32[]{:S(2)}) %collective-permute-start.5) | collective-permute-done | bytes 524320 | tf_op jit(solution)/shard_map/ppermute | solution.py:22
  88.6 27.4 %mix_forward.1 = (f32[4,2,128,640]{3,2,1,0:T(8,128)}, f32[4,2,128,640]{3,2,1,0:T(8,128)}, f32[8,2,128,256]{3,2,1,0:T(8,128)}, f32[8,2,128,1]{3,2,1,0:T(8,128)}, ...) custom-call(s32[1]{0:T(128)} %bitcast.10.refs_0_.turn_ref, ...), custom_call_target="tpu_custom_call" | custom-call | flops 1024 | bytes 1024 | tf_op jit(solution)/shard_map/mix_forward/pallas_call | solution.py:1073
  127.7 8.4 %collective-permute-done.17 = f32[2,256]{1,0:T(2,128)S(1)} collective-permute-done((f32[2,256]{1,0:T(2,128)S(1)}, f32[2,256]{1,0:T(2,128)S(1)}, u32[]{:S(2)}, u32[]{:S(2)}) %collective-permute-start.17) | collective-permute-done | bytes 2080 | tf_op jit(solution)/shard_map/ppermute | solution.py:22
  138.9 4.5 onward_sums.3
  145.7 22.1 %collective-permute-done.18 = f32[1,256]{1,0:T(1,128)S(1)} collective-permute-done((f32[1,256]{1,0:T(1,128)S(1)}, f32[1,256]{1,0:T(1,128)S(1)}, u32[]{:S(2)}, u32[]{:S(2)}) %collective-permute-start.18) | collective-permute-done | bytes 1056 | tf_op jit(solution)/shard_map/ppermute | solution.py:22
  179.6 18.2 %collective-permute-done.25.refs_3_.refs_2_.refs_4_.refs_13_ = bf16[256,2048]{1,0:T(8,128)(2,1)S(1)} collective-permute-done((bf16[256,2048]{1,0:T(8,128)(2,1)S(1)}, bf16[256,2048]{1,0:T(8,128)(2,1)S(1)}, u32[]{:S(2)}, u32[]{:S(2)}) %collective-permute-start.25) | collective-permute-done | bytes 1048608 | tf_op jit(solution)/shard_map/ppermute | solution.py:22
  206.5 12.7 %ffn.7 = (bf16[768,320]{1,0:T(8,128)(2,1)}, bf16[768,640]{1,0:T(8,128)(2,1)}, f32[768,2048]{1,0:T(8,128)}) custom-call(bf16[4,3840,128]{2,1,0:T(8,128)(2,1)} %all-gather.8.cloned.1.call-done.refs_0_.refs_6_, bf16[256,2048]{1,0:T(8,128)(2,1)} %copy-done.42, bf16[256,2048]{1,0:T(8,128)(2,1)} %copy-done.32, bf16[256,2048]{1,0:T(8,128)(2,1)} %copy-done.31, ...), custom_call_target="tpu_custom_call" | custom-call | flops 5033164800 | bytes 1024 | tf_op jit(solution)/shard_map/ffn/pallas_call | solution.py:821
  220.4 12.6 %ffn.6 = (bf16[768,320]{1,0:T(8,128)(2,1)}, bf16[768,640]{1,0:T(8,128)(2,1)}, f32[768,2048]{1,0:T(8,128)}) custom-call(bf16[4,3840,128]{2,1,0:T(8,128)(2,1)} %all-gather.8.cloned.1.call-done.refs_0_.refs_6_, bf16[256,2048]{1,0:T(8,128)(2,1)} %copy-done.17, bf16[256,2048]{1,0:T(8,128)(2,1)} %copy-done.21, bf16[256,2048]{1,0:T(8,128)(2,1)} %copy-done.19, ...), custom_call_target="tpu_custom_call" | custom-call | flops 5033164800 | bytes 1024 | tf_op jit(solution)/shard_map/ffn/pallas_call | solution.py:821
  234.7 10.1 %ffn.8 = (bf16[512,320]{1,0:T(8,128)(2,1)}, bf16[512,640]{1,0:T(8,128)(2,1)}, f32[512,2048]{1,0:T(8,128)}) custom-call(bf16[4,3840,128]{2,1,0:T(8,128)(2,1)} %all-gather.8.cloned.1.call-done.refs_0_.refs_6_, bf16[128,2048]{1,0:T(8,128)(2,1)} %collective-permute-done.32.refs_1_.refs_16_.refs_3_.refs_2_, ...), custom_call_target="tpu_custom_call" | custom-call | flops 1024 | bytes 1024 | tf_op jit(solution)/shard_map/ffn/pallas_call | solution.py:821
  244.8 15.9 %weight_grads.3 = bf16[4,3840,128]{2,1,0:T(8,128)(2,1)} custom-call(s32[1]{0:T(128)} %bitcast.10.refs_0_.turn_ref, bf16[256,2048]{1,0:T(8,128)(2,1)} %copy-done.17, bf16[256,2048]{1,0:T(8,128)(2,1)} %copy-done.21, bf16[256,2048]{1,0:T(8,128)(2,1)} %copy-done.19, bf16[256,2048]{1,0:T(8,128)(2,1)} %bitcast.8.refs_4_.refs_3_.refs_23_, ...), custom_call_target="tpu_custom_call" | custom-call | flops 16106127360 | bytes 1024 | tf_op jit(solution)/shard_map/weight_grads/pallas_call | solution.py:906
  260.8 12.1 %ffn.9 = (bf16[512,384]{1,0:T(8,128)(2,1)}, bf16[512,768]{1,0:T(8,128)(2,1)}, bf16[256,2048]{1,0:T(8,128)(2,1)}, bf16[256,2048]{1,0:T(8,128)(2,1)}) custom-call(bf16[4,4608,128]{2,1,0:T(8,128)(2,1)} %all-gather.6.cloned.1.call-done.refs_0_.refs_7_, bf16[128,2048]{1,0:T(8,128)(2,1)} %copy-done.25, bf16[128,2048]{1,0:T(8,128)(2,1)} %copy-done.26, ...), custom_call_target="tpu_custom_call" | custom-call | flops 1024 | bytes 1024 | tf_op jit(solution)/shard_map/ffn/pallas_call | solution.py:821
  280.2 18.7 %ffn.10 = (bf16[1024,384]{1,0:T(8,128)(2,1)}, bf16[1024,768]{1,0:T(8,128)(2,1)}, bf16[256,2048]{1,0:T(8,128)(2,1)}, bf16[256,2048]{1,0:T(8,128)(2,1)}, bf16[256,...) custom-call(bf16[4,4608,128]{2,1,0:T(8,128)(2,1)} %all-gather.6.cloned.1.call-done.refs_0_.refs_7_, ...), custom_call_target="tpu_custom_call" | custom-call | flops 8053063680 | bytes 1024 | tf_op jit(solution)/shard_map/ffn/pallas_call | solution.py:821
  305.1 4.5 onward_sums.4
  311.7 12.0 %ffn.11 = (bf16[512,384]{1,0:T(8,128)(2,1)}, bf16[512,768]{1,0:T(8,128)(2,1)}, bf16[256,2048]{1,0:T(8,128)(2,1)}, bf16[256,2048]{1,0:T(8,128)(2,1)}) custom-call(bf16[4,4608,128]{2,1,0:T(8,128)(2,1)} %all-gather.6.cloned.1.call-done.refs_0_.refs_7_, bf16[256,2048]{1,0:T(8,128)(2,1)} %copy-done.42, bf16[256,2048]{1,0:T(8,128)(2,1)} %copy-done.17, ...), custom_call_target="tpu_custom_call" | custom-call | flops 4026531840 | bytes 1024 | tf_op jit(solution)/shard_map/ffn/pallas_call | solution.py:821
  323.7 17.2 %weight_grads.4 = bf16[4,4608,128]{2,1,0:T(8,128)(2,1)} custom-call(s32[1]{0:T(128)} %bitcast.10.refs_0_.turn_ref, bf16[128,2048]{1,0:T(8,128)(2,1)} %copy-done.25, bf16[128,2048]{1,0:T(8,128)(2,1)} %copy-done.26, bf16[128,2048]{1,0:T(8,128)(2,1)} %collective-permute-done.32.refs_1_.refs_16_.refs_3_.refs_2_, ...), custom_call_target="tpu_custom_call" | custom-call | flops 19327352832 | bytes 1024 | tf_op jit(solution)/shard_map/weight_grads/pallas_call | solution.py:906
  344.2 5.9 multiply_reduce_fusion.1
  352.2 10.1 %ffn_result.3 = (bf16[256,2048]{1,0:T(8,128)(2,1)S(1)}, bf16[256,2048]{1,0:T(8,128)(2,1)S(1)}, bf16[256,2048]{1,0:T(8,128)(2,1)}, bf16[256,2048]{1,0:T(8,128)(2,1)}) custom-call(bf16[768,320]{1,0:T(8,128)(2,1)S(1)} %copy-done.4, bf16[768,320]{1,0:T(8,128)(2,1)S(1)} %copy-done.3, bf16[512,320]{1,0:T(8,128)(2,1)S(1)} %copy-done.7, ...), custom_call_target="tpu_custom_call" | custom-call | flops 2952790016 | bytes 1024 | tf_op jit(solution)/shard_map/ffn_result/pallas_call | solution.py:958
  363.3 10.2 %ffn_result.2 = (bf16[256,2048]{1,0:T(8,128)(2,1)S(1)}, bf16[256,2048]{1,0:T(8,128)(2,1)S(1)}, bf16[256,2048]{1,0:T(8,128)(2,1)}, bf16[256,2048]{1,0:T(8,128)(2,1)}) custom-call(bf16[768,320]{1,0:T(8,128)(2,1)S(1)} %copy-done.4, bf16[768,320]{1,0:T(8,128)(2,1)S(1)} %copy-done.3, bf16[512,320]{1,0:T(8,128)(2,1)S(1)} %copy-done.7, ...), custom_call_target="tpu_custom_call" | custom-call | flops 2952790016 | bytes 1024 | tf_op jit(solution)/shard_map/ffn_result/pallas_call | solution.py:958
  381.6 9.7 %collective-permute-done.54.refs_16_.refs_9_ = bf16[128,2048]{1,0:T(8,128)(2,1)} collective-permute-done((bf16[128,2048]{1,0:T(8,128)(2,1)S(1)}, bf16[128,2048]{1,0:T(8,128)(2,1)}, u32[]{:S(2)}, u32[]{:S(2)}) %collective-permute-start.54) | collective-permute-done | bytes 524320 | tf_op jit(solution)/shard_map/ppermute | solution.py:22
  408.7 32.1 %mix_backward.1 = (bf16[4,2,128,640]{3,2,1,0:T(8,128)(2,1)}, bf16[4,2,128,640]{3,2,1,0:T(8,128)(2,1)}, bf16[4,2,128,256]{3,2,1,0:T(8,128)(2,1)}, bf16[4,2,128,25...) custom-call(s32[1]{0:T(128)} %bitcast.10.refs_0_.turn_ref, ...), custom_call_target="tpu_custom_call" | custom-call | flops 1024 | bytes 1024 | tf_op jit(solution)/shard_map/mix_backward/pallas_call | solution.py:1187
  441.9 15.0 %weight_grads.5 = bf16[4,3584,128]{2,1,0:T(8,128)(2,1)} custom-call(s32[1]{0:T(128)} %constant.147.clone.1.turn_ref, bf16[256,2048]{1,0:T(8,128)(2,1)} %copy-done.13, bf16[256,2048]{1,0:T(8,128)(2,1)} %collective-permute-done.2.refs_8_.refs_1_, bf16[256,2048]{1,0:T(8,128)(2,1)} %collective-permute-done.3.refs_9_.refs_2_, ...), custom_call_target="tpu_custom_call" | custom-call | flops 15032385536 | bytes 1024 | tf_op jit(solution)/shard_map/weight_grads/pallas_call | solution.py:906
  474.4 5.0 all-to-all-start.1
  489.5 15.4 %collective-permute-done.74.far_low = bf16[128,2048]{1,0:T(8,128)(2,1)S(1)} collective-permute-done((bf16[128,2048]{1,0:T(8,128)(2,1)S(1)}, bf16[128,2048]{1,0:T(8,128)(2,1)S(1)}, u32[]{:S(2)}, u32[]{:S(2)}) %collective-permute-start.74) | collective-permute-done | bytes 524320 | tf_op jit(solution)/shard_map/ppermute | solution.py:22
  505.8 4.4 onward_sums.5
  520.7 4.5 collective-permute-start.87
  529.6 5.7 collective-permute-done.77
  537.7 5.8 all-to-all-start.2
  552.4 11.0 %collective-permute-start.80 = (f32[8195]{0:T(1024)S(1)}, f32[8195]{0:T(1024)S(1)}, u32[]{:S(2)}, u32[]{:S(2)}) collective-permute-start(f32[8195]{0:T(1024)S(1)} %add.322), channel_id=1, source_target_pairs={{0,8},{4,12},{8,0},{12,4},{16,24},{20,28},{24,16},{28,20},{1,9},{5... | collective-permute-start | bytes 98348 | tf_op jit(solution)/shard_map/ppermute | solution.py:22
  579.2 5.2 fusion.44
  (466 shorter events, 205.8 us)
Async XLA Ops:
  7.2 81.4 %all-gather.4.cloned.1.call-start = ((), (), s32[]{:S(2)}) async-start(), calls=%async_computation.6 | async-start | bytes 4587520 | tf_op jit(solution)/shard_map/all_gather | solution.py:261
  7.2 28.7 %collective-permute-start.1 = (bf16[256,2048]{1,0:T(8,128)(2,1)}, bf16[256,2048]{1,0:T(8,128)(2,1)}, u32[]{:S(2)}, u32[]{:S(2)}) collective-permute-start(bf16[256,2048]{1,0:T(8,128)(2,1)} %bitcast.8.refs_4_.refs_3_.refs_23_), channel_id=1, source_target_pairs={{0,16},{4,20},{8,24},{12,28},{16,0},{20,4},{24,8},{28,12},{1,17},{... | collective-permute-start | bytes 3145736 | tf_op jit(solution)/shard_map/ppermute | solution.py:22
  7.3 28.7 %collective-permute-start = (bf16[256,2048]{1,0:T(8,128)(2,1)}, bf16[256,2048]{1,0:T(8,128)(2,1)}, u32[]{:S(2)}, u32[]{:S(2)}) collective-permute-start(bf16[256,2048]{1,0:T(8,128)(2,1)} %bitcast.8.refs_4_.refs_3_.refs_23_), channel_id=1, source_target_pairs={{0,8},{4,12},{8,0},{12,4},{16,24},{20,28},{24,16},{28,20},{1,9},{5... | collective-permute-start | bytes 3145736 | tf_op jit(solution)/shard_map/ppermute | solution.py:22
  15.7 190.8 %all-gather.8.cloned.1.call-start = ((), (), s32[]{:S(2)}) async-start(), calls=%async_computation.8 | async-start | bytes 4915200 | tf_op jit(solution)/shard_map/all_gather | solution.py:261
  38.3 24.5 %collective-permute-start.3 = (bf16[256,2048]{1,0:T(8,128)(2,1)S(1)}, bf16[256,2048]{1,0:T(8,128)(2,1)}, u32[]{:S(2)}, u32[]{:S(2)}) collective-permute-start(bf16[256,2048]{1,0:T(8,128)(2,1)S(1)} %fusion.41.refs_7_.refs_0_), channel_id=1, source_target_pairs={{0,16},{4,20},{8,24},{12,28},{16,0},{20,4},{24,8},{28,12},{1,17},{... | collective-permute-start | bytes 3145736 | tf_op jit(solution)/shard_map/ppermute | solution.py:22
  64.1 196.7 %all-gather.6.cloned.1.call-start = ((), (), s32[]{:S(2)}) async-start(), calls=%async_computation.7 | async-start | bytes 5898240 | tf_op jit(solution)/shard_map/all_gather | solution.py:261
  75.1 40.9 %collective-permute-start.12 = (bf16[128,2048]{1,0:T(8,128)(2,1)}, bf16[128,2048]{1,0:T(8,128)(2,1)}, u32[]{:S(2)}, u32[]{:S(2)}) collective-permute-start(bf16[128,2048]{1,0:T(8,128)(2,1)} %slice.140), channel_id=1, source_target_pairs={{0,8},{4,12},{8,0},{12,4},{16,24},{20,28},{24,16},{28,20},{1,9},{5... | collective-permute-start | bytes 1572872 | tf_op jit(solution)/shard_map/ppermute | solution.py:22
  81.9 34.1 %collective-permute-start.11 = (bf16[128,2048]{1,0:T(8,128)(2,1)}, bf16[128,2048]{1,0:T(8,128)(2,1)}, u32[]{:S(2)}, u32[]{:S(2)}) collective-permute-start(bf16[128,2048]{1,0:T(8,128)(2,1)} %slice.139), channel_id=1, source_target_pairs={{0,16},{4,20},{8,24},{12,28},{16,0},{20,4},{24,8},{28,12},{1,17},{... | collective-permute-start | bytes 1572872 | tf_op jit(solution)/shard_map/ppermute | solution.py:22
  127.2 314.7 %reduce-scatter.4.cloned.1.call-start = ((), (), s32[]{:S(2)}) async-start(), calls=%async_computation.9 | async-start | bytes 4915200 | tf_op jit(solution)/shard_map/reduce_scatter | solution.py:265
  136.1 31.7 %collective-permute-start.19 = (bf16[256,2048]{1,0:T(8,128)(2,1)}, bf16[256,2048]{1,0:T(8,128)(2,1)}, u32[]{:S(2)}, u32[]{:S(2)}) collective-permute-start(bf16[256,2048]{1,0:T(8,128)(2,1)} %bitcast.223), channel_id=1, source_target_pairs={{0,4},{4,0},{8,12},{12,8},{16,20},{20,16},{24,28},{28,24},{1,5},{5... | collective-permute-start | bytes 3145736 | tf_op jit(solution)/shard_map/ppermute | solution.py:22
  143.7 25.5 %collective-permute-start.23 = (bf16[256,2048]{1,0:T(8,128)(2,1)}, bf16[256,2048]{1,0:T(8,128)(2,1)S(1)}, u32[]{:S(2)}, u32[]{:S(2)}) collective-permute-start(bf16[256,2048]{1,0:T(8,128)(2,1)} %get-tuple-element.196), channel_id=1, source_target_pairs={{0,16},{4,20},{8,24},{12,28},{16,0},{20,4},{24,8},{28,12},{1,17},{... | collective-permute-start | bytes 3145736 | tf_op jit(solution)/shard_map/ppermute | solution.py:22
  145.7 30.1 %collective-permute-start.29 = (bf16[256,2048]{1,0:T(8,128)(2,1)}, bf16[256,2048]{1,0:T(8,128)(2,1)S(1)}, u32[]{:S(2)}, u32[]{:S(2)}) collective-permute-start(bf16[256,2048]{1,0:T(8,128)(2,1)} %bitcast.8.refs_4_.refs_3_.refs_23_), channel_id=1, source_target_pairs={{0,4},{4,0},{8,12},{12,8},{16,20},{20,16},{24,28},{28,24},{1,5},{5... | collective-permute-start | bytes 3145736 | tf_op jit(solution)/shard_map/ppermute | solution.py:22
  173.3 24.5 %collective-permute-start.25 = (bf16[256,2048]{1,0:T(8,128)(2,1)S(1)}, bf16[256,2048]{1,0:T(8,128)(2,1)S(1)}, u32[]{:S(2)}, u32[]{:S(2)}) collective-permute-start(bf16[256,2048]{1,0:T(8,128)(2,1)S(1)} %multiply_convert_fusion.refs_1_.refs_0_.refs_2_.refs_21_), channel_id=1, source_target_pairs={{0,16},{4,20},{8,24},{12,28},{16,0},{20,4},{24,8},{28,12},{1,17},{... | collective-permute-start | bytes 3145736 | tf_op jit(solution)/shard_map/ppermute | solution.py:22
  175.3 25.9 %collective-permute-start.31 = (bf16[256,2048]{1,0:T(8,128)(2,1)}, bf16[256,2048]{1,0:T(8,128)(2,1)S(1)}, u32[]{:S(2)}, u32[]{:S(2)}) collective-permute-start(bf16[256,2048]{1,0:T(8,128)(2,1)} %collective-permute-done.1.refs_6_.refs_5_.refs_8_.refs_17_), channel_id=1, source_target_pairs={{0,4},{4,0},{8,12},{12,8},{16,20},{20,16},{24,28},{28,24},{1,5},{5... | collective-permute-start | bytes 3145736 | tf_op jit(solution)/shard_map/ppermute | solution.py:22
  203.4 29.7 %collective-permute-start.36 = (bf16[128,2048]{1,0:T(8,128)(2,1)}, bf16[128,2048]{1,0:T(8,128)(2,1)}, u32[]{:S(2)}, u32[]{:S(2)}) collective-permute-start(bf16[128,2048]{1,0:T(8,128)(2,1)} %collective-permute-done.11.refs_5_.refs_20_.refs_7_.refs_6_), channel_id=1, source_target_pairs={{0,4},{4,0},{8,12},{12,8},{16,20},{20,16},{24,28},{28,24},{1,5},{5... | collective-permute-start | bytes 1572872 | tf_op jit(solution)/shard_map/ppermute | solution.py:22
  203.5 29.6 %collective-permute-start.37 = (bf16[128,2048]{1,0:T(8,128)(2,1)}, bf16[128,2048]{1,0:T(8,128)(2,1)}, u32[]{:S(2)}, u32[]{:S(2)}) collective-permute-start(bf16[128,2048]{1,0:T(8,128)(2,1)} %collective-permute-done.12.refs_6_.refs_21_.refs_8_.refs_7_), channel_id=1, source_target_pairs={{0,4},{4,0},{8,12},{12,8},{16,20},{20,16},{24,28},{28,24},{1,5},{5... | collective-permute-start | bytes 1572872 | tf_op jit(solution)/shard_map/ppermute | solution.py:22
  260.7 181.2 %reduce-scatter.6.cloned.1.call-start = ((), (), s32[]{:S(2)}) async-start(), calls=%async_computation.10 | async-start | bytes 5898240 | tf_op jit(solution)/shard_map/reduce_scatter | solution.py:265
  309.6 31.3 %collective-permute-start.46 = (bf16[256,2048]{1,0:T(8,128)(2,1)}, bf16[256,2048]{1,0:T(8,128)(2,1)S(1)}, u32[]{:S(2)}, u32[]{:S(2)}) collective-permute-start(bf16[256,2048]{1,0:T(8,128)(2,1)} %get-tuple-element.235), channel_id=1, source_target_pairs={{0,8},{4,12},{8,0},{12,4},{16,24},{20,28},{24,16},{28,20},{1,9},{5... | collective-permute-start | bytes 3145736 | tf_op jit(solution)/shard_map/ppermute | solution.py:22
  310.8 30.1 %collective-permute-start.47 = (bf16[256,2048]{1,0:T(8,128)(2,1)}, bf16[256,2048]{1,0:T(8,128)(2,1)}, u32[]{:S(2)}, u32[]{:S(2)}) collective-permute-start(bf16[256,2048]{1,0:T(8,128)(2,1)} %get-tuple-element.236), channel_id=1, source_target_pairs={{0,16},{4,20},{8,24},{12,28},{16,0},{20,4},{24,8},{28,12},{1,17},{... | collective-permute-start | bytes 3145736 | tf_op jit(solution)/shard_map/ppermute | solution.py:22
  341.0 194.8 %reduce-scatter.8.cloned.1.call-start = ((), (), s32[]{:S(2)}) async-start(), calls=%async_computation.11 | async-start | bytes 4587520 | tf_op jit(solution)/shard_map/reduce_scatter | solution.py:265
  350.1 26.6 %collective-permute-start.50 = (bf16[256,2048]{1,0:T(8,128)(2,1)}, bf16[256,2048]{1,0:T(8,128)(2,1)S(1)}, u32[]{:S(2)}, u32[]{:S(2)}) collective-permute-start(bf16[256,2048]{1,0:T(8,128)(2,1)} %get-tuple-element.341.refs_12_.refs_5_), channel_id=1, source_target_pairs={{0,16},{4,20},{8,24},{12,28},{16,0},{20,4},{24,8},{28,12},{1,17},{... | collective-permute-start | bytes 3145736 | tf_op jit(solution)/shard_map/ppermute | solution.py:22
  351.1 25.7 %collective-permute-start.49 = (bf16[256,2048]{1,0:T(8,128)(2,1)}, bf16[256,2048]{1,0:T(8,128)(2,1)}, u32[]{:S(2)}, u32[]{:S(2)}) collective-permute-start(bf16[256,2048]{1,0:T(8,128)(2,1)} %get-tuple-element.341.refs_12_.refs_5_), channel_id=1, source_target_pairs={{0,8},{4,12},{8,0},{12,4},{16,24},{20,28},{24,16},{28,20},{1,9},{5... | collective-permute-start | bytes 3145736 | tf_op jit(solution)/shard_map/ppermute | solution.py:22
  401.3 39.6 %collective-permute-start.69 = (bf16[128,2048]{1,0:T(8,128)(2,1)}, bf16[128,2048]{1,0:T(8,128)(2,1)}, u32[]{:S(2)}, u32[]{:S(2)}) collective-permute-start(bf16[128,2048]{1,0:T(8,128)(2,1)} %get-tuple-element.280), channel_id=1, source_target_pairs={{0,8},{4,12},{8,0},{12,4},{16,24},{20,28},{24,16},{28,20},{1,9},{5... | collective-permute-start | bytes 1572872 | tf_op jit(solution)/shard_map/ppermute | solution.py:22
  402.0 39.4 %collective-permute-start.70 = (bf16[128,2048]{1,0:T(8,128)(2,1)}, bf16[128,2048]{1,0:T(8,128)(2,1)}, u32[]{:S(2)}, u32[]{:S(2)}) collective-permute-start(bf16[128,2048]{1,0:T(8,128)(2,1)} %get-tuple-element.281), channel_id=1, source_target_pairs={{0,16},{4,20},{8,24},{12,28},{16,0},{20,4},{24,8},{28,12},{1,17},{... | collective-permute-start | bytes 1572872 | tf_op jit(solution)/shard_map/ppermute | solution.py:22
  403.2 38.3 %collective-permute-start.71 = (bf16[128,2048]{1,0:T(8,128)(2,1)}, bf16[128,2048]{1,0:T(8,128)(2,1)}, u32[]{:S(2)}, u32[]{:S(2)}) collective-permute-start(bf16[128,2048]{1,0:T(8,128)(2,1)} %get-tuple-element.282), channel_id=1, source_target_pairs={{0,8},{4,12},{8,0},{12,4},{16,24},{20,28},{24,16},{28,20},{1,9},{5... | collective-permute-start | bytes 1572872 | tf_op jit(solution)/shard_map/ppermute | solution.py:22
  404.1 37.9 %collective-permute-start.72 = (bf16[128,2048]{1,0:T(8,128)(2,1)}, bf16[128,2048]{1,0:T(8,128)(2,1)}, u32[]{:S(2)}, u32[]{:S(2)}) collective-permute-start(bf16[128,2048]{1,0:T(8,128)(2,1)} %get-tuple-element.283), channel_id=1, source_target_pairs={{0,16},{4,20},{8,24},{12,28},{16,0},{20,4},{24,8},{28,12},{1,17},{... | collective-permute-start | bytes 1572872 | tf_op jit(solution)/shard_map/ppermute | solution.py:22
  474.4 30.5 %all-to-all-start.1 = ((bf16[8,384,128]{2,1,0:T(8,128)(2,1)}), bf16[8,384,128]{2,1,0:T(8,128)(2,1)S(1)}, u32[]{:S(2)}, u32[]{:S(2)}) async-start(bf16[8,384,128]{2,1,0:T(8,128)(2,1)} %bitcast.56), calls=%async_computation.3 | async-start | bytes 1572864 | tf_op jit(solution)/shard_map/all_to_all | solution.py:1844
  510.2 25.1 %collective-permute-start.77 = (bf16[256,2048]{1,0:T(8,128)(2,1)}, bf16[256,2048]{1,0:T(8,128)(2,1)}, u32[]{:S(2)}, u32[]{:S(2)}) collective-permute-start(bf16[256,2048]{1,0:T(8,128)(2,1)} %get-tuple-element.313), channel_id=1, source_target_pairs={{0,8},{4,12},{8,0},{12,4},{16,24},{20,28},{24,16},{28,20},{1,9},{5... | collective-permute-start | bytes 3145736 | tf_op jit(solution)/shard_map/ppermute | solution.py:22
  510.7 25.0 %collective-permute-start.78 = (bf16[256,2048]{1,0:T(8,128)(2,1)}, bf16[256,2048]{1,0:T(8,128)(2,1)}, u32[]{:S(2)}, u32[]{:S(2)}) collective-permute-start(bf16[256,2048]{1,0:T(8,128)(2,1)} %get-tuple-element.314), channel_id=1, source_target_pairs={{0,16},{4,20},{8,24},{12,28},{16,0},{20,4},{24,8},{28,12},{1,17},{... | collective-permute-start | bytes 3145736 | tf_op jit(solution)/shard_map/ppermute | solution.py:22
  518.8 44.6 %collective-permute-start.86 = (bf16[1280,128]{1,0:T(8,128)(2,1)}, bf16[1280,128]{1,0:T(8,128)(2,1)S(1)}, u32[]{:S(2)}, u32[]{:S(2)}) collective-permute-start(bf16[1280,128]{1,0:T(8,128)(2,1)} %slice.177), channel_id=1, source_target_pairs={{0,0},{1,9},{2,18},{3,27},{4,24},{5,1},{6,10},{7,19},{8,16},{9,25}... | collective-permute-start | bytes 983048 | tf_op jit(solution)/shard_map/ppermute | solution.py:1846
  520.7 42.7 %collective-permute-start.87 = (bf16[1536,128]{1,0:T(8,128)(2,1)}, bf16[1536,128]{1,0:T(8,128)(2,1)S(1)}, u32[]{:S(2)}, u32[]{:S(2)}) collective-permute-start(bf16[1536,128]{1,0:T(8,128)(2,1)} %slice.178), channel_id=1, source_target_pairs={{0,0},{1,9},{2,18},{3,27},{4,24},{5,1},{6,10},{7,19},{8,16},{9,25}... | collective-permute-start | bytes 1179656 | tf_op jit(solution)/shard_map/ppermute | solution.py:1846
  537.7 37.1 %all-to-all-start.2 = ((bf16[8,320,128]{2,1,0:T(8,128)(2,1)}), bf16[8,320,128]{2,1,0:T(8,128)(2,1)S(1)}, u32[]{:S(2)}, u32[]{:S(2)}) async-start(bf16[8,320,128]{2,1,0:T(8,128)(2,1)} %bitcast.187), calls=%async_computation.5 | async-start | bytes 1310720 | tf_op jit(solution)/shard_map/all_to_all | solution.py:1844
  (137 other events, 1558.1 us)
Sparse Core Ops, SparseCore 0:
  15.8 72.7 all-gather.3
  90.2 75.0 all-gather.7
  167.4 87.9 all-gather.5
  260.9 73.6 reduce-scatter.3
  341.1 86.2 reduce-scatter.5
  458.2 68.8 reduce-scatter.7
